TPU v7x, 128 devices: a whole 4x4x4 slice. The times are simulated.
128 devices in a mesh: az: 8 (over z_lo, y), col: 16 (over z_hi, x, core).
Axes of the slice: x: 4, y: 4, z: 4 (z_hi: 2, z_lo: 2; z = z_hi * 2 + z_lo), core: 2. Of those that a mesh axis runs over, the one named last changes fastest.
Arguments:
- phase_field: float32 [64, 1024, 2048], P(None, 'col', 'az'), may hold values from -1 to 1
- velocity: bfloat16 [2, 64, 1024, 2048], P(None, None, 'col', 'az'), may hold values from -4 to 4
- owned_modes: int32 [128, 4], replicated, may hold values from 0 to 511, as said below
- legendre: bfloat16 [512, 1024, 512], P(('az', 'col')), as said below
- radial_inverse: bfloat16 [512, 64, 64], replicated, as said below
Outputs:
- new_phase: float32 [64, 1024, 2048], P(None, 'col', 'az')
Inputs may be any that keep to these rules, and one draw needn't show every extreme that they name: `owned_modes`: every order from 0 to 511 appears exactly once; the second half of each row is 511 minus its first half. legendre[q, t, l] is the orthonormal associated Legendre function of degree l and order m_q (owned_modes flattened at q) at cos(theta_t), normalized so that the integral of its square times sin(theta) over theta is 1, rounded to bfloat16; it is 0 for l < m_q. `radial_inverse`: one matrix for each degree.
All inputs are finite; a program needn't handle non-finite values.
Results may differ from a plain program's by a relative error of at most 0.0003.
Values sent between devices are 32-bit elements; how exact they have to be, the bound alone decides.
No kernel may reach another device: no remote copies, remote signals or barrier semaphores. Data moves between devices by JAX's collectives and lax.ppermute only.
A program may use at most 192 MiB of HBM per device.

v0:
```python
import math

import jax
import jax.numpy as jnp
from jax import lax
from jax.sharding import PartitionSpec as P

step_time = 0.002
mobility_step = 4e-06
highest_precision = lax.Precision.HIGHEST


def padded_2(block, sides, width):
    for axis, dim in sides:
        count = lax.axis_size(axis)
        forward = [(i, i + 1) for i in range(count - 1)]
        forward.append((count - 1, 0))
        backward = [(target, source) for source, target in forward]
        low = lax.ppermute(
            lax.slice_in_dim(block, block.shape[dim] - width, None, axis=dim), axis, forward
        )
        high = lax.ppermute(lax.slice_in_dim(block, 0, width, axis=dim), axis, backward)
        block = jnp.concatenate([low, block, high], axis=dim)
    return block


def shell_radii(shells):
    return 0.75 + 0.25 * (jnp.arange(shells, dtype=jnp.float32) + 0.5) / shells


def colat_weights(count):
    row_index = jnp.arange(count, dtype=jnp.int32)
    waves = jnp.arange(1, count // 2 + 1, dtype=jnp.int32)
    turns = (2 * row_index[:, None] + 1) * waves[None, :] % (2 * count)
    cosines = jnp.cos(turns.astype(jnp.float32) * (math.pi / count))
    wave_float = waves.astype(jnp.float32)
    coefs = 1.0 / (4.0 * wave_float * wave_float - 1.0)
    return 2.0 / count * (1.0 - 2.0 * jnp.dot(cosines, coefs, precision=highest_precision))


def forward_waves(phi_index, mode_list, phi_count):
    turns = phi_index[:, None] * mode_list[None, :] % phi_count
    angle = turns.astype(jnp.float32) * (2.0 * math.pi / phi_count)
    return jnp.stack([jnp.cos(angle), -jnp.sin(angle)], axis=1) / phi_count


def inverse_waves(mode_list, phi_count):
    phi_index = jnp.arange(phi_count, dtype=jnp.int32)
    turns = mode_list[:, None] * phi_index[None, :] % phi_count
    angle = turns.astype(jnp.float32) * (2.0 * math.pi / phi_count)
    doubling = jnp.where(mode_list == 0, 1.0, 2.0).astype(jnp.float32)[:, None]
    return jnp.stack([doubling * jnp.cos(angle), -doubling * jnp.sin(angle)], axis=0)


def body(phase_field, velocity, owned_modes, legendre, radial_inverse):
    shells, theta_local, phi_local = phase_field.shape
    az_count = lax.axis_size("az")
    col_count = lax.axis_size("col")
    phi_count = phi_local * az_count
    theta_count = theta_local * col_count
    theta_block = theta_local // az_count
    mode_list = owned_modes.reshape(-1)
    mode_count = mode_list.shape[0]
    mode_dev = legendre.shape[0]
    degree_count = legendre.shape[2]
    legendre_full = legendre.astype(jnp.float32)
    shell_radius = shell_radii(shells)
    padded = padded_2(phase_field, (("az", 2), ("col", 1)), 1)
    col_here = lax.axis_index("col")
    row_index = jnp.arange(theta_local + 2, dtype=jnp.int32)
    row_mask = jnp.logical_not(
        jnp.logical_or(
            jnp.logical_and(row_index == 0, col_here == 0),
            jnp.logical_and(row_index == theta_local + 1, col_here == col_count - 1),
        )
    )
    padded = padded * row_mask.astype(jnp.float32)[None, :, None]
    centre_rows = padded[:, 1:-1, :]
    east_cell = centre_rows[:, :, 2:]
    west_cell = centre_rows[:, :, :-2]
    south_cell = padded[:, 2:, 1:-1]
    north_cell = padded[:, :-2, 1:-1]
    d_phi = (east_cell - west_cell) * (phi_count / (4.0 * math.pi))
    d_theta = (south_cell - north_cell) * (theta_count / (2.0 * math.pi))
    spin_rate = velocity[0].astype(jnp.float32)
    sweep_speed = velocity[1].astype(jnp.float32)
    advected = phase_field - step_time * (
        spin_rate * d_phi + sweep_speed / shell_radius[:, None, None] * d_theta
    )
    potential = phase_field * phase_field * phase_field - phase_field
    fields = jnp.stack([advected, potential])
    wave_table = forward_waves(jnp.arange(phi_count, dtype=jnp.int32), mode_list, phi_count)
    spectra = jnp.einsum(
        "frtp,pqk->ktqfr",
        lax.all_to_all(fields, "az", split_axis=2, concat_axis=3, tiled=True),
        wave_table,
        precision=highest_precision,
    )
    spectra = spectra.reshape(mode_count, theta_block, 4 * shells)
    gathered = lax.all_to_all(spectra, ("az", "col"), split_axis=0, concat_axis=1, tiled=True)
    gathered = gathered.reshape(mode_dev, az_count, col_count, theta_block, 4 * shells)
    gathered = jnp.transpose(gathered, (0, 2, 1, 3, 4))
    gathered = gathered.reshape(mode_dev, theta_count, 4 * shells)
    weights = colat_weights(theta_count)
    weighted = gathered * weights[None, :, None]
    coeffs = jnp.einsum("ktx,ktl->klx", weighted, legendre_full, precision=highest_precision)
    coeffs = coeffs.reshape(mode_dev, degree_count, 2, 2, shells)
    degrees = jnp.arange(degree_count, dtype=jnp.float32)
    factor = (
        mobility_step
        * (degrees * (degrees + 1.0))[:, None]
        / (shell_radius * shell_radius)[None, :]
    )
    right_side = coeffs[:, :, :, 0, :] - factor[None, :, None, :] * coeffs[:, :, :, 1, :]
    solved = jnp.einsum(
        "lrs,klqs->klqr",
        radial_inverse.astype(jnp.float32),
        right_side,
        precision=highest_precision,
    )
    synthesis = jnp.einsum(
        "ktl,klx->ktx",
        legendre_full,
        solved.reshape(mode_dev, degree_count, 2 * shells),
        precision=highest_precision,
    )
    synthesis = synthesis.reshape(mode_dev, col_count, az_count, theta_block, 2 * shells)
    synthesis = jnp.transpose(synthesis, (0, 2, 1, 3, 4)).reshape(mode_dev, theta_count, 2 * shells)
    grid_modes = lax.all_to_all(synthesis, ("az", "col"), split_axis=1, concat_axis=0, tiled=True)
    grid_modes = grid_modes.reshape(mode_count, theta_block, 2, shells)
    inverse_table = inverse_waves(mode_list, phi_count)
    row_fields = jnp.einsum("ktqr,qkp->rtp", grid_modes, inverse_table, precision=highest_precision)
    new_phase = lax.all_to_all(row_fields, "az", split_axis=2, concat_axis=1, tiled=True)
    return new_phase


def solution(mesh):
    in_specs = (
        P(None, "col", "az"),
        P(None, None, "col", "az"),
        P(),
        P(("az", "col"), None, None),
        P(),
    )
    out_specs = P(None, "col", "az")
    return jax.shard_map(body, mesh=mesh, in_specs=in_specs, out_specs=out_specs, check_vma=False)
```

profile of v0, /device:TPU:0, one launch (start us, length us, event | category | flops | bytes accessed | tf_op | source)
XLA Modules:
  0.0 518.5 jit_solution(17031054977183519346)
XLA Ops:
  0.0 4.2 fusion.74
  4.2 2.3 copy.81
  6.5 1.7 collective-permute-start
  8.2 0.7 copy.82
  8.9 2.9 collective-permute-start.1
  11.7 4.8 fusion.73
  16.5 0.0 copy-done
  16.5 4.4 copy.50
  21.0 0.0 collective-permute-done
  21.0 1.9 copy.46
  22.9 0.0 collective-permute-done.1
  22.9 2.9 copy.48
  25.8 1.2 pad_maximum_fusion.3
  27.0 0.1 collective-permute-start.2
  27.1 5.8 %collective-permute-start.3 = (f32[64,1,258]{2,0,1:T(8,128)S(1)}, f32[64,1,258]{2,0,1:T(8,128)S(1)}, u32[]{:S(2)}, u32[]{:S(2)}) collective-permute-start(f32[64,1,258]{2,0,1:T(8,128)S(1)} %get-tuple-element.6), channel_id=1, source_target_pairs={{1,0},{2,1},{3,2},{4,3},{5,4},{6,5},{7,6},{8,7},{9,8},{10,9},{11,1... | collective-permute-start | bytes 198152 | tf_op jit(solution)/shard_map/ppermute | solution.py:22
  33.0 1.8 collective-permute-done.2
  34.7 0.4 collective-permute-done.3
  35.2 0.0 copy-done.2
  35.2 3.1 maximum_multiply_fusion.1
  38.3 10.6 %fusion.20 = (f32[1,64,64,256]{3,1,0,2:T(8,128)S(1)}, f32[1,64,64,256]{3,1,0,2:T(8,128)}) fusion(f32[64,66,258]{2,0,1:T(8,128)S(1)} %maximum_multiply_fusion.1, bf16[1,64,64,256]{3,2,1,0:T(8,128)(2,1)} %get-tuple-element.10, bf16[1,64,64,256]{3,2,1,0:T(8,128)(2,1)} %get-tuple-element.9, f32[64]{0:T(128)S(1)} %multiply_add_fusion.1, ...), kind=kLoop, calls=%fused_computation.32 | loop fusion | flops 15728640 | bytes 33554688 | tf_op jit(solution)/shard_map/stack | solution.py:91
  49.0 6.3 %pad_maximum_fusion = f32[2,64,64,256]{3,1,0,2:T(8,128)} fusion(f32[1,64,64,256]{3,1,0,2:T(8,128)} %get-tuple-element.8, f32[1,64,64,256]{3,1,0,2:T(8,128)S(1)} %get-tuple-element.7), kind=kLoop, calls=%fused_computation.9 | loop fusion | flops 2097152 | bytes 16777216 | tf_op jit(solution)/shard_map/stack | solution.py:91
  55.2 5.3 %all-to-all-start = ((f32[2,64,64,256]{3,1,0,2:T(8,128)}), f32[2,64,64,256]{3,1,0,2:T(8,128)}, u32[]{:S(2)}, u32[]{:S(2)}) async-start(f32[2,64,64,256]{3,1,0,2:T(8,128)} %pad_maximum_fusion), calls=%async_computation | async-start | bytes 16777216 | tf_op jit(solution)/shard_map/all_to_all | solution.py:95
  60.5 0.1 copy.42
  60.6 0.1 reshape.391
  60.7 18.0 %fusion.47 = (f32[2048,1,512]{2,0,1:T(8,128)}, f32[2048,1,512]{2,0,1:T(8,128)}) fusion(s32[512]{0:T(512)S(1)} %reshape.391), kind=kLoop, calls=%fused_computation.68 | loop fusion | flops 15728640 | bytes 8390656 | tf_op jit(solution)/shard_map/cos | solution.py:44
  78.8 75.0 %all-to-all-done = f32[2,64,64,256]{3,1,0,2:T(8,128)} async-done(((f32[2,64,64,256]{3,1,0,2:T(8,128)}), f32[2,64,64,256]{3,1,0,2:T(8,128)}, u32[]{:S(2)}, u32[]{:S(2)}) %all-to-all-start) | async-done | bytes 8388640 | tf_op jit(solution)/shard_map/all_to_all | solution.py:95
  153.7 13.2 %copy.100 = f32[2,64,8,8,256]{4,2,1,3,0:T(8,128)} copy(f32[2,64,8,8,256]{4,1,0,3,2:T(8,128)} %bitcast.6) | data formatting | bytes 16777216 | tf_op jit(solution)/shard_map/all_to_all | solution.py:95
  166.9 9.3 %reshape.403 = f32[2,64,8,2048,1]{3,1,2,0,4:T(8,128)} reshape(f32[2,64,8,8,256]{4,3,1,2,0:T(8,128)} %bitcast.103) | data formatting | bytes 16777216 | tf_op jit(solution)/shard_map/all_to_all | solution.py:95
  176.2 32.8 %fusion.34 = f32[512,8,2,2,64]{0,4,1,3,2:T(8,128)S(1)} fusion(f32[2,64,8,2048,1]{3,1,2,0,4:T(8,128)} %reshape.403, f32[2048,1,512]{2,0,1:T(8,128)} %get-tuple-element.20, f32[2048,1,512]{2,0,1:T(8,128)} %get-tuple-element.19), kind=kOutput, calls=%fused_computation.55 | convolution fusion | flops 25773998080 | bytes 20971520 | tf_op jit(solution)/shard_map/frtp,pqk->ktqfr/dot_general | solution.py:93
  209.0 2.5 copy.56
  211.5 5.4 %copy.57 = f32[512,8,256]{2,1,0:T(8,128)} copy(f32[512,8,256]{0,2,1:T(8,128)} %bitcast.104) | data formatting | bytes 8388608 | tf_op jit(solution)/shard_map/reshape | solution.py:99
  216.9 41.0 %all-to-all-start.1 = ((f32[512,8,256]{2,1,0:T(8,128)}), f32[512,8,256]{2,1,0:T(8,128)}, u32[]{:S(2)}, u32[]{:S(2)}) async-start(f32[512,8,256]{2,1,0:T(8,128)} %copy.57), calls=%async_computation.1 | async-start | bytes 8388608 | tf_op jit(solution)/shard_map/all_to_all | solution.py:100
  257.9 13.0 %copy.75 = bf16[512,64,64,1]{2,1,3,0:T(8,128)(2,1)} copy(bf16[512,64,64,1]{0,2,1,3:T(8,128)(2,1)} %bitcast.109) | data formatting | bytes 8388608 | tf_op args[4]
  270.9 9.9 %fusion.40 = f32[1,1024]{1,0:T(1,128)S(1)} fusion(f32[512,1]{0,1:T(1,128)S(1)} %bitcast.112, s32[512]{0:T(512)S(1)} %iota_add_fusion, s32[1024]{0:T(1024)S(1)} %multiply_add_fusion), kind=kOutput, calls=%fused_computation.59 | convolution fusion | flops 13631488 | bytes 12288 | tf_op jit(solution)/shard_map/dot_general | solution.py:38
  280.8 0.2 broadcast_divide_fusion
  281.0 29.5 %all-to-all-done.1 = f32[512,8,256]{2,1,0:T(8,128)} async-done(((f32[512,8,256]{2,1,0:T(8,128)}), f32[512,8,256]{2,1,0:T(8,128)}, u32[]{:S(2)}, u32[]{:S(2)}) %all-to-all-start.1) | async-done | bytes 4194336 | tf_op jit(solution)/shard_map/all_to_all | solution.py:100
  310.5 2.7 copy.59
  313.2 0.0 copy-start.4
  313.2 0.6 bitcast_multiply_fusion
  313.8 1.6 copy-done.4
  315.4 3.5 fusion.76
  318.9 1.2 fusion.75
  320.1 2.1 copy.84
  322.1 1.8 copy.85
  323.9 16.9 %fusion.51 = f32[4,512,2,64]{3,0,2,1:T(4,128)} fusion(bf16[512,64,64,1]{2,1,3,0:T(8,128)(2,1)} %copy.75, f32[4,512,2,1,64]{4,0,2,1,3:T(4,128)} %copy.85, f32[4,512,2,1,64]{4,0,2,1,3:T(4,128)S(1)} %copy.84, f32[512,64]{1,0:T(8,128)S(1)} %broadcast_divide_fusion), kind=kOutput, calls=%fused_computation.73 | convolution fusion | flops 201850880 | bytes 7471104 | tf_op jit(solution)/shard_map/lrs,klqs->klqr/dot_general | solution.py:115
  340.8 1.9 copy.64
  342.7 6.4 %convolution_bitcast_fusion = f32[4,1024,128]{1,2,0:T(8,128)S(1)} fusion(f32[4,512,128]{1,2,0:T(8,128)S(1)} %bitcast.110, bf16[4,1024,512]{2,1,0:T(8,128)(2,1)} %param.8), kind=kOutput, calls=%fused_computation.72 | convolution fusion | flops 3221225472 | bytes 7340032 | tf_op jit(solution)/shard_map/ktl,klx->ktx/dot_general | solution.py:121
  349.1 1.8 copy.65
  350.9 1.8 copy.66
  352.7 2.7 copy.67
  355.4 5.8 %all-to-all-start.2 = ((f32[4,1024,128]{2,0,1:T(4,128)}), f32[4,1024,128]{2,0,1:T(4,128)S(1)}, u32[]{:S(2)}, u32[]{:S(2)}) async-start(f32[4,1024,128]{2,0,1:T(4,128)} %copy.67), calls=%async_computation.2 | async-start | bytes 4194304 | tf_op jit(solution)/shard_map/all_to_all | solution.py:129
  361.2 19.1 %cosine_multiply_fusion = (f32[1,512,2048]{2,1,0:T(8,128)}, f32[1,512,2048]{2,1,0:T(8,128)}) fusion(s32[512]{0:T(512)S(1)} %reshape.391, f32[512]{0:T(512)S(1)} %get-tuple-element.17, f32[512]{0:T(512)S(1)} %get-tuple-element.18), kind=kLoop, calls=%fused_computation.44 | loop fusion | flops 16777216 | bytes 8394752 | tf_op jit(solution)/shard_map/mul | solution.py:52
  380.3 11.3 %all-to-all-done.2 = f32[4,1024,128]{2,0,1:T(4,128)S(1)} async-done(((f32[4,1024,128]{2,0,1:T(4,128)}), f32[4,1024,128]{2,0,1:T(4,128)S(1)}, u32[]{:S(2)}, u32[]{:S(2)}) %all-to-all-start.2) | async-done | bytes 2097184 | tf_op jit(solution)/shard_map/all_to_all | solution.py:129
  391.6 0.1 copy.101
  391.8 0.3 copy.69
  392.1 3.7 reshape.399
  395.7 21.0 %fusion.31 = f32[64,8,2048]{2,0,1:T(8,128)} fusion(f32[512,8,2,64]{3,2,1,0:T(2,128)} %reshape.399, f32[1,512,2048]{2,1,0:T(8,128)} %get-tuple-element.16, f32[1,512,2048]{2,1,0:T(8,128)} %get-tuple-element.15), kind=kOutput, calls=%fused_computation.52 | convolution fusion | flops 12886999040 | bytes 14680064 | tf_op jit(solution)/shard_map/ktqr,qkp->rtp/dot_general | solution.py:132
  416.8 7.0 %copy.71 = f32[64,8,2048]{0,1,2:T(8,128)} copy(f32[64,8,2048]{2,0,1:T(8,128)} %fusion.31) | data formatting | bytes 8388608 | tf_op jit(solution)/shard_map/ktqr,qkp->rtp/transpose | solution.py:132
  423.7 10.0 %reshape.410 = f32[8,1,131072]{2,1,0:T(1,128)} reshape(f32[2048,8,64]{2,1,0:T(8,128)} %bitcast.101) | data formatting | bytes 8388608
  433.8 53.6 %all_to_all.66 = f32[8,1,131072]{2,1,0:T(1,128)} all-to-all(f32[8,1,131072]{2,1,0:T(1,128)} %reshape.410), channel_id=1, replica_groups=mesh['az'=8,'col'=16] {'az'}, dimensions={0} | all-to-all | bytes 8388608 | tf_op jit(solution)/shard_map/all_to_all | solution.py:133
  487.4 0.6 broadcast.379
  488.0 13.8 %reduce = f32[8,131072]{1,0:T(8,128)} reduce(f32[8,1,131072]{2,1,0:T(1,128)} %all_to_all.66, f32[]{:T(128)} %broadcast.379), dimensions={1}, to_apply=%all_to_all.58.reduce_sub_computation | reduce | bytes 8388612 | tf_op jit(solution)/shard_map/all_to_all | solution.py:133
  501.8 8.7 %reshape.411 = f32[2048,8,64]{2,1,0:T(8,128)} reshape(f32[8,131072]{1,0:T(8,128)} %reduce) | data formatting | bytes 8388608
  510.5 7.6 %copy.72 = f32[64,8,8,256]{3,2,1,0:T(8,128)} copy(f32[64,8,8,256]{0,2,3,1:T(8,128)} %bitcast.102) | data formatting | bytes 8388608 | tf_op jit(solution)/shard_map/all_to_all | solution.py:133
  (17 shorter events, 0.1 us)
Async XLA Ops:
  6.5 14.5 %collective-permute-start = (f32[64,64,1]{1,0,2:T(8,128)S(1)}, f32[64,64,1]{1,0,2:T(8,128)S(1)}, u32[]{:S(2)}, u32[]{:S(2)}) collective-permute-start(f32[64,64,1]{1,0,2:T(8,128)S(1)} %copy.81), channel_id=1, source_target_pairs={{0,16},{16,32},{32,48},{48,64},{64,80},{80,96},{96,112},{112,0},{1... | collective-permute-start | bytes 49160 | tf_op jit(solution)/shard_map/ppermute | solution.py:19
  8.9 7.6 %copy-start = (f32[64,64,256]{2,1,0:T(8,128)S(1)}, f32[64,64,256]{2,1,0:T(8,128)}, u32[]{:S(2)}) copy-start(f32[64,64,256]{2,1,0:T(8,128)} %param.5) | copy-start | bytes 12582916
  8.9 14.0 %collective-permute-start.1 = (f32[64,64,1]{1,0,2:T(8,128)S(1)}, f32[64,64,1]{1,0,2:T(8,128)S(1)}, u32[]{:S(2)}, u32[]{:S(2)}) collective-permute-start(f32[64,64,1]{1,0,2:T(8,128)S(1)} %copy.82), channel_id=1, source_target_pairs={{16,0},{32,16},{48,32},{64,48},{80,64},{96,80},{112,96},{0,112},{1... | collective-permute-start | bytes 49160 | tf_op jit(solution)/shard_map/ppermute | solution.py:22
  25.8 9.3 %copy-start.2 = (f32[64,64,256]{2,0,1:T(8,128)S(1)}, f32[64,64,256]{2,0,1:T(8,128)}, u32[]{:S(2)}) copy-start(f32[64,64,256]{2,0,1:T(8,128)} %copy.50) | copy-start | bytes 12582916
  25.8 9.3 %copy-start.3 = (f32[64,64,1]{2,0,1:T(8,128)S(1)}, f32[64,64,1]{2,0,1:T(8,128)}, u32[]{:S(2)}) copy-start(f32[64,64,1]{2,0,1:T(8,128)} %copy.48) | copy-start | bytes 49156
  27.0 7.7 %collective-permute-start.2 = (f32[64,1,258]{2,0,1:T(8,128)S(1)}, f32[64,1,258]{2,0,1:T(8,128)S(1)}, u32[]{:S(2)}, u32[]{:S(2)}) collective-permute-start(f32[64,1,258]{2,0,1:T(8,128)S(1)} %get-tuple-element.5), channel_id=1, source_target_pairs={{0,1},{1,2},{2,3},{3,4},{4,5},{5,6},{6,7},{7,8},{8,9},{9,10},{10,1... | collective-permute-start | bytes 198152 | tf_op jit(solution)/shard_map/ppermute | solution.py:19
  27.1 8.1 %collective-permute-start.3 = (f32[64,1,258]{2,0,1:T(8,128)S(1)}, f32[64,1,258]{2,0,1:T(8,128)S(1)}, u32[]{:S(2)}, u32[]{:S(2)}) collective-permute-start(f32[64,1,258]{2,0,1:T(8,128)S(1)} %get-tuple-element.6), channel_id=1, source_target_pairs={{1,0},{2,1},{3,2},{4,3},{5,4},{6,5},{7,6},{8,7},{9,8},{10,9},{11,1... | collective-permute-start | bytes 198152 | tf_op jit(solution)/shard_map/ppermute | solution.py:22
  33.0 5.4 %copy-start.1 = (f32[64,64,256]{2,1,0:T(8,128)S(1)}, f32[64,64,256]{2,1,0:T(8,128)}, u32[]{:S(2)}) copy-start(f32[64,64,256]{2,1,0:T(8,128)} %param.5) | copy-start | bytes 12582916
  55.2 5.3 %copy-start.5 = (s32[128,4]{0,1:T(4,128)S(1)}, s32[128,4]{0,1:T(4,128)}, u32[]{:S(2)}) copy-start(s32[128,4]{0,1:T(4,128)} %param.7) | copy-start | bytes 6148
  55.2 98.5 %all-to-all-start = ((f32[2,64,64,256]{3,1,0,2:T(8,128)}), f32[2,64,64,256]{3,1,0,2:T(8,128)}, u32[]{:S(2)}, u32[]{:S(2)}) async-start(f32[2,64,64,256]{3,1,0,2:T(8,128)} %pad_maximum_fusion), calls=%async_computation | async-start | bytes 16777216 | tf_op jit(solution)/shard_map/all_to_all | solution.py:95
  216.9 93.6 %all-to-all-start.1 = ((f32[512,8,256]{2,1,0:T(8,128)}), f32[512,8,256]{2,1,0:T(8,128)}, u32[]{:S(2)}, u32[]{:S(2)}) async-start(f32[512,8,256]{2,1,0:T(8,128)} %copy.57), calls=%async_computation.1 | async-start | bytes 8388608 | tf_op jit(solution)/shard_map/all_to_all | solution.py:100
  313.2 2.2 copy-start.4
  355.4 36.2 %all-to-all-start.2 = ((f32[4,1024,128]{2,0,1:T(4,128)}), f32[4,1024,128]{2,0,1:T(4,128)S(1)}, u32[]{:S(2)}, u32[]{:S(2)}) async-start(f32[4,1024,128]{2,0,1:T(4,128)} %copy.67), calls=%async_computation.2 | async-start | bytes 4194304 | tf_op jit(solution)/shard_map/all_to_all | solution.py:129
where the time goes:
time: 526 us; the launch traced here: 519 us
  local copies, waits for them, and re-layouts  120 us (23%)
  waiting for transfers between devices  118 us (22%)
  matrix products  90.4 us (17%)
  other arithmetic  73 us (14%)
  starting transfers between devices  62.5 us (12%)
  blocking collectives  53.6 us (10%)
    all_to_all x1, waiting for transfers between devices, body(): lax.all_to_all(fields, 'az', split_axis=2, concat_axis=3, tiled=True)  75 us
    all_to_all x1, blocking collectives, body(): lax.all_to_all(row_fields, 'az', split_axis=2, concat_axis=1, tiled=True)  53.6 us
    unnamed x21, local copies, waits for them, and re-layouts  44.7 us
    all_to_all x1, starting transfers between devices, body(): lax.all_to_all(spectra, ('az', 'col'), split_axis=0, concat_axis=1, tiled...  41 us
    dot_general x1, matrix products, body(): jnp.einsum('frtp,pqk->ktqfr', lax.all_to_all(fields, 'az', split_axis=2,...  32.8 us
    all_to_all x1, waiting for transfers between devices, body(): lax.all_to_all(spectra, ('az', 'col'), split_axis=0, concat_axis=1, tiled...  29.5 us
    all_to_all x2, local copies, waits for them, and re-layouts, body(): lax.all_to_all(fields, 'az', split_axis=2, concat_axis=3, tiled=True)  22.5 us
    dot_general x1, matrix products, body(): jnp.einsum('ktqr,qkp->rtp', grid_modes, inverse_table, precision=highest_...  21 us
  transfers between devices with their start and end apart: 7, of which 5 were waited for; matrix products, arithmetic and copies ran while one was open for 14% of the time, Pallas kernels for 0%

commit v1 on v0

v1 whole, which is shorter than its diff:
```python
import math

import jax
import jax.numpy as jnp
import numpy as np
from jax import lax
from jax.experimental import pallas as pl
from jax.experimental.pallas import tpu as pltpu
from jax.sharding import PartitionSpec as P

step_time = 0.002
mobility_step = 4e-06
f32 = jnp.float32
bf16 = jnp.bfloat16
everyone = ("az", "col")


def params(mib=48):
    return pltpu.CompilerParams(vmem_limit_bytes=mib * 1024 * 1024)


def colat_weights(count):
    theta = math.pi * (np.arange(count) + 0.5) / count
    waves = np.arange(1, count // 2 + 1)
    total = (np.cos(2.0 * waves[None, :] * theta[:, None]) / (4.0 * waves * waves - 1.0)).sum(1)
    return 2.0 / count * (1.0 - 2.0 * total)


def shell_radii(shells):
    return 0.75 + 0.25 * (np.arange(shells) + 0.5) / shells


def split(x):
    hi = x.astype(bf16)
    return hi, (x - hi.astype(f32)).astype(bf16)


def dot_nn(a, b):
    return lax.dot_general(a, b, (((1,), (0,)), ((), ())), preferred_element_type=f32)


def dot_nt(a, b):
    return lax.dot_general(a, b, (((1,), (1,)), ((), ())), preferred_element_type=f32)


def swap_halves(a, b):
    half = lax.broadcasted_iota(jnp.int32, a.shape, 1) < 64
    first = jnp.where(half, a, pltpu.roll(b, 64, 1))
    second = jnp.where(half, pltpu.roll(a, 64, 1), b)
    return first, second


def edges_kernel(c_ref, west_ref, east_ref, north_ref, south_ref):
    shells, rows, cols = c_ref.shape
    block = pl.program_id(0)
    lane = lax.broadcasted_iota(jnp.int32, (rows, 128), 1)
    west = jnp.where(block == 0, 0.0, west_ref[...])
    east = jnp.where(block == 0, 0.0, east_ref[...])
    for k in range(shells):
        at = block * shells + k
        west = jnp.where(lane == at, pltpu.roll(c_ref[k, :, :128], at, 1), west)
        east = jnp.where(lane == at, pltpu.roll(c_ref[k, :, cols - 128 :], at + 1, 1), east)
    west_ref[...] = west
    east_ref[...] = east
    north_ref[...] = c_ref[:, 0, :]
    south_ref[...] = c_ref[:, rows - 1, :]


def edges_stage(phase):
    shells, rows, cols = phase.shape
    kb = 16
    return pl.pallas_call(
        edges_kernel,
        grid=(shells // kb,),
        in_specs=[pl.BlockSpec((kb, rows, cols), lambda i: (i, 0, 0))],
        out_specs=[
            pl.BlockSpec((rows, 128), lambda i: (0, 0)),
            pl.BlockSpec((rows, 128), lambda i: (0, 0)),
            pl.BlockSpec((kb, cols), lambda i: (i, 0)),
            pl.BlockSpec((kb, cols), lambda i: (i, 0)),
        ],
        out_shape=[
            jax.ShapeDtypeStruct((rows, 128), f32),
            jax.ShapeDtypeStruct((rows, 128), f32),
            jax.ShapeDtypeStruct((shells, cols), f32),
            jax.ShapeDtypeStruct((shells, cols), f32),
        ],
        compiler_params=params(61),
        name="edges",
    )(phase)


def potential_kernel(c_ref, w_ref, out_ref):
    shells, rows, cols = c_ref.shape
    weights = w_ref[...]
    for k in range(shells):
        x = c_ref[k]
        y = (x * x * x - x) * weights
        for a in range(rows // 8):
            for h in range(cols // 128):
                out_ref[a, k, h] = y[8 * a : 8 * a + 8, 128 * h : 128 * h + 128]


def potential_stage(phase, weights):
    shells, rows, cols = phase.shape
    kb = 8
    return pl.pallas_call(
        potential_kernel,
        grid=(shells // kb,),
        in_specs=[
            pl.BlockSpec((kb, rows, cols), lambda i: (i, 0, 0)),
            pl.BlockSpec((rows, cols), lambda i: (0, 0)),
        ],
        out_specs=pl.BlockSpec((rows // 8, kb, cols // 128, 8, 128), lambda i: (0, i, 0, 0, 0)),
        out_shape=jax.ShapeDtypeStruct((rows // 8, shells, cols // 128, 8, 128), f32),
        compiler_params=params(61),
        name="potential",
    )(phase, weights)


def advect_kernel(scale_phi, scale_ref, c_ref, v_ref, w_ref, west_ref, east_ref, north_ref, south_ref, out_ref):
    shells, rows, cols = c_ref.shape
    block = pl.program_id(0)
    weights = w_ref[...]
    lane = lax.broadcasted_iota(jnp.int32, (rows, cols), 1)
    row = lax.broadcasted_iota(jnp.int32, (rows, cols), 0)
    turn = jnp.where(block == 0, 0, 128 - block * shells)
    west_all = pltpu.roll(west_ref[...], turn, 1)
    east_all = pltpu.roll(east_ref[...], turn, 1)
    for k in range(shells):
        x = c_ref[k]
        west_edge = jnp.broadcast_to(west_all[:, k : k + 1], (rows, cols))
        east_edge = jnp.broadcast_to(east_all[:, k : k + 1], (rows, cols))
        west = jnp.where(lane == 0, west_edge, pltpu.roll(x, 1, 1))
        east = jnp.where(lane == cols - 1, east_edge, pltpu.roll(x, cols - 1, 1))
        north = jnp.where(row == 0, north_ref[k : k + 1, :], pltpu.roll(x, 1, 0))
        south = jnp.where(row == rows - 1, south_ref[k : k + 1, :], pltpu.roll(x, rows - 1, 0))
        spin = v_ref[0, k].astype(f32)
        sweep = v_ref[1, k].astype(f32)
        scale_theta = scale_ref[block * shells + k]
        y = x - (spin * ((east - west) * scale_phi) + sweep * ((south - north) * scale_theta))
        y = y * weights
        for a in range(rows // 8):
            for h in range(cols // 128):
                out_ref[a, k, h] = y[8 * a : 8 * a + 8, 128 * h : 128 * h + 128]


def advect_stage(phase, velocity, weights, west, east, north, south, scale_phi, scale_theta):
    shells, rows, cols = phase.shape
    kb = 8

    def kernel(*refs):
        advect_kernel(scale_phi, *refs)

    return pl.pallas_call(
        kernel,
        grid=(shells // kb,),
        in_specs=[
            pl.BlockSpec(memory_space=pltpu.SMEM),
            pl.BlockSpec((kb, rows, cols), lambda i: (i, 0, 0)),
            pl.BlockSpec((2, kb, rows, cols), lambda i: (0, i, 0, 0)),
            pl.BlockSpec((rows, cols), lambda i: (0, 0)),
            pl.BlockSpec((rows, 128), lambda i: (0, 0)),
            pl.BlockSpec((rows, 128), lambda i: (0, 0)),
            pl.BlockSpec((kb, cols), lambda i: (i, 0)),
            pl.BlockSpec((kb, cols), lambda i: (i, 0)),
        ],
        out_specs=pl.BlockSpec((rows // 8, kb, cols // 128, 8, 128), lambda i: (0, i, 0, 0, 0)),
        out_shape=jax.ShapeDtypeStruct((rows // 8, shells, cols // 128, 8, 128), f32),
        compiler_params=params(61),
        name="advect",
    )(scale_theta, phase, velocity, weights, west, east, north, south)


def fourier_kernel(p_ref, table_ref, *rest):
    out_ref, xh, xl, ysc = rest[-4:]
    parts = p_ref.shape[0]
    half = parts // 2
    per = xh.shape[0] // 8
    tiles = xh.shape[1] // half // 128
    sign = jnp.where(pl.program_id(0) == 0, 1.0, -1.0).astype(f32)
    for a in range(half):
        for t in range(8):
            for j in range(tiles):
                strided = pl.ds(8 * j + t, per, stride=8 * tiles)
                x = p_ref[a, strided, :] + sign * p_ref[a + half, strided, :]
                h, l = split(x)
                lanes = slice((a * tiles + j) * 128, (a * tiles + j + 1) * 128)
                xh[t * per : (t + 1) * per, lanes] = h
                xl[t * per : (t + 1) * per, lanes] = l
    ph, plo = xh[...], xl[...]
    both = table_ref.shape[1] // 2
    count = both // 2
    y = dot_nt(table_ref[0], ph)
    y = y[:both] + (y[both:] + dot_nt(table_ref[0, :both], plo))
    for u in range(4):
        first, second = swap_halves(y[:count, 128 * u : 128 * u + 128], y[count:, 128 * u : 128 * u + 128])
        ysc[pl.ds(2 * u, count, stride=8), :] = first
        ysc[pl.ds(2 * u + 1, count, stride=8), :] = second
    owners = count // 2
    for s in range(2):
        out_ref[:, 0, 0, s] = ysc[s * owners * 8 : (s + 1) * owners * 8, :].reshape(owners, 8, 128)


def fourier_stage(rows_all, table, field, buffer):
    parts, shells, tiles, tb, _ = rows_all.shape
    half_phi = table.shape[2]
    modes2 = table.shape[1] // 2
    owners = modes2 // 4
    flat = rows_all.reshape(parts, shells * tiles * tb, 128)
    in_specs = [
        pl.BlockSpec((parts, shells * tiles * tb, 128), lambda i: (0, 0, 0)),
        pl.BlockSpec((1, 2 * modes2, half_phi), lambda i: (i, 0, 0)),
    ]
    args = [flat, table]
    aliases = {}
    if buffer is not None:
        in_specs.append(pl.BlockSpec(memory_space=pl.ANY))
        args.append(buffer)
        aliases = {2: 0}
    return pl.pallas_call(
        fourier_kernel,
        grid=(2,),
        in_specs=in_specs,
        out_specs=pl.BlockSpec((owners, 1, 1, 2, 8, 128), lambda i: (0, field, i, 0, 0, 0)),
        out_shape=jax.ShapeDtypeStruct((owners, 2, 2, 2, 8, 128), f32),
        scratch_shapes=[
            pltpu.VMEM((shells * tb, half_phi), bf16),
            pltpu.VMEM((shells * tb, half_phi), bf16),
            pltpu.VMEM((modes2 * 4, 128), f32),
        ],
        input_output_aliases=aliases,
        compiler_params=params(61),
        name="fourier" + str(field),
    )(*args)


def spectral_kernel(az, col, sel_ref, r_ref, legt_ref, leg_ref, rad_ref, fac_ref, out_ref, xh, xl, rhs, sol, radf):
    step = pl.program_id(0)
    degrees = legt_ref.shape[1]
    shells = rad_ref.shape[0]
    theta = legt_ref.shape[2]
    tb = az * 8

    @pl.when(step < 4)
    def _():
        for f in range(2):
            for c in range(col):
                x = jnp.concatenate([r_ref[a * col + c, f, 0, 0] for a in range(az)], axis=0)
                h, l = split(x)
                xh[c * tb : (c + 1) * tb, f * 128 : (f + 1) * 128] = h
                xl[c * tb : (c + 1) * tb, f * 128 : (f + 1) * 128] = l
        leg = legt_ref[0]
        coef = dot_nn(leg, xh[...]) + dot_nn(leg, xl[...])
        right = (coef[:, :128] - fac_ref[...] * coef[:, 128:]).T
        for q in range(4):

            @pl.when(step == q)
            def _():
                for i in range(2):
                    for lt in range(degrees // 128):
                        rhs[lt, pl.ds(2 * q + i, shells, stride=8), :] = right[
                            i * shells : (i + 1) * shells, lt * 128 : lt * 128 + 128
                        ]

    @pl.when(step == 3)
    def _():
        rb = 8

        def outer(block, carry):
            radf[...] = rad_ref[pl.ds(block * rb, rb)].astype(f32)
            for lt in range(degrees // 128):
                lanes = slice(lt * 128, lt * 128 + 128)
                acc = [jnp.zeros((8, 128), f32) for _ in range(rb)]
                for s in range(shells):
                    v = rhs[lt, 8 * s : 8 * s + 8, :]
                    for r in range(rb):
                        acc[r] = acc[r] + radf[r, s : s + 1, lanes] * v
                for r in range(rb):
                    sol[lt, pl.ds(pl.multiple_of((block * rb + r) * 8, 8), 8), :] = acc[r]
            return carry

        lax.fori_loop(0, shells // rb, outer, 0)

    for q in range(4):

        @pl.when(step == 4 + q)
        def _():
            gain = sel_ref[4 + q].astype(f32)
            x = jnp.concatenate(
                [
                    jnp.concatenate(
                        [sol[lt, pl.ds(2 * q + i, shells, stride=8), :] for lt in range(degrees // 128)], axis=1
                    )
                    for i in range(2)
                ],
                axis=0,
            )
            h, l = split(x * gain)
            leg = leg_ref[0]
            y = dot_nt(leg, h) + dot_nt(leg, l)
            for c in range(col):
                for a in range(az):
                    out_ref[a * col + c, 0] = y[c * tb + a * 8 : c * tb + a * 8 + 8]


def spectral_stage(received, legendre_t, legendre, radial, factor, select, az, col):
    owners = received.shape[0]
    modes, theta, degrees = legendre.shape
    shells = radial.shape[0]

    def first(i):
        return jnp.minimum(i, 3)

    def last(i):
        return jnp.maximum(i - 4, 0)

    def kernel(*refs):
        spectral_kernel(az, col, *refs)

    return pl.pallas_call(
        kernel,
        grid_spec=pltpu.PrefetchScalarGridSpec(
            num_scalar_prefetch=1,
            grid=(8,),
            in_specs=[
                pl.BlockSpec((owners, 2, 1, 1, 8, 128), lambda i, s: (0, 0, first(i) // 2, first(i) % 2, 0, 0)),
                pl.BlockSpec((1, degrees, theta), lambda i, s: (s[first(i)], 0, 0)),
                pl.BlockSpec((1, theta, degrees), lambda i, s: (s[last(i)], 0, 0)),
                pl.BlockSpec((shells, shells, degrees), lambda i, s: (0, 0, 0)),
                pl.BlockSpec((degrees, 2 * shells), lambda i, s: (0, 0)),
            ],
            out_specs=pl.BlockSpec((owners, 1, 8, 128), lambda i, s: (0, last(i), 0, 0)),
            scratch_shapes=[
                pltpu.VMEM((theta, 256), bf16),
                pltpu.VMEM((theta, 256), bf16),
                pltpu.VMEM((degrees // 128, 8 * shells, 128), f32),
                pltpu.VMEM((degrees // 128, 8 * shells, 128), f32),
                pltpu.VMEM((8, shells, degrees), f32),
            ],
        ),
        out_shape=jax.ShapeDtypeStruct((owners, 4, 8, 128), f32),
        compiler_params=params(61),
        name="spectral",
    )(select, received, legendre_t, legendre, radial, factor)


def inverse_kernel(z_ref, table_ref, out_ref, gh, gl):
    owners = z_ref.shape[0] // 32
    rows = gh.shape[1]
    per = rows // 8

    @pl.when(pl.program_id(0) == 0)
    def _():
        for par in range(2):
            halves = [[], []]
            for s in range(2):
                base = (par * 2 + s) * 8
                cos_u, sin_u = [], []
                for u in range(4):
                    a = z_ref[pl.ds(base + 2 * u, owners, stride=32), :]
                    b = z_ref[pl.ds(base + 2 * u + 1, owners, stride=32), :]
                    first, second = swap_halves(a, b)
                    cos_u.append(first)
                    sin_u.append(second)
                halves[0].append(jnp.concatenate(cos_u, axis=1))
                halves[1].append(jnp.concatenate(sin_u, axis=1))
            for i in range(2):
                for s in range(2):
                    h, l = split(halves[i][s].T)
                    at = (2 * i + s) * owners
                    gh[par, :, at : at + owners] = h
                    gl[par, :, at : at + owners] = l

    sums = []
    for par in range(2):
        both = table_ref.shape[1] // 2
        th, tl = table_ref[par, :both], table_ref[par, both:]
        h, l = gh[par], gl[par]
        sums.append(dot_nn(h, th) + (dot_nn(h, tl) + dot_nn(l, th)))
    near = sums[0] + sums[1]
    far = sums[0] - sums[1]
    tiles = near.shape[1] // 128
    for t in range(8):
        for j in range(tiles):
            lanes = slice(j * 128, j * 128 + 128)
            strided = pl.ds(8 * j + t, per, stride=8 * tiles)
            out_ref[0, 0, strided, :] = near[t * per : (t + 1) * per, lanes]
            out_ref[1, 0, strided, :] = far[t * per : (t + 1) * per, lanes]


def inverse_stage(received, table, shells, az):
    owners, _, tb, _ = received.shape
    half_phi = table.shape[2]
    modes2 = table.shape[1] // 2
    flat = received.reshape(owners * 4 * tb, 128)
    cols = 2 * half_phi // az
    rows = shells * tb
    out = pl.pallas_call(
        inverse_kernel,
        grid=(az // 2,),
        in_specs=[
            pl.BlockSpec((owners * 4 * tb, 128), lambda i: (0, 0)),
            pl.BlockSpec((2, 2 * modes2, cols), lambda i: (0, 0, i)),
        ],
        out_specs=pl.BlockSpec((2, 1, rows * cols // 128, 128), lambda i: (0, i, 0, 0)),
        out_shape=jax.ShapeDtypeStruct((2, az // 2, rows * cols // 128, 128), f32),
        scratch_shapes=[
            pltpu.VMEM((2, rows, modes2), bf16),
            pltpu.VMEM((2, rows, modes2), bf16),
        ],
        compiler_params=params(24),
        name="inverse",
    )(flat, table)
    return out.reshape(az, shells, cols // 128, tb, 128)


def gather_kernel(w_ref, out_ref):
    parts, shells = w_ref.shape[:2]
    for k in range(shells):
        for a in range(parts):
            for h in range(w_ref.shape[2]):
                out_ref[k, 8 * a : 8 * a + 8, 128 * h : 128 * h + 128] = w_ref[a, k, h]


def gather_stage(blocks):
    parts, shells, tiles, tb, _ = blocks.shape
    cols = tiles * 128
    kb = 8
    return pl.pallas_call(
        gather_kernel,
        grid=(shells // kb,),
        in_specs=[pl.BlockSpec((parts, kb, tiles, tb, 128), lambda i: (0, i, 0, 0, 0))],
        out_specs=pl.BlockSpec((kb, parts * tb, cols), lambda i: (i, 0, 0)),
        out_shape=jax.ShapeDtypeStruct((shells, parts * tb, cols), f32),
        compiler_params=params(16),
        name="gather",
    )(blocks)


def exchange(x, axes):
    return lax.all_to_all(x, axes, split_axis=0, concat_axis=0, tiled=True)


def wave_tables(owned_modes, phi_count):
    first_half = owned_modes[:, :2].T.reshape(-1)
    top = owned_modes.shape[0] * owned_modes.shape[1] - 1
    even = jnp.where(first_half % 2 == 0, first_half, top - first_half)
    modes = jnp.stack([even, top - even])
    phi_index = jnp.arange(phi_count // 2, dtype=jnp.int32)
    quarter = jnp.arange(2, dtype=jnp.int32) * (phi_count // 4)
    turns = modes[:, None, :, None] * phi_index + quarter[None, :, None, None]
    turns = turns % phi_count
    table = jnp.cos(turns.astype(f32) * (2.0 * math.pi / phi_count))
    table = table.reshape(2, -1, phi_count // 2)
    rounded = lax.reduce_precision(table, 8, 7)
    return jnp.concatenate([rounded.astype(bf16), (table - rounded).astype(bf16)], axis=1)


def body(phase_field, velocity, owned_modes, legendre, radial_inverse):
    shells, theta_local, phi_local = phase_field.shape
    az_count = lax.axis_size("az")
    col_count = lax.axis_size("col")
    az_here = lax.axis_index("az")
    col_here = lax.axis_index("col")
    phi_count = phi_local * az_count
    theta_count = theta_local * col_count
    degree_count = legendre.shape[2]
    radius = shell_radii(shells)

    weights = jnp.asarray((colat_weights(theta_count) / phi_count).astype(np.float32))
    weights = lax.dynamic_slice(weights, (col_here * theta_local,), (theta_local,))
    weights = jnp.broadcast_to(weights[:, None], (theta_local, phi_local))

    west_out, east_out, north_out, south_out = edges_stage(phase_field)
    forward_az = [(i, (i + 1) % az_count) for i in range(az_count)]
    backward_az = [(target, source) for source, target in forward_az]
    forward_col = [(i, i + 1) for i in range(col_count - 1)]
    backward_col = [(target, source) for source, target in forward_col]
    west = lax.ppermute(east_out, "az", forward_az)
    east = lax.ppermute(west_out, "az", backward_az)
    north = lax.ppermute(south_out, "col", forward_col)
    south = lax.ppermute(north_out, "col", backward_col)
    potential = potential_stage(phase_field, weights)
    potential, west, east, north, south = lax.optimization_barrier((potential, west, east, north, south))
    rows_potential = exchange(potential, "az")

    scale_phi = step_time * phi_count / (4.0 * math.pi)
    scale_theta = jnp.asarray((step_time * theta_count / (2.0 * math.pi) / radius).astype(np.float32))
    advected = advect_stage(
        phase_field, velocity, weights, west, east, north, south, scale_phi, scale_theta
    )
    table = wave_tables(owned_modes, phi_count)
    rows_advected = exchange(advected, "az")

    spectra = fourier_stage(rows_potential, table, 1, None)
    spectra = fourier_stage(rows_advected, table, 0, spectra)
    received = exchange(spectra, everyone)

    here = az_here * col_count + col_here
    mine = lax.dynamic_slice(owned_modes, (here, 0), (1, owned_modes.shape[1]))[0]
    odd = mine[:2] % 2
    slot = jnp.arange(2, dtype=jnp.int32)
    even_slot = slot + 2 * odd
    odd_slot = slot + 2 * (1 - odd)
    slots = jnp.concatenate([even_slot, odd_slot])
    top = owned_modes.shape[0] * owned_modes.shape[1] - 1
    even_mode = jnp.where(odd == 0, mine[:2], top - mine[:2])
    gains = jnp.concatenate([jnp.where(even_mode == 0, 1, 2), jnp.full((2,), 2, jnp.int32)])
    select = jnp.concatenate([slots, gains]).astype(jnp.int32)
    degrees = np.arange(degree_count)
    factor = mobility_step * (degrees * (degrees + 1.0))[:, None] / (radius * radius)[None, :]
    factor = jnp.asarray(np.concatenate([factor, factor], axis=1).astype(np.float32))
    legendre_t = jnp.transpose(legendre, (0, 2, 1))
    radial = jnp.transpose(radial_inverse, (1, 2, 0))
    synthesis = spectral_stage(
        received, legendre_t, legendre, radial, factor, select, az_count, col_count
    )
    grid_modes = exchange(synthesis, everyone)

    blocks = inverse_stage(grid_modes, table, shells, az_count)
    return gather_stage(exchange(blocks, "az"))


def solution(mesh):
    in_specs = (
        P(None, "col", "az"),
        P(None, None, "col", "az"),
        P(),
        P(("az", "col"), None, None),
        P(),
    )
    out_specs = P(None, "col", "az")
    return jax.shard_map(body, mesh=mesh, in_specs=in_specs, out_specs=out_specs, check_vma=False)
```

time: 526 us -> 349 us (0.66); the launches traced: 519 us -> 348 us
  local copies, waits for them, and re-layouts: 120 us -> 7.96 us
  matrix products: 90.4 us -> 0 us
  Pallas kernels: 0 us -> 71.8 us
  other arithmetic: 73 us -> 19.3 us
  blocking collectives: 53.6 us -> 87.5 us
  waiting for transfers between devices: 118 us -> 108 us
  starting transfers between devices: 62.5 us -> 53 us
    dot_general x6 -> x0, matrix products: 90.4 us -> none  [the longest x1 32.8 us: body(): jnp.einsum('frtp,pqk->ktqfr', lax.all_to_all(fields, 'az', split_axis=2,...]
    pallas_call x0 -> x8, Pallas kernels: none -> 71.8 us  [the longest x2 20.4 us: fourier_stage(): pl.pallas_call(fourier_kernel, grid=(2,), in_specs=in_specs, out_specs=pl...]
    unnamed x21 -> x15, local copies, waits for them, and re-layouts: 44.7 us -> 6.31 us
    all_to_all x1 -> x2, blocking collectives: 53.6 us -> 87.5 us  [exchange(): return lax.all_to_all(x, axes, split_axis=0, concat_axis=0, tiled=True)]
    all_to_all x6 -> x0, local copies, waits for them, and re-layouts: 31.1 us -> none  [the longest x2 22.5 us: body(): lax.all_to_all(fields, 'az', split_axis=2, concat_axis=3, tiled=True)]
    mul x6 -> x2, other arithmetic: 22.9 us -> 0.2 us  [the longest x1 0.2 us: wave_tables(): turns = modes[:, None, :, None] * phi_index + quarter[None, :, None, None]]
    cos x1 -> x0, other arithmetic: 18 us -> none  [forward_waves(): return jnp.stack([jnp.cos(angle), -jnp.sin(angle)], axis=1) / phi_count]
    another operation x2 -> x1, other arithmetic: 16.9 us -> 0.01 us  [wave_tables(): modes = jnp.stack([even, top - even])]
  transfers between devices with their start and end apart: 7 -> 7, of which waited for: 5 -> 3; matrix products, arithmetic and copies ran while one was open for 14% -> 8% of each run, Pallas kernels for 0% -> 8%
where the time goes in v1:
time: 349 us; the launch traced here: 348 us
  waiting for transfers between devices  108 us (31%)
  blocking collectives  87.5 us (25%)
  Pallas kernels  71.8 us (21%)
  starting transfers between devices  53 us (15%)
  other arithmetic  19.3 us (6%)
  local copies, waits for them, and re-layouts  7.96 us (2%)
    all_to_all x3, waiting for transfers between devices, exchange(): return lax.all_to_all(x, axes, split_axis=0, concat_axis=0, tiled=True)  108 us
    all_to_all x2, blocking collectives, exchange(): return lax.all_to_all(x, axes, split_axis=0, concat_axis=0, tiled=True)  87.5 us
    all_to_all x3, starting transfers between devices, exchange(): return lax.all_to_all(x, axes, split_axis=0, concat_axis=0, tiled=True)  45.3 us
    pallas_call x2, Pallas kernels, fourier_stage(): pl.pallas_call(fourier_kernel, grid=(2,), in_specs=in_specs, out_specs=pl...  20.4 us
    pallas_call x1, Pallas kernels, spectral_stage(): pl.pallas_call(kernel, grid_spec=pltpu.PrefetchScalarGridSpec(num_scalar_...  18.7 us
    convert_element_type x1, other arithmetic, wave_tables(): rounded.astype(bf16)  15.4 us
    pallas_call x1, Pallas kernels, advect_stage(): pl.pallas_call(kernel, grid=(shells // kb,), in_specs=[pl.BlockSpec(memor...  9.36 us
    pallas_call x1, Pallas kernels, inverse_stage(): pl.pallas_call(inverse_kernel, grid=(az // 2,), in_specs=[pl.BlockSpec((o...  8.5 us
  transfers between devices with their start and end apart: 7, of which 3 were waited for; matrix products, arithmetic and copies ran while one was open for 8% of the time, Pallas kernels for 8%

profile of v1, /device:TPU:0, one launch (start us, length us, event | category | flops | bytes accessed | tf_op | source)
XLA Modules:
  0.0 348.2 jit_solution(16446274585899775963)
XLA Ops:
  0.0 4.4 %edges.1 = (f32[64,128]{1,0:T(8,128)}, f32[64,128]{1,0:T(8,128)}, f32[64,256]{1,0:T(8,128)}, f32[64,256]{1,0:T(8,128)}) custom-call(f32[64,64,256]{2,1,0:T(8,128)} %refs_1_.1), custom_call_target="tpu_custom_call" | custom-call | tf_op jit(solution)/shard_map/edges/pallas_call | solution.py:72
  4.4 1.3 collective-permute-start.2
  5.7 1.3 collective-permute-start.3
  7.0 2.2 collective-permute-start
  9.1 2.9 collective-permute-start.1
  12.0 0.8 dynamic_slice.7
  12.8 0.7 broadcast_in_dim.4.w_ref.refs_3_
  13.5 6.8 %potential.1 = f32[8,64,2,8,128]{4,3,2,1,0:T(8,128)} custom-call(f32[64,64,256]{2,1,0:T(8,128)} %refs_1_.1, f32[64,256]{1,0:T(8,128)} %broadcast_in_dim.4.w_ref.refs_3_), custom_call_target="tpu_custom_call" | custom-call | tf_op jit(solution)/shard_map/potential/pallas_call | solution.py:107
  20.3 0.0 collective-permute-done.refs_4_
  20.3 0.0 copy-start.3
  20.3 0.0 collective-permute-done.1.refs_5_
  20.3 0.0 copy-start.4
  20.3 0.0 collective-permute-done.2.refs_6_
  20.3 0.0 copy-start.1
  20.3 0.0 collective-permute-done.3.refs_7_
  20.4 0.0 copy-start.2
  20.4 4.6 %all-to-all-start.1 = ((f32[8,64,2,8,128]{4,3,2,1,0:T(8,128)}), f32[8,64,2,8,128]{4,3,2,1,0:T(8,128)}, u32[]{:S(2)}, u32[]{:S(2)}) async-start(f32[8,64,2,8,128]{4,3,2,1,0:T(8,128)} %potential.1), calls=%async_computation.1 | async-start | bytes 8388608 | tf_op jit(solution)/shard_map/all_to_all | solution.py:442
  24.9 0.0 copy-done.3
  24.9 0.0 copy-done.4
  25.0 0.0 copy-done.1
  25.0 0.0 copy-done.2
  25.0 9.4 %advect.1 = f32[8,64,2,8,128]{4,3,2,1,0:T(8,128)} custom-call(f32[64]{0:T(128)} %constant.74.clone.refs_0_, f32[64,64,256]{2,1,0:T(8,128)} %refs_1_.1, bf16[2,64,64,256]{3,2,1,0:T(8,128)(2,1)} %refs_2_.1, f32[64,256]{1,0:T(8,128)} %broadcast_in_dim.4.w_ref.refs_3_, f32[64,128]{1,0:T(8,128)} %copy-done.3, f32[64,128]{1,0:T(8,128)} %copy-done.4, ...), custom_call_target="tpu_custom_call" | custom-call | tf_op jit(solution)/shard_map/advect/pallas_call | solution.py:155
  34.3 0.0 slice-start
  34.3 41.0 %all-to-all-done.1 = f32[8,64,2,8,128]{4,3,2,1,0:T(8,128)} async-done(((f32[8,64,2,8,128]{4,3,2,1,0:T(8,128)}), f32[8,64,2,8,128]{4,3,2,1,0:T(8,128)}, u32[]{:S(2)}, u32[]{:S(2)}) %all-to-all-start.1) | async-done | bytes 4194336 | tf_op jit(solution)/shard_map/all_to_all | solution.py:442
  75.4 16.6 %all-to-all-start = ((f32[8,64,2,8,128]{4,3,2,1,0:T(8,128)}), f32[8,64,2,8,128]{4,3,2,1,0:T(8,128)}, u32[]{:S(2)}, u32[]{:S(2)}) async-start(f32[8,64,2,8,128]{4,3,2,1,0:T(8,128)} %advect.1), calls=%async_computation | async-start | bytes 8388608 | tf_op jit(solution)/shard_map/all_to_all | solution.py:442
  92.0 0.1 broadcast_bitcast_fusion
  92.1 0.0 slice-done
  92.1 0.2 iota_multiply_fusion
  92.3 15.4 %reduce-precision_convert_fusion = (bf16[2,512,1024]{2,1,0:T(8,128)(2,1)S(1)}, f32[2,512,1024]{2,1,0:T(8,128)S(1)}) fusion(s32[512]{0:T(512)S(1)} %bitcast.33, s32[2,256,1024]{2,1,0:T(8,128)S(1)} %iota_multiply_fusion), kind=kLoop, calls=%fused_computation.4 | loop fusion | flops 16777216 | bytes 8390656 | tf_op jit(solution)/shard_map/convert_element_type | solution.py:457
  107.7 0.7 fusion
  108.4 2.4 pad_maximum_fusion.table_ref
  110.8 10.2 %fourier1.1.rest_0_ = f32[128,2,2,2,8,128]{5,4,3,2,1,0:T(8,128)} custom-call(f32[8,1024,128]{2,1,0:T(8,128)} %bitcast.5.p_ref, bf16[2,1024,1024]{2,1,0:T(8,128)(2,1)} %pad_maximum_fusion.table_ref), custom_call_target="tpu_custom_call" | custom-call | tf_op jit(solution)/shard_map/fourier1/pallas_call | solution.py:221
  121.1 21.6 %all-to-all-done = f32[8,64,2,8,128]{4,3,2,1,0:T(8,128)} async-done(((f32[8,64,2,8,128]{4,3,2,1,0:T(8,128)}), f32[8,64,2,8,128]{4,3,2,1,0:T(8,128)}, u32[]{:S(2)}, u32[]{:S(2)}) %all-to-all-start) | async-done | bytes 4194336 | tf_op jit(solution)/shard_map/all_to_all | solution.py:442
  142.7 10.2 %fourier0.1 = f32[128,2,2,2,8,128]{5,4,3,2,1,0:T(8,128)} custom-call(f32[8,1024,128]{2,1,0:T(8,128)} %bitcast.p_ref, bf16[2,1024,1024]{2,1,0:T(8,128)(2,1)} %pad_maximum_fusion.table_ref, f32[128,2,2,2,8,128]{5,4,3,2,1,0:T(8,128)} %fourier1.1.rest_0_), custom_call_target="tpu_custom_call", output_to_operand_aliasing={{}: (2, {})} | custom-call | tf_op jit(solution)/shard_map/fourier0/pallas_call | solution.py:221
  152.9 24.1 %all-to-all-start.2 = ((f32[128,2,2,2,8,128]{5,4,3,2,1,0:T(8,128)}), f32[128,2,2,2,8,128]{5,4,3,2,1,0:T(8,128)}, u32[]{:S(2)}, u32[]{:S(2)}) async-start(f32[128,2,2,2,8,128]{5,4,3,2,1,0:T(8,128)} %fourier0.1), calls=%async_computation.2 | async-start | bytes 8388608 | tf_op jit(solution)/shard_map/all_to_all | solution.py:442
  177.0 0.0 copy-start.5
  177.0 6.2 %copy.10 = bf16[4,1024,512]{1,2,0:T(8,128)(2,1)} copy(bf16[4,1024,512]{2,1,0:T(8,128)(2,1)} %refs_3_.1) | data formatting | bytes 8388608 | tf_op args[3]
  183.2 0.0 copy-done.5
  183.3 0.1 constant_dynamic-slice_fusion
  183.3 0.1 slice_reduce_fusion
  183.5 0.6 pad_add_fusion.1.refs_0_
  184.1 45.7 %all-to-all-done.2.refs_1_ = f32[128,2,2,2,8,128]{5,4,3,2,1,0:T(8,128)} async-done(((f32[128,2,2,2,8,128]{5,4,3,2,1,0:T(8,128)}), f32[128,2,2,2,8,128]{5,4,3,2,1,0:T(8,128)}, u32[]{:S(2)}, u32[]{:S(2)}) %all-to-all-start.2) | async-done | bytes 4194336 | tf_op jit(solution)/shard_map/all_to_all | solution.py:442
  229.8 18.7 %spectral.1 = f32[128,4,8,128]{3,2,1,0:T(8,128)} custom-call(s32[8]{0:T(128)} %pad_add_fusion.1.refs_0_, f32[128,2,2,2,8,128]{5,4,3,2,1,0:T(8,128)} %all-to-all-done.2.refs_1_, bf16[4,512,1024]{2,1,0:T(8,128)(2,1)} %bitcast.31, bf16[4,1024,512]{2,1,0:T(8,128)(2,1)} %refs_3_.1, bf16[64,64,512]{2,1,0:T(8,128)(2,1)} %bitcast.32, f32[512,128]{1,0:T(8,128)} %constant.75.clone.refs_5_), custom_call_target="tpu_custom_call" | custom-call | tf_op jit(solution)/shard_map/spectral/pallas_call | solution.py:321
  248.5 0.0 copy-start
  248.5 35.9 %all_to_all.25 = f32[128,4,8,128]{3,2,1,0:T(8,128)S(1)} all-to-all(f32[128,4,8,128]{3,2,1,0:T(8,128)} %spectral.1), channel_id=1, replica_groups=mesh['az'=8,'col'=16] {'az','col'}, dimensions={0} | all-to-all | bytes 4194304 | tf_op jit(solution)/shard_map/all_to_all | solution.py:442
  284.4 0.0 copy-done
  284.4 8.5 %inverse.1 = f32[2,4,1024,128]{3,2,1,0:T(8,128)S(1)} custom-call(f32[4096,128]{1,0:T(8,128)S(1)} %bitcast.30, bf16[2,1024,1024]{2,1,0:T(8,128)(2,1)S(1)} %copy-done), custom_call_target="tpu_custom_call" | custom-call | tf_op jit(solution)/shard_map/inverse/pallas_call | solution.py:399
  292.9 51.6 %all_to_all.26.w_ref = f32[8,64,2,8,128]{4,3,2,1,0:T(8,128)S(1)} all-to-all(f32[8,64,2,8,128]{4,3,2,1,0:T(8,128)S(1)} %bitcast.29), channel_id=1, replica_groups=mesh['az'=8,'col'=16] {'az'}, dimensions={0} | all-to-all | bytes 8388608 | tf_op jit(solution)/shard_map/all_to_all | solution.py:442
  344.6 3.7 %gather.1 = f32[64,64,256]{2,1,0:T(8,128)} custom-call(f32[8,64,2,8,128]{4,3,2,1,0:T(8,128)S(1)} %all_to_all.26.w_ref), custom_call_target="tpu_custom_call" | custom-call | tf_op jit(solution)/shard_map/gather/pallas_call | solution.py:430
  (7 shorter events, 0.1 us)
Async XLA Ops:
  4.4 16.0 %collective-permute-start.2 = (f32[64,256]{1,0:T(8,128)}, f32[64,256]{1,0:T(8,128)S(1)}, u32[]{:S(2)}, u32[]{:S(2)}) collective-permute-start(f32[64,256]{1,0:T(8,128)} %get-tuple-element.16), channel_id=1, source_target_pairs={{0,1},{1,2},{2,3},{3,4},{4,5},{5,6},{6,7},{7,8},{8,9},{9,10},{10,1... | collective-permute-start | bytes 196616 | tf_op jit(solution)/shard_map/ppermute | solution.py:482
  5.7 14.7 %collective-permute-start.3 = (f32[64,256]{1,0:T(8,128)}, f32[64,256]{1,0:T(8,128)S(1)}, u32[]{:S(2)}, u32[]{:S(2)}) collective-permute-start(f32[64,256]{1,0:T(8,128)} %get-tuple-element.17), channel_id=1, source_target_pairs={{1,0},{2,1},{3,2},{4,3},{5,4},{6,5},{7,6},{8,7},{9,8},{10,9},{11,1... | collective-permute-start | bytes 196616 | tf_op jit(solution)/shard_map/ppermute | solution.py:483
  7.0 13.3 %collective-permute-start = (f32[64,128]{1,0:T(8,128)}, f32[64,128]{1,0:T(8,128)S(1)}, u32[]{:S(2)}, u32[]{:S(2)}) collective-permute-start(f32[64,128]{1,0:T(8,128)} %get-tuple-element.14), channel_id=1, source_target_pairs={{0,16},{16,32},{32,48},{48,64},{64,80},{80,96},{96,112},{112,0},{1... | collective-permute-start | bytes 98312 | tf_op jit(solution)/shard_map/ppermute | solution.py:480
  9.1 11.2 %collective-permute-start.1 = (f32[64,128]{1,0:T(8,128)}, f32[64,128]{1,0:T(8,128)S(1)}, u32[]{:S(2)}, u32[]{:S(2)}) collective-permute-start(f32[64,128]{1,0:T(8,128)} %get-tuple-element.15), channel_id=1, source_target_pairs={{16,0},{32,16},{48,32},{64,48},{80,64},{96,80},{112,96},{0,112},{1... | collective-permute-start | bytes 98312 | tf_op jit(solution)/shard_map/ppermute | solution.py:481
  20.3 4.6 %copy-start.3 = (f32[64,128]{1,0:T(8,128)}, f32[64,128]{1,0:T(8,128)S(1)}, u32[]{:S(2)}) copy-start(f32[64,128]{1,0:T(8,128)S(1)} %collective-permute-done.refs_4_) | copy-start | bytes 98308
  20.3 4.6 %copy-start.4 = (f32[64,128]{1,0:T(8,128)}, f32[64,128]{1,0:T(8,128)S(1)}, u32[]{:S(2)}) copy-start(f32[64,128]{1,0:T(8,128)S(1)} %collective-permute-done.1.refs_5_) | copy-start | bytes 98308
  20.3 4.6 %copy-start.1 = (f32[64,256]{1,0:T(8,128)}, f32[64,256]{1,0:T(8,128)S(1)}, u32[]{:S(2)}) copy-start(f32[64,256]{1,0:T(8,128)S(1)} %collective-permute-done.2.refs_6_) | copy-start | bytes 196612
  20.4 4.6 %copy-start.2 = (f32[64,256]{1,0:T(8,128)}, f32[64,256]{1,0:T(8,128)S(1)}, u32[]{:S(2)}) copy-start(f32[64,256]{1,0:T(8,128)S(1)} %collective-permute-done.3.refs_7_) | copy-start | bytes 196612
  20.4 55.0 %all-to-all-start.1 = ((f32[8,64,2,8,128]{4,3,2,1,0:T(8,128)}), f32[8,64,2,8,128]{4,3,2,1,0:T(8,128)}, u32[]{:S(2)}, u32[]{:S(2)}) async-start(f32[8,64,2,8,128]{4,3,2,1,0:T(8,128)} %potential.1), calls=%async_computation.1 | async-start | bytes 8388608 | tf_op jit(solution)/shard_map/all_to_all | solution.py:442
  34.3 57.8 %slice-start = ((s32[128,4]{0,1:T(4,128)}), s32[128,2]{0,1:T(2,128)S(1)}, s32[]{:S(2)}) async-start(s32[128,4]{0,1:T(4,128)} %param.10), calls=%async_computation.5 | async-start | bytes 2048 | tf_op jit(solution)/shard_map/slice | solution.py:446
  75.4 67.3 %all-to-all-start = ((f32[8,64,2,8,128]{4,3,2,1,0:T(8,128)}), f32[8,64,2,8,128]{4,3,2,1,0:T(8,128)}, u32[]{:S(2)}, u32[]{:S(2)}) async-start(f32[8,64,2,8,128]{4,3,2,1,0:T(8,128)} %advect.1), calls=%async_computation | async-start | bytes 8388608 | tf_op jit(solution)/shard_map/all_to_all | solution.py:442
  152.9 76.9 %all-to-all-start.2 = ((f32[128,2,2,2,8,128]{5,4,3,2,1,0:T(8,128)}), f32[128,2,2,2,8,128]{5,4,3,2,1,0:T(8,128)}, u32[]{:S(2)}, u32[]{:S(2)}) async-start(f32[128,2,2,2,8,128]{5,4,3,2,1,0:T(8,128)} %fourier0.1), calls=%async_computation.2 | async-start | bytes 8388608 | tf_op jit(solution)/shard_map/all_to_all | solution.py:442
  177.0 6.2 %copy-start.5 = (s32[128,4]{0,1:T(4,128)S(1)}, s32[128,4]{0,1:T(4,128)}, u32[]{:S(2)}) copy-start(s32[128,4]{0,1:T(4,128)} %param.10) | copy-start | bytes 6148
  248.5 35.9 %copy-start = (bf16[2,1024,1024]{2,1,0:T(8,128)(2,1)S(1)}, bf16[2,1024,1024]{2,1,0:T(8,128)(2,1)}, u32[]{:S(2)}) copy-start(bf16[2,1024,1024]{2,1,0:T(8,128)(2,1)} %pad_maximum_fusion.table_ref) | copy-start | bytes 12582916

commit v2 on v1

--- a/solution.py
+++ b/solution.py
@@ -90,35 +90,7 @@
     )(phase)
 
 
-def potential_kernel(c_ref, w_ref, out_ref):
-    shells, rows, cols = c_ref.shape
-    weights = w_ref[...]
-    for k in range(shells):
-        x = c_ref[k]
-        y = (x * x * x - x) * weights
-        for a in range(rows // 8):
-            for h in range(cols // 128):
-                out_ref[a, k, h] = y[8 * a : 8 * a + 8, 128 * h : 128 * h + 128]
-
-
-def potential_stage(phase, weights):
-    shells, rows, cols = phase.shape
-    kb = 8
-    return pl.pallas_call(
-        potential_kernel,
-        grid=(shells // kb,),
-        in_specs=[
-            pl.BlockSpec((kb, rows, cols), lambda i: (i, 0, 0)),
-            pl.BlockSpec((rows, cols), lambda i: (0, 0)),
-        ],
-        out_specs=pl.BlockSpec((rows // 8, kb, cols // 128, 8, 128), lambda i: (0, i, 0, 0, 0)),
-        out_shape=jax.ShapeDtypeStruct((rows // 8, shells, cols // 128, 8, 128), f32),
-        compiler_params=params(61),
-        name="potential",
-    )(phase, weights)
-
-
-def advect_kernel(scale_phi, scale_ref, c_ref, v_ref, w_ref, west_ref, east_ref, north_ref, south_ref, out_ref):
+def stencil_kernel(scale_phi, scale_ref, c_ref, v_ref, w_ref, west_ref, east_ref, north_ref, south_ref, out_ref):
     shells, rows, cols = c_ref.shape
     block = pl.program_id(0)
     weights = w_ref[...]
@@ -140,17 +112,19 @@
         scale_theta = scale_ref[block * shells + k]
         y = x - (spin * ((east - west) * scale_phi) + sweep * ((south - north) * scale_theta))
         y = y * weights
+        z = (x * x * x - x) * weights
         for a in range(rows // 8):
             for h in range(cols // 128):
-                out_ref[a, k, h] = y[8 * a : 8 * a + 8, 128 * h : 128 * h + 128]
-
-
-def advect_stage(phase, velocity, weights, west, east, north, south, scale_phi, scale_theta):
+                out_ref[a, 0, k, h] = y[8 * a : 8 * a + 8, 128 * h : 128 * h + 128]
+                out_ref[a, 1, k, h] = z[8 * a : 8 * a + 8, 128 * h : 128 * h + 128]
+
+
+def stencil_stage(phase, velocity, weights, west, east, north, south, scale_phi, scale_theta):
     shells, rows, cols = phase.shape
     kb = 8
 
     def kernel(*refs):
-        advect_kernel(scale_phi, *refs)
+        stencil_kernel(scale_phi, *refs)
 
     return pl.pallas_call(
         kernel,
@@ -165,25 +139,66 @@
             pl.BlockSpec((kb, cols), lambda i: (i, 0)),
             pl.BlockSpec((kb, cols), lambda i: (i, 0)),
         ],
-        out_specs=pl.BlockSpec((rows // 8, kb, cols // 128, 8, 128), lambda i: (0, i, 0, 0, 0)),
-        out_shape=jax.ShapeDtypeStruct((rows // 8, shells, cols // 128, 8, 128), f32),
-        compiler_params=params(61),
-        name="advect",
+        out_specs=pl.BlockSpec((rows // 8, 2, kb, cols // 128, 8, 128), lambda i: (0, 0, i, 0, 0, 0)),
+        out_shape=jax.ShapeDtypeStruct((rows // 8, 2, shells, cols // 128, 8, 128), f32),
+        compiler_params=params(54),
+        name="stencil",
     )(scale_theta, phase, velocity, weights, west, east, north, south)
 
 
-def fourier_kernel(p_ref, table_ref, *rest):
-    out_ref, xh, xl, ysc = rest[-4:]
+def table_kernel(fine_ref, coarse_ref, out_ref):
+    modes = fine_ref.shape[2]
+    tiles = out_ref.shape[2] // 128
+    fc, fs = fine_ref[0, 0], fine_ref[1, 0]
+    for u in range(tiles):
+        cc = jnp.broadcast_to(coarse_ref[0, 0, :, u : u + 1], (modes, 128))
+        cs = jnp.broadcast_to(coarse_ref[1, 0, :, u : u + 1], (modes, 128))
+        for i, value in enumerate((fc * cc - fs * cs, fs * cc + fc * cs)):
+            h, l = split(value)
+            lanes = slice(128 * u, 128 * u + 128)
+            out_ref[0, i * modes : (i + 1) * modes, lanes] = h
+            out_ref[0, (2 + i) * modes : (3 + i) * modes, lanes] = l
+
+
+def wave_tables(owned_modes, phi_count):
+    first_half = owned_modes[:, :2].T.reshape(-1)
+    top = owned_modes.shape[0] * owned_modes.shape[1] - 1
+    even = jnp.where(first_half % 2 == 0, first_half, top - first_half)
+    modes = jnp.stack([even, top - even])
+    count = modes.shape[1]
+    half_phi = phi_count // 2
+
+    def waves(step):
+        quarter = jnp.arange(2, dtype=jnp.int32) * (phi_count // 4)
+        lanes = jnp.arange(128, dtype=jnp.int32) * step
+        turns = (modes[None, :, :, None] * lanes + quarter[:, None, None, None]) % phi_count
+        return jnp.cos(turns.astype(f32) * (2.0 * math.pi / phi_count))
+
+    return pl.pallas_call(
+        table_kernel,
+        grid=(2,),
+        in_specs=[
+            pl.BlockSpec((2, 1, count, 128), lambda i: (0, i, 0, 0)),
+            pl.BlockSpec((2, 1, count, 128), lambda i: (0, i, 0, 0)),
+        ],
+        out_specs=pl.BlockSpec((1, 4 * count, half_phi), lambda i: (i, 0, 0)),
+        out_shape=jax.ShapeDtypeStruct((2, 4 * count, half_phi), bf16),
+        compiler_params=params(40),
+        name="table",
+    )(waves(1), waves(128))
+
+
+def fourier_kernel(p_ref, table_ref, out_ref, xh, xl, ysc):
     parts = p_ref.shape[0]
     half = parts // 2
     per = xh.shape[0] // 8
     tiles = xh.shape[1] // half // 128
-    sign = jnp.where(pl.program_id(0) == 0, 1.0, -1.0).astype(f32)
+    sign = jnp.where(pl.program_id(1) == 0, 1.0, -1.0).astype(f32)
     for a in range(half):
         for t in range(8):
             for j in range(tiles):
                 strided = pl.ds(8 * j + t, per, stride=8 * tiles)
-                x = p_ref[a, strided, :] + sign * p_ref[a + half, strided, :]
+                x = p_ref[a, 0, strided, :] + sign * p_ref[a + half, 0, strided, :]
                 h, l = split(x)
                 lanes = slice((a * tiles + j) * 128, (a * tiles + j + 1) * 128)
                 xh[t * per : (t + 1) * per, lanes] = h
@@ -202,37 +217,29 @@
         out_ref[:, 0, 0, s] = ysc[s * owners * 8 : (s + 1) * owners * 8, :].reshape(owners, 8, 128)
 
 
-def fourier_stage(rows_all, table, field, buffer):
-    parts, shells, tiles, tb, _ = rows_all.shape
+def fourier_stage(rows_all, table):
+    parts, fields, shells, tiles, tb, _ = rows_all.shape
     half_phi = table.shape[2]
     modes2 = table.shape[1] // 2
     owners = modes2 // 4
-    flat = rows_all.reshape(parts, shells * tiles * tb, 128)
-    in_specs = [
-        pl.BlockSpec((parts, shells * tiles * tb, 128), lambda i: (0, 0, 0)),
-        pl.BlockSpec((1, 2 * modes2, half_phi), lambda i: (i, 0, 0)),
-    ]
-    args = [flat, table]
-    aliases = {}
-    if buffer is not None:
-        in_specs.append(pl.BlockSpec(memory_space=pl.ANY))
-        args.append(buffer)
-        aliases = {2: 0}
+    flat = rows_all.reshape(parts, fields, shells * tiles * tb, 128)
     return pl.pallas_call(
         fourier_kernel,
-        grid=(2,),
-        in_specs=in_specs,
-        out_specs=pl.BlockSpec((owners, 1, 1, 2, 8, 128), lambda i: (0, field, i, 0, 0, 0)),
-        out_shape=jax.ShapeDtypeStruct((owners, 2, 2, 2, 8, 128), f32),
+        grid=(fields, 2),
+        in_specs=[
+            pl.BlockSpec((parts, 1, shells * tiles * tb, 128), lambda f, i: (0, f, 0, 0)),
+            pl.BlockSpec((1, 2 * modes2, half_phi), lambda f, i: (i, 0, 0)),
+        ],
+        out_specs=pl.BlockSpec((owners, 1, 1, 2, 8, 128), lambda f, i: (0, f, i, 0, 0, 0)),
+        out_shape=jax.ShapeDtypeStruct((owners, fields, 2, 2, 8, 128), f32),
         scratch_shapes=[
             pltpu.VMEM((shells * tb, half_phi), bf16),
             pltpu.VMEM((shells * tb, half_phi), bf16),
             pltpu.VMEM((modes2 * 4, 128), f32),
         ],
-        input_output_aliases=aliases,
-        compiler_params=params(61),
-        name="fourier" + str(field),
-    )(*args)
+        compiler_params=params(40),
+        name="fourier",
+    )(flat, table)
 
 
 def spectral_kernel(az, col, sel_ref, r_ref, legt_ref, leg_ref, rad_ref, fac_ref, out_ref, xh, xl, rhs, sol, radf):
@@ -442,21 +449,6 @@
     return lax.all_to_all(x, axes, split_axis=0, concat_axis=0, tiled=True)
 
 
-def wave_tables(owned_modes, phi_count):
-    first_half = owned_modes[:, :2].T.reshape(-1)
-    top = owned_modes.shape[0] * owned_modes.shape[1] - 1
-    even = jnp.where(first_half % 2 == 0, first_half, top - first_half)
-    modes = jnp.stack([even, top - even])
-    phi_index = jnp.arange(phi_count // 2, dtype=jnp.int32)
-    quarter = jnp.arange(2, dtype=jnp.int32) * (phi_count // 4)
-    turns = modes[:, None, :, None] * phi_index + quarter[None, :, None, None]
-    turns = turns % phi_count
-    table = jnp.cos(turns.astype(f32) * (2.0 * math.pi / phi_count))
-    table = table.reshape(2, -1, phi_count // 2)
-    rounded = lax.reduce_precision(table, 8, 7)
-    return jnp.concatenate([rounded.astype(bf16), (table - rounded).astype(bf16)], axis=1)
-
-
 def body(phase_field, velocity, owned_modes, legendre, radial_inverse):
     shells, theta_local, phi_local = phase_field.shape
     az_count = lax.axis_size("az")
@@ -481,21 +473,6 @@
     east = lax.ppermute(west_out, "az", backward_az)
     north = lax.ppermute(south_out, "col", forward_col)
     south = lax.ppermute(north_out, "col", backward_col)
-    potential = potential_stage(phase_field, weights)
-    potential, west, east, north, south = lax.optimization_barrier((potential, west, east, north, south))
-    rows_potential = exchange(potential, "az")
-
-    scale_phi = step_time * phi_count / (4.0 * math.pi)
-    scale_theta = jnp.asarray((step_time * theta_count / (2.0 * math.pi) / radius).astype(np.float32))
-    advected = advect_stage(
-        phase_field, velocity, weights, west, east, north, south, scale_phi, scale_theta
-    )
-    table = wave_tables(owned_modes, phi_count)
-    rows_advected = exchange(advected, "az")
-
-    spectra = fourier_stage(rows_potential, table, 1, None)
-    spectra = fourier_stage(rows_advected, table, 0, spectra)
-    received = exchange(spectra, everyone)
 
     here = az_here * col_count + col_here
     mine = lax.dynamic_slice(owned_modes, (here, 0), (1, owned_modes.shape[1]))[0]
@@ -513,6 +490,15 @@
     factor = jnp.asarray(np.concatenate([factor, factor], axis=1).astype(np.float32))
     legendre_t = jnp.transpose(legendre, (0, 2, 1))
     radial = jnp.transpose(radial_inverse, (1, 2, 0))
+    table = wave_tables(owned_modes, phi_count)
+
+    scale_phi = step_time * phi_count / (4.0 * math.pi)
+    scale_theta = jnp.asarray((step_time * theta_count / (2.0 * math.pi) / radius).astype(np.float32))
+    fields = stencil_stage(
+        phase_field, velocity, weights, west, east, north, south, scale_phi, scale_theta
+    )
+    fields, table, select, legendre_t = lax.optimization_barrier((fields, table, select, legendre_t))
+    received = exchange(fourier_stage(exchange(fields, "az"), table), everyone)
     synthesis = spectral_stage(
         received, legendre_t, legendre, radial, factor, select, az_count, col_count
     )

time: 349 us -> 337 us (0.966)
  blocking collectives: 87.5 us -> 253 us
  waiting for transfers between devices: 108 us -> 0.01 us
  starting transfers between devices: 53 us -> 7.34 us
  other arithmetic: 19.3 us -> 4.61 us
  Pallas kernels: 71.8 us -> 62.9 us
    all_to_all x2 -> x4, blocking collectives: 87.5 us -> 253 us  [exchange(): return lax.all_to_all(x, axes, split_axis=0, concat_axis=0, tiled=True)]
    all_to_all x3 -> x0, waiting for transfers between devices: 108 us -> none  [exchange(): return lax.all_to_all(x, axes, split_axis=0, concat_axis=0, tiled=True)]
    all_to_all x3 -> x0, starting transfers between devices: 45.3 us -> none  [exchange(): return lax.all_to_all(x, axes, split_axis=0, concat_axis=0, tiled=True)]
    convert_element_type x2 -> x0, other arithmetic: 16.1 us -> none  [the longest x1 15.4 us: wave_tables(): rounded.astype(bf16)]
    pallas_call x4 -> x3, Pallas kernels: 36.6 us -> 27.6 us  [the longest x1 14.7 us: fourier_stage(): pl.pallas_call(fourier_kernel, grid=(fields, 2), in_specs=[pl.BlockSpec((...]
    cos x0 -> x1, other arithmetic: none -> 3.83 us  [waves(): return jnp.cos(turns.astype(f32) * (2.0 * math.pi / phi_count))]
  transfers between devices with their start and end apart: 7 -> 4, of which waited for: 3 -> 0; matrix products, arithmetic and copies ran while one was open for 8% -> 3% of each run, Pallas kernels for 8% -> 1%
where the time goes in v2:
time: 337 us; the launch traced here: 336 us
  blocking collectives  253 us (75%)
  Pallas kernels  62.9 us (19%)
  local copies, waits for them, and re-layouts  8.06 us (2%)
  starting transfers between devices  7.34 us (2%)
  other arithmetic  4.61 us (1%)
    all_to_all x4, blocking collectives, exchange(): return lax.all_to_all(x, axes, split_axis=0, concat_axis=0, tiled=True)  253 us
    pallas_call x1, Pallas kernels, spectral_stage(): pl.pallas_call(kernel, grid_spec=pltpu.PrefetchScalarGridSpec(num_scalar_...  18.7 us
    pallas_call x1, Pallas kernels, fourier_stage(): pl.pallas_call(fourier_kernel, grid=(fields, 2), in_specs=[pl.BlockSpec((...  14.7 us
    pallas_call x1, Pallas kernels, stencil_stage(): pl.pallas_call(kernel, grid=(shells // kb,), in_specs=[pl.BlockSpec(memor...  11 us
    pallas_call x1, Pallas kernels, inverse_stage(): pl.pallas_call(inverse_kernel, grid=(az // 2,), in_specs=[pl.BlockSpec((o...  8.5 us
  transfers between devices with their start and end apart: 4, of which 0 were waited for; matrix products, arithmetic and copies ran while one was open for 3% of the time, Pallas kernels for 1%

profile of v2, /device:TPU:0, one launch (start us, length us, event | category | flops | bytes accessed | tf_op | source)
XLA Modules:
  0.0 336.5 jit_solution(17870853026587914189)
XLA Ops:
  0.0 0.0 slice-start
  0.0 0.0 copy-start.6
  0.0 4.4 %edges.1 = (f32[64,128]{1,0:T(8,128)}, f32[64,128]{1,0:T(8,128)}, f32[64,256]{1,0:T(8,128)}, f32[64,256]{1,0:T(8,128)}) custom-call(f32[64,64,256]{2,1,0:T(8,128)} %refs_1_.1), custom_call_target="tpu_custom_call" | custom-call | tf_op jit(solution)/shard_map/edges/pallas_call | solution.py:72
  4.4 1.7 collective-permute-start
  6.1 2.9 collective-permute-start.1
  9.0 1.4 collective-permute-start.2
  10.5 1.3 collective-permute-start.3
  11.8 0.0 slice-done
  11.8 0.0 copy-done.6
  11.8 0.1 constant_dynamic-slice_fusion
  11.9 0.1 slice_reduce_fusion
  12.1 0.1 broadcast_multiply_fusion
  12.2 3.8 %fusion.5 = (f32[2,2,256,128]{3,2,1,0:T(8,128)S(1)}, f32[2,2,256,128]{3,2,1,0:T(8,128)S(1)}) fusion(s32[2,256,128]{2,1,0:T(8,128)S(1)} %get-tuple-element.25, s32[2]{0:T(128)S(1)} %iota_multiply_fusion.2, s32[2,256,128]{2,1,0:T(8,128)S(1)} %get-tuple-element.26), kind=kLoop, calls=%fused_computation.15 | loop fusion | flops 3670016 | bytes 1572872 | tf_op jit(solution)/shard_map/cos | solution.py:175
  16.0 0.6 pad_add_fusion.1.refs_0_
  16.6 6.2 %copy.9 = bf16[4,1024,512]{1,2,0:T(8,128)(2,1)} copy(bf16[4,1024,512]{2,1,0:T(8,128)(2,1)} %refs_3_.1) | data formatting | bytes 8388608 | tf_op args[3]
  22.8 0.8 dynamic_slice.6
  23.6 1.8 table.1.table_ref
  25.4 0.0 copy-start
  25.4 0.0 collective-permute-done.refs_4_
  25.5 0.0 copy-start.4
  25.5 0.0 collective-permute-done.1.refs_5_
  25.5 0.0 copy-start.5
  25.5 0.0 collective-permute-done.2.refs_6_
  25.5 0.0 copy-start.2
  25.5 0.0 collective-permute-done.3.refs_7_
  25.5 0.0 copy-start.3
  25.5 0.9 broadcast_in_dim.4.refs_3_
  26.4 0.0 copy-done.4
  26.4 0.0 copy-done.5
  26.4 0.0 copy-done.2
  26.4 0.0 copy-done.3
  26.4 11.0 %stencil.1 = f32[8,2,64,2,8,128]{5,4,3,2,1,0:T(8,128)} custom-call(f32[64]{0:T(128)} %constant.81.clone.refs_0_, f32[64,64,256]{2,1,0:T(8,128)} %refs_1_.1, bf16[2,64,64,256]{3,2,1,0:T(8,128)(2,1)} %refs_2_.1, f32[64,256]{1,0:T(8,128)} %broadcast_in_dim.4.refs_3_, f32[64,128]{1,0:T(8,128)} %copy-done.4, f32[64,128]{1,0:T(8,128)} %copy-done.5, ...), custom_call_target="tpu_custom_call" | custom-call | tf_op jit(solution)/shard_map/stencil/pallas_call | solution.py:129
  37.5 99.8 %all_to_all.20 = f32[8,2,64,2,8,128]{5,4,3,2,1,0:T(8,128)} all-to-all(f32[8,2,64,2,8,128]{5,4,3,2,1,0:T(8,128)} %stencil.1), channel_id=1, replica_groups=mesh['az'=8,'col'=16] {'az'}, dimensions={0} | all-to-all | bytes 16777216 | tf_op jit(solution)/shard_map/all_to_all | solution.py:449
  137.3 0.0 copy-done
  137.3 14.7 %fourier.1 = f32[128,2,2,2,8,128]{5,4,3,2,1,0:T(8,128)S(1)} custom-call(f32[8,2,1024,128]{3,2,1,0:T(8,128)} %bitcast.10, bf16[2,1024,1024]{2,1,0:T(8,128)(2,1)S(1)} %table.1.table_ref), custom_call_target="tpu_custom_call" | custom-call | tf_op jit(solution)/shard_map/fourier/pallas_call | solution.py:226
  152.1 66.0 %all_to_all.21.refs_1_ = f32[128,2,2,2,8,128]{5,4,3,2,1,0:T(8,128)} all-to-all(f32[128,2,2,2,8,128]{5,4,3,2,1,0:T(8,128)S(1)} %fourier.1), channel_id=1, replica_groups=mesh['az'=8,'col'=16] {'az','col'}, dimensions={0} | all-to-all | bytes 8388608 | tf_op jit(solution)/shard_map/all_to_all | solution.py:449
  218.0 18.7 %spectral.1 = f32[128,4,8,128]{3,2,1,0:T(8,128)} custom-call(s32[8]{0:T(128)} %pad_add_fusion.1.refs_0_, f32[128,2,2,2,8,128]{5,4,3,2,1,0:T(8,128)} %all_to_all.21.refs_1_, bf16[4,512,1024]{2,1,0:T(8,128)(2,1)} %bitcast.11, bf16[4,1024,512]{2,1,0:T(8,128)(2,1)} %refs_3_.1, bf16[64,64,512]{2,1,0:T(8,128)(2,1)} %bitcast.12, f32[512,128]{1,0:T(8,128)} %constant.80.clone.refs_5_), custom_call_target="tpu_custom_call" | custom-call | tf_op jit(solution)/shard_map/spectral/pallas_call | solution.py:328
  236.7 0.0 copy-start.1
  236.7 35.9 %all_to_all.22 = f32[128,4,8,128]{3,2,1,0:T(8,128)S(1)} all-to-all(f32[128,4,8,128]{3,2,1,0:T(8,128)} %spectral.1), channel_id=1, replica_groups=mesh['az'=8,'col'=16] {'az','col'}, dimensions={0} | all-to-all | bytes 4194304 | tf_op jit(solution)/shard_map/all_to_all | solution.py:449
  272.7 0.0 copy-done.1
  272.7 8.5 %inverse.1 = f32[2,4,1024,128]{3,2,1,0:T(8,128)S(1)} custom-call(f32[4096,128]{1,0:T(8,128)S(1)} %bitcast.9, bf16[2,1024,1024]{2,1,0:T(8,128)(2,1)S(1)} %copy-done.1), custom_call_target="tpu_custom_call" | custom-call | tf_op jit(solution)/shard_map/inverse/pallas_call | solution.py:406
  281.2 51.6 %all_to_all.23.w_ref = f32[8,64,2,8,128]{4,3,2,1,0:T(8,128)S(1)} all-to-all(f32[8,64,2,8,128]{4,3,2,1,0:T(8,128)S(1)} %bitcast.8), channel_id=1, replica_groups=mesh['az'=8,'col'=16] {'az'}, dimensions={0} | all-to-all | bytes 8388608 | tf_op jit(solution)/shard_map/all_to_all | solution.py:449
  332.8 3.7 %gather.1 = f32[64,64,256]{2,1,0:T(8,128)} custom-call(f32[8,64,2,8,128]{4,3,2,1,0:T(8,128)S(1)} %all_to_all.23.w_ref), custom_call_target="tpu_custom_call" | custom-call | tf_op jit(solution)/shard_map/gather/pallas_call | solution.py:437
  (7 shorter events, 0.1 us)
Async XLA Ops:
  0.0 11.8 %slice-start = ((s32[128,4]{0,1:T(4,128)}), s32[128,2]{0,1:T(2,128)S(1)}, s32[]{:S(2)}) async-start(s32[128,4]{0,1:T(4,128)} %param.10), calls=%async_computation.4 | async-start | bytes 2048 | tf_op jit(solution)/shard_map/slice | solution.py:164
  0.0 11.8 %copy-start.6 = (s32[128,4]{0,1:T(4,128)S(1)}, s32[128,4]{0,1:T(4,128)}, u32[]{:S(2)}) copy-start(s32[128,4]{0,1:T(4,128)} %param.10) | copy-start | bytes 6148
  4.4 21.1 %collective-permute-start = (f32[64,128]{1,0:T(8,128)}, f32[64,128]{1,0:T(8,128)S(1)}, u32[]{:S(2)}, u32[]{:S(2)}) collective-permute-start(f32[64,128]{1,0:T(8,128)} %get-tuple-element.13), channel_id=1, source_target_pairs={{0,16},{16,32},{32,48},{48,64},{64,80},{80,96},{96,112},{112,0},{1... | collective-permute-start | bytes 98312 | tf_op jit(solution)/shard_map/ppermute | solution.py:472
  6.1 19.4 %collective-permute-start.1 = (f32[64,128]{1,0:T(8,128)}, f32[64,128]{1,0:T(8,128)S(1)}, u32[]{:S(2)}, u32[]{:S(2)}) collective-permute-start(f32[64,128]{1,0:T(8,128)} %get-tuple-element.14), channel_id=1, source_target_pairs={{16,0},{32,16},{48,32},{64,48},{80,64},{96,80},{112,96},{0,112},{1... | collective-permute-start | bytes 98312 | tf_op jit(solution)/shard_map/ppermute | solution.py:473
  9.0 16.5 %collective-permute-start.2 = (f32[64,256]{1,0:T(8,128)}, f32[64,256]{1,0:T(8,128)S(1)}, u32[]{:S(2)}, u32[]{:S(2)}) collective-permute-start(f32[64,256]{1,0:T(8,128)} %get-tuple-element.15), channel_id=1, source_target_pairs={{0,1},{1,2},{2,3},{3,4},{4,5},{5,6},{6,7},{7,8},{8,9},{9,10},{10,1... | collective-permute-start | bytes 196616 | tf_op jit(solution)/shard_map/ppermute | solution.py:474
  10.5 15.1 %collective-permute-start.3 = (f32[64,256]{1,0:T(8,128)}, f32[64,256]{1,0:T(8,128)S(1)}, u32[]{:S(2)}, u32[]{:S(2)}) collective-permute-start(f32[64,256]{1,0:T(8,128)} %get-tuple-element.16), channel_id=1, source_target_pairs={{1,0},{2,1},{3,2},{4,3},{5,4},{6,5},{7,6},{8,7},{9,8},{10,9},{11,1... | collective-permute-start | bytes 196616 | tf_op jit(solution)/shard_map/ppermute | solution.py:475
  25.4 111.9 %copy-start = (bf16[2,1024,1024]{2,1,0:T(8,128)(2,1)}, bf16[2,1024,1024]{2,1,0:T(8,128)(2,1)S(1)}, u32[]{:S(2)}) copy-start(bf16[2,1024,1024]{2,1,0:T(8,128)(2,1)S(1)} %table.1.table_ref) | copy-start | bytes 12582916
  25.5 1.0 copy-start.4
  25.5 0.9 copy-start.5
  25.5 0.9 copy-start.2
  25.5 0.9 copy-start.3
  236.7 35.9 %copy-start.1 = (bf16[2,1024,1024]{2,1,0:T(8,128)(2,1)S(1)}, bf16[2,1024,1024]{2,1,0:T(8,128)(2,1)}, u32[]{:S(2)}) copy-start(bf16[2,1024,1024]{2,1,0:T(8,128)(2,1)} %copy-done) | copy-start | bytes 12582916

commit v3 on v2

v3 whole, which is shorter than its diff:
```python
import math

import jax
import jax.numpy as jnp
import numpy as np
from jax import lax
from jax.experimental import pallas as pl
from jax.experimental.pallas import tpu as pltpu
from jax.sharding import PartitionSpec as P

step_time = 0.002
mobility_step = 4e-06
f32 = jnp.float32
bf16 = jnp.bfloat16
everyone = ("az", "col")


def params(mib=48):
    return pltpu.CompilerParams(vmem_limit_bytes=mib * 1024 * 1024)


def colat_weights(count):
    theta = math.pi * (np.arange(count) + 0.5) / count
    waves = np.arange(1, count // 2 + 1)
    total = (np.cos(2.0 * waves[None, :] * theta[:, None]) / (4.0 * waves * waves - 1.0)).sum(1)
    return 2.0 / count * (1.0 - 2.0 * total)


def shell_radii(shells):
    return 0.75 + 0.25 * (np.arange(shells) + 0.5) / shells


def split(x):
    hi = x.astype(bf16)
    return hi, (x - hi.astype(f32)).astype(bf16)


def dot_nn(a, b):
    return lax.dot_general(a, b, (((1,), (0,)), ((), ())), preferred_element_type=f32)


def dot_nt(a, b):
    return lax.dot_general(a, b, (((1,), (1,)), ((), ())), preferred_element_type=f32)


def swap_halves(a, b):
    half = lax.broadcasted_iota(jnp.int32, a.shape, 1) < 64
    first = jnp.where(half, a, pltpu.roll(b, 64, 1))
    second = jnp.where(half, pltpu.roll(a, 64, 1), b)
    return first, second


def edges_kernel(c_ref, west_ref, east_ref, north_ref, south_ref):
    shells, rows, cols = c_ref.shape
    block = pl.program_id(0)
    lane = lax.broadcasted_iota(jnp.int32, (rows, 128), 1)
    west = jnp.where(block == 0, 0.0, west_ref[...])
    east = jnp.where(block == 0, 0.0, east_ref[...])
    for k in range(shells):
        at = block * shells + k
        west = jnp.where(lane == at, pltpu.roll(c_ref[k, :, :128], at, 1), west)
        east = jnp.where(lane == at, pltpu.roll(c_ref[k, :, cols - 128 :], at + 1, 1), east)
    west_ref[...] = west
    east_ref[...] = east
    north_ref[...] = c_ref[:, 0, :]
    south_ref[...] = c_ref[:, rows - 1, :]


def edges_stage(phase):
    shells, rows, cols = phase.shape
    kb = 16
    return pl.pallas_call(
        edges_kernel,
        grid=(shells // kb,),
        in_specs=[pl.BlockSpec((kb, rows, cols), lambda i: (i, 0, 0))],
        out_specs=[
            pl.BlockSpec((rows, 128), lambda i: (0, 0)),
            pl.BlockSpec((rows, 128), lambda i: (0, 0)),
            pl.BlockSpec((kb, cols), lambda i: (i, 0)),
            pl.BlockSpec((kb, cols), lambda i: (i, 0)),
        ],
        out_shape=[
            jax.ShapeDtypeStruct((rows, 128), f32),
            jax.ShapeDtypeStruct((rows, 128), f32),
            jax.ShapeDtypeStruct((shells, cols), f32),
            jax.ShapeDtypeStruct((shells, cols), f32),
        ],
        compiler_params=params(61),
        name="edges",
    )(phase)


def stencil_kernel(scale_phi, where_ref, scale_ref, c_ref, v_ref, w_ref, west_ref, east_ref, north_ref, south_ref, out_ref):
    shells, rows, cols = c_ref.shape
    block = pl.program_id(0)
    weights = jnp.concatenate([w_ref[...]] * (cols // 128), axis=1)
    lane = lax.broadcasted_iota(jnp.int32, (rows, cols), 1)
    row = lax.broadcasted_iota(jnp.int32, (rows, cols), 0)
    turn = jnp.where(block == 0, 0, 128 - block * shells)
    west_all = pltpu.roll(west_ref[...], turn, 1)
    east_all = pltpu.roll(east_ref[...], turn, 1)
    for k in range(shells):
        x = c_ref[k]
        west_edge = jnp.broadcast_to(west_all[:, k : k + 1], (rows, cols))
        east_edge = jnp.broadcast_to(east_all[:, k : k + 1], (rows, cols))
        west = jnp.where(lane == 0, west_edge, pltpu.roll(x, 1, 1))
        east = jnp.where(lane == cols - 1, east_edge, pltpu.roll(x, cols - 1, 1))
        north = jnp.where(row == 0, north_ref[k : k + 1, :], pltpu.roll(x, 1, 0))
        south = jnp.where(row == rows - 1, south_ref[k : k + 1, :], pltpu.roll(x, rows - 1, 0))
        spin = v_ref[0, k].astype(f32)
        sweep = v_ref[1, k].astype(f32)
        scale_theta = scale_ref[block * shells + k]
        y = x - (spin * ((east - west) * scale_phi) + sweep * ((south - north) * scale_theta))
        y = y * weights
        z = (x * x * x - x) * weights
        for a in range(rows // 8):
            for h in range(cols // 128):
                out_ref[a, 0, k, h] = y[8 * a : 8 * a + 8, 128 * h : 128 * h + 128]
                out_ref[a, 1, k, h] = z[8 * a : 8 * a + 8, 128 * h : 128 * h + 128]


def stencil_stage(phase, velocity, weights, where, west, east, north, south, scale_phi, scale_theta):
    shells, rows, cols = phase.shape
    kb = 16

    def kernel(*refs):
        stencil_kernel(scale_phi, *refs)

    return pl.pallas_call(
        kernel,
        grid_spec=pltpu.PrefetchScalarGridSpec(
            num_scalar_prefetch=1,
            grid=(shells // kb,),
            in_specs=[
                pl.BlockSpec(memory_space=pltpu.SMEM),
                pl.BlockSpec((kb, rows, cols), lambda i, s: (i, 0, 0)),
                pl.BlockSpec((2, kb, rows, cols), lambda i, s: (0, i, 0, 0)),
                pl.BlockSpec((rows, 128), lambda i, s: (s[0], 0)),
                pl.BlockSpec((rows, 128), lambda i, s: (0, 0)),
                pl.BlockSpec((rows, 128), lambda i, s: (0, 0)),
                pl.BlockSpec((kb, cols), lambda i, s: (i, 0)),
                pl.BlockSpec((kb, cols), lambda i, s: (i, 0)),
            ],
            out_specs=pl.BlockSpec((rows // 8, 2, kb, cols // 128, 8, 128), lambda i, s: (0, 0, i, 0, 0, 0)),
        ),
        out_shape=jax.ShapeDtypeStruct((rows // 8, 2, shells, cols // 128, 8, 128), f32),
        compiler_params=params(48),
        name="stencil",
    )(where, scale_theta, phase, velocity, weights, west, east, north, south)


def table_kernel(fine_ref, coarse_ref, out_ref):
    modes = fine_ref.shape[2]
    tiles = out_ref.shape[2] // 128
    fc, fs = fine_ref[0, 0], fine_ref[1, 0]
    coarse = [coarse_ref[i, 0].T for i in range(2)]
    for u in range(tiles):
        cc = jnp.broadcast_to(coarse[0][:, u : u + 1], (modes, 128))
        cs = jnp.broadcast_to(coarse[1][:, u : u + 1], (modes, 128))
        for i, value in enumerate((fc * cc - fs * cs, fs * cc + fc * cs)):
            h, l = split(value)
            lanes = slice(128 * u, 128 * u + 128)
            out_ref[0, i * modes : (i + 1) * modes, lanes] = h
            out_ref[0, (2 + i) * modes : (3 + i) * modes, lanes] = l


def wave_tables(owned_modes, phi_count):
    first_half = owned_modes[:, :2].T.reshape(-1)
    top = owned_modes.shape[0] * owned_modes.shape[1] - 1
    even = jnp.where(first_half % 2 == 0, first_half, top - first_half)
    modes = jnp.stack([even, top - even])
    count = modes.shape[1]
    half_phi = phi_count // 2

    quarter = jnp.arange(2, dtype=jnp.int32) * (phi_count // 4)

    def waves(turns):
        turns = (turns + quarter[:, None, None, None]) % phi_count
        return jnp.cos(turns.astype(f32) * (2.0 * math.pi / phi_count))

    lanes = jnp.arange(128, dtype=jnp.int32)
    tiles = jnp.arange(half_phi // 128, dtype=jnp.int32) * 128
    fine = waves(modes[None, :, :, None] * lanes)
    coarse = waves(modes[None, :, None, :] * tiles[:, None])

    return pl.pallas_call(
        table_kernel,
        grid=(2,),
        in_specs=[
            pl.BlockSpec((2, 1, count, 128), lambda i: (0, i, 0, 0)),
            pl.BlockSpec((2, 1, half_phi // 128, count), lambda i: (0, i, 0, 0)),
        ],
        out_specs=pl.BlockSpec((1, 4 * count, half_phi), lambda i: (i, 0, 0)),
        out_shape=jax.ShapeDtypeStruct((2, 4 * count, half_phi), bf16),
        compiler_params=params(40),
        name="table",
    )(fine, coarse)


def fourier_kernel(p_ref, table_ref, out_ref, xh, xl, ysc):
    parts, fields = p_ref.shape[:2]
    half = parts // 2
    per = xh.shape[0] // 8
    tiles = xh.shape[1] // half // 128
    both = table_ref.shape[1] // 2
    count = both // 2
    owners = count // 2

    def one(index, carry):
        f, parity = index // 2, index % 2
        sign = jnp.where(parity == 0, 1.0, -1.0).astype(f32)
        for a in range(half):
            for t in range(8):
                for j in range(tiles):
                    strided = pl.ds(8 * j + t, per, stride=8 * tiles)
                    x = p_ref[a, f, strided, :] + sign * p_ref[a + half, f, strided, :]
                    h, l = split(x)
                    lanes = slice((a * tiles + j) * 128, (a * tiles + j + 1) * 128)
                    xh[t * per : (t + 1) * per, lanes] = h
                    xl[t * per : (t + 1) * per, lanes] = l
        y = dot_nt(table_ref[parity], xh[...])
        y = y[:both] + (y[both:] + dot_nt(table_ref[parity, :both], xl[...]))
        for u in range(4):
            first, second = swap_halves(y[:count, 128 * u : 128 * u + 128], y[count:, 128 * u : 128 * u + 128])
            ysc[pl.ds(2 * u, count, stride=8), :] = first
            ysc[pl.ds(2 * u + 1, count, stride=8), :] = second
        for s in range(2):
            out_ref[:, f, parity, s] = ysc[s * owners * 8 : (s + 1) * owners * 8, :].reshape(owners, 8, 128)
        return carry

    lax.fori_loop(0, 2 * fields, one, 0)


def fourier_stage(rows_all, table):
    parts, fields, shells, tiles, tb, _ = rows_all.shape
    half_phi = table.shape[2]
    modes2 = table.shape[1] // 2
    owners = modes2 // 4
    flat = rows_all.reshape(parts, fields, shells * tiles * tb, 128)
    whole = pl.BlockSpec(memory_space=pltpu.VMEM)
    return pl.pallas_call(
        fourier_kernel,
        in_specs=[whole, whole],
        out_specs=whole,
        out_shape=jax.ShapeDtypeStruct((owners, fields, 2, 2, 8, 128), f32),
        scratch_shapes=[
            pltpu.VMEM((shells * tb, half_phi), bf16),
            pltpu.VMEM((shells * tb, half_phi), bf16),
            pltpu.VMEM((modes2 * 4, 128), f32),
        ],
        compiler_params=params(32),
        name="fourier",
    )(flat, table)


def spectral_kernel(az, col, mode_ref, r_ref, leg, rad, fac_ref, out_ref, xh, xl, rhs, sol, radf):
    degrees = leg.shape[2]
    shells = rad.shape[0]
    tb = az * 8
    tiles = degrees // 128
    for q in range(4):
        parity = mode_ref[q] % 2
        for f in range(2):
            x = jnp.concatenate(
                [r_ref[a * col + c, f, parity, q % 2] for c in range(col) for a in range(az)], axis=0
            )
            h, l = split(x.T)
            xh[f * 128 : (f + 1) * 128, :] = h
            xl[f * 128 : (f + 1) * 128, :] = l
        coef = dot_nn(xh[...], leg[q]) + dot_nn(xl[...], leg[q])
        right = coef[:128] - fac_ref[...] * coef[128:]
        for i in range(2):
            for lt in range(tiles):
                rhs[lt, pl.ds(2 * q + i, shells, stride=8), :] = right[
                    i * shells : (i + 1) * shells, lt * 128 : lt * 128 + 128
                ]

    rb = 8

    def outer(block, carry):
        radf[...] = rad[pl.ds(block * rb, rb)].astype(f32)
        for lt in range(tiles):
            lanes = slice(lt * 128, lt * 128 + 128)
            acc = [jnp.zeros((8, 128), f32) for _ in range(rb)]
            for s in range(shells):
                v = rhs[lt, 8 * s : 8 * s + 8, :]
                for r in range(rb):
                    acc[r] = acc[r] + radf[r, s : s + 1, lanes] * v
            for r in range(rb):
                sol[lt, pl.ds(pl.multiple_of((block * rb + r) * 8, 8), 8), :] = acc[r]
        return carry

    lax.fori_loop(0, shells // rb, outer, 0)

    for q in range(4):
        parity = mode_ref[q] % 2
        gain = jnp.where(mode_ref[q] == 0, 1.0, 2.0).astype(f32)
        x = jnp.concatenate(
            [
                jnp.concatenate([sol[lt, pl.ds(2 * q + i, shells, stride=8), :] for lt in range(tiles)], axis=1)
                for i in range(2)
            ],
            axis=0,
        )
        h, l = split(x * gain)
        y = dot_nt(leg[q], h) + dot_nt(leg[q], l)
        for c in range(col):
            for a in range(az):
                out_ref[a * col + c, 2 * parity + q % 2] = y[c * tb + a * 8 : c * tb + a * 8 + 8]


def spectral_stage(received, legendre, radial, factor, own, az, col):
    owners = received.shape[0]
    modes, theta, degrees = legendre.shape
    shells = radial.shape[0]

    def kernel(*refs):
        spectral_kernel(az, col, *refs)

    whole = pl.BlockSpec(memory_space=pltpu.VMEM)
    return pl.pallas_call(
        kernel,
        in_specs=[pl.BlockSpec(memory_space=pltpu.SMEM), whole, whole, whole, whole],
        out_specs=whole,
        scratch_shapes=[
            pltpu.VMEM((256, theta), bf16),
            pltpu.VMEM((256, theta), bf16),
            pltpu.VMEM((degrees // 128, 8 * shells, 128), f32),
            pltpu.VMEM((degrees // 128, 8 * shells, 128), f32),
            pltpu.VMEM((8, shells, degrees), f32),
        ],
        out_shape=jax.ShapeDtypeStruct((owners, 4, 8, 128), f32),
        compiler_params=params(32),
        name="spectral",
    )(own, received, legendre, radial, factor)


def inverse_kernel(z_ref, table_ref, out_ref, gh, gl):
    owners = z_ref.shape[0] // 32
    rows = gh.shape[1]
    per = rows // 8
    both = table_ref.shape[1] // 2
    quarters = out_ref.shape[1]
    cols = table_ref.shape[2] // quarters
    tiles = cols // 128
    for par in range(2):
        halves = [[], []]
        for s in range(2):
            base = (par * 2 + s) * 8
            cos_u, sin_u = [], []
            for u in range(4):
                a = z_ref[pl.ds(base + 2 * u, owners, stride=32), :]
                b = z_ref[pl.ds(base + 2 * u + 1, owners, stride=32), :]
                first, second = swap_halves(a, b)
                cos_u.append(first)
                sin_u.append(second)
            halves[0].append(jnp.concatenate(cos_u, axis=1))
            halves[1].append(jnp.concatenate(sin_u, axis=1))
        for i in range(2):
            for s in range(2):
                h, l = split(halves[i][s].T)
                at = (2 * i + s) * owners
                gh[par, :, at : at + owners] = h
                gl[par, :, at : at + owners] = l

    for quarter in range(quarters):
        lanes = slice(quarter * cols, (quarter + 1) * cols)
        sums = []
        for par in range(2):
            th, tl = table_ref[par, :both, lanes], table_ref[par, both:, lanes]
            h, l = gh[par], gl[par]
            sums.append(dot_nn(h, th) + (dot_nn(h, tl) + dot_nn(l, th)))
        near = sums[0] + sums[1]
        far = sums[0] - sums[1]
        for t in range(8):
            for j in range(tiles):
                part = slice(j * 128, j * 128 + 128)
                strided = pl.ds(8 * j + t, per, stride=8 * tiles)
                out_ref[0, quarter, strided, :] = near[t * per : (t + 1) * per, part]
                out_ref[1, quarter, strided, :] = far[t * per : (t + 1) * per, part]


def inverse_stage(received, table, shells, az):
    owners, _, tb, _ = received.shape
    half_phi = table.shape[2]
    modes2 = table.shape[1] // 2
    flat = received.reshape(owners * 4 * tb, 128)
    cols = 2 * half_phi // az
    rows = shells * tb
    whole = pl.BlockSpec(memory_space=pltpu.VMEM)
    out = pl.pallas_call(
        inverse_kernel,
        in_specs=[whole, whole],
        out_specs=whole,
        out_shape=jax.ShapeDtypeStruct((2, az // 2, rows * cols // 128, 128), f32),
        scratch_shapes=[
            pltpu.VMEM((2, rows, modes2), bf16),
            pltpu.VMEM((2, rows, modes2), bf16),
        ],
        compiler_params=params(32),
        name="inverse",
    )(flat, table)
    return out.reshape(az, shells, cols // 128, tb, 128)


def gather_kernel(w_ref, out_ref):
    parts, shells = w_ref.shape[:2]
    for k in range(shells):
        for a in range(parts):
            for h in range(w_ref.shape[2]):
                out_ref[k, 8 * a : 8 * a + 8, 128 * h : 128 * h + 128] = w_ref[a, k, h]


def gather_stage(blocks):
    parts, shells, tiles, tb, _ = blocks.shape
    cols = tiles * 128
    kb = 16
    return pl.pallas_call(
        gather_kernel,
        grid=(shells // kb,),
        in_specs=[pl.BlockSpec((parts, kb, tiles, tb, 128), lambda i: (0, i, 0, 0, 0))],
        out_specs=pl.BlockSpec((kb, parts * tb, cols), lambda i: (i, 0, 0)),
        out_shape=jax.ShapeDtypeStruct((shells, parts * tb, cols), f32),
        compiler_params=params(16),
        name="gather",
    )(blocks)


def exchange(x, axes):
    return lax.all_to_all(x, axes, split_axis=0, concat_axis=0, tiled=True)


def body(phase_field, velocity, owned_modes, legendre, radial_inverse):
    shells, theta_local, phi_local = phase_field.shape
    az_count = lax.axis_size("az")
    col_count = lax.axis_size("col")
    az_here = lax.axis_index("az")
    col_here = lax.axis_index("col")
    phi_count = phi_local * az_count
    theta_count = theta_local * col_count
    degree_count = legendre.shape[2]
    radius = shell_radii(shells)

    weights = (colat_weights(theta_count) / phi_count).astype(np.float32)
    weights = jnp.asarray(np.repeat(weights[:, None], 128, axis=1))
    where = jnp.reshape(col_here, (1,)).astype(jnp.int32)

    west_out, east_out, north_out, south_out = edges_stage(phase_field)
    forward_az = [(i, (i + 1) % az_count) for i in range(az_count)]
    backward_az = [(target, source) for source, target in forward_az]
    forward_col = [(i, i + 1) for i in range(col_count - 1)]
    backward_col = [(target, source) for source, target in forward_col]
    west = lax.ppermute(east_out, "az", forward_az)
    east = lax.ppermute(west_out, "az", backward_az)
    north = lax.ppermute(south_out, "col", forward_col)
    south = lax.ppermute(north_out, "col", backward_col)

    here = az_here * col_count + col_here
    own = lax.dynamic_slice(owned_modes, (here, 0), (1, owned_modes.shape[1])).reshape(-1)
    degrees = np.arange(degree_count)
    factor = mobility_step * (degrees * (degrees + 1.0))[None, :] / (radius * radius)[:, None]
    factor = jnp.asarray(np.concatenate([factor, factor], axis=0).astype(np.float32))
    radial = jnp.transpose(radial_inverse, (1, 2, 0))
    table = wave_tables(owned_modes, phi_count)

    scale_phi = step_time * phi_count / (4.0 * math.pi)
    scale_theta = jnp.asarray((step_time * theta_count / (2.0 * math.pi) / radius).astype(np.float32))
    fields = stencil_stage(
        phase_field, velocity, weights, where, west, east, north, south, scale_phi, scale_theta
    )
    fields, table, own = lax.optimization_barrier((fields, table, own))
    received = exchange(fourier_stage(exchange(fields, "az"), table), everyone)
    synthesis = spectral_stage(
        received, legendre, radial, factor, own, az_count, col_count
    )
    grid_modes = exchange(synthesis, everyone)

    blocks = inverse_stage(grid_modes, table, shells, az_count)
    return gather_stage(exchange(blocks, "az"))


def solution(mesh):
    in_specs = (
        P(None, "col", "az"),
        P(None, None, "col", "az"),
        P(),
        P(("az", "col"), None, None),
        P(),
    )
    out_specs = P(None, "col", "az")
    return jax.shard_map(body, mesh=mesh, in_specs=in_specs, out_specs=out_specs, check_vma=False)
```

time: 337 us -> 309 us (0.917)
  Pallas kernels: 62.9 us -> 47.6 us
  local copies, waits for them, and re-layouts: 8.06 us -> 0.22 us
    pallas_call x4, Pallas kernels: 53 us -> 38.4 us  [the longest x1 13.7 us: fourier_stage(): pl.pallas_call(fourier_kernel, in_specs=[whole, whole], out_specs=whole,...]
    unnamed x15 -> x14, local copies, waits for them, and re-layouts: 6.22 us -> 0.03 us
  transfers between devices with their start and end apart: 4 -> 4, of which waited for: 0 -> 0; matrix products, arithmetic and copies ran while one was open for 3% -> 1% of each run, Pallas kernels for 1% -> 1%
where the time goes in v3:
time: 309 us
  blocking collectives  251 us (81%)
  Pallas kernels  47.6 us (15%)
  starting transfers between devices  7.34 us (2%)
    all_to_all x4, blocking collectives, exchange(): return lax.all_to_all(x, axes, split_axis=0, concat_axis=0, tiled=True)  251 us
    pallas_call x1, Pallas kernels, fourier_stage(): pl.pallas_call(fourier_kernel, in_specs=[whole, whole], out_specs=whole,...  13.7 us
    pallas_call x1, Pallas kernels, spectral_stage(): pl.pallas_call(kernel, in_specs=[pl.BlockSpec(memory_space=pltpu.SMEM), w...  10.4 us
    pallas_call x1, Pallas kernels, stencil_stage(): pl.pallas_call(kernel, grid_spec=pltpu.PrefetchScalarGridSpec(num_scalar_...  7.95 us
    pallas_call x1, Pallas kernels, inverse_stage(): pl.pallas_call(inverse_kernel, in_specs=[whole, whole], out_specs=whole,...  6.33 us
  transfers between devices with their start and end apart: 4, of which 0 were waited for; matrix products, arithmetic and copies ran while one was open for 1% of the time, Pallas kernels for 1%

profile of v3, /device:TPU:0, one launch (start us, length us, event | category | flops | bytes accessed | tf_op | source)
XLA Modules:
  0.0 308.9 jit_solution(16915923868255415141)
XLA Ops:
  0.0 0.0 copy-start.3
  0.0 0.0 copy-start.5
  0.0 0.0 slice-start
  0.0 0.0 copy-start.6
  0.0 4.4 %edges.1 = (f32[64,128]{1,0:T(8,128)}, f32[64,128]{1,0:T(8,128)}, f32[64,256]{1,0:T(8,128)}, f32[64,256]{1,0:T(8,128)}) custom-call(f32[64,64,256]{2,1,0:T(8,128)} %refs_2_.2), custom_call_target="tpu_custom_call" | custom-call | tf_op jit(solution)/shard_map/edges/pallas_call | solution.py:72
  4.4 1.7 collective-permute-start
  6.2 2.9 collective-permute-start.1
  9.0 1.4 collective-permute-start.2
  10.5 1.3 collective-permute-start.3
  11.8 0.0 slice-done
  11.9 0.1 iota_multiply_fusion
  12.0 0.1 broadcast_multiply_fusion
  12.1 2.0 fusion.2.fine_ref
  14.0 0.2 fusion.6.coarse_ref
  14.3 0.0 copy-done.6
  14.3 0.0 copy-start
  14.3 0.2 dynamic-slice_reduce_fusion.refs_0_
  14.5 2.1 table.1.table_ref
  16.6 0.0 collective-permute-done.refs_5_
  16.6 0.0 collective-permute-done.1.refs_6_
  16.6 0.0 collective-permute-done.2.refs_7_
  16.6 0.0 collective-permute-done.3.refs_8_
  16.6 0.0 copy-done.3
  16.6 0.0 copy-done.5
  16.6 0.0 copy-done
  16.6 7.9 %stencil.1 = f32[8,2,64,2,8,128]{5,4,3,2,1,0:T(8,128)} custom-call(s32[1]{0:T(128)} %bitcast.refs_0_, f32[64]{0:T(128)S(1)} %copy-done.5, f32[64,64,256]{2,1,0:T(8,128)S(1)} %copy-done, bf16[2,64,64,256]{3,2,1,0:T(8,128)(2,1)} %refs_3_.1, f32[1024,128]{1,0:T(8,128)S(1)} %copy-done.3, f32[64,128]{1,0:T(8,128)S(1)} %collective-permute-done.refs_5_, ...), custom_call_target="tpu_custom_call" | custom-call | tf_op jit(solution)/shard_map/stencil/pallas_call | solution.py:129
  24.6 97.9 %all_to_all.20 = f32[8,2,64,2,8,128]{5,4,3,2,1,0:T(8,128)S(1)} all-to-all(f32[8,2,64,2,8,128]{5,4,3,2,1,0:T(8,128)} %stencil.1), channel_id=1, replica_groups=mesh['az'=8,'col'=16] {'az'}, dimensions={0} | all-to-all | bytes 16777216 | tf_op jit(solution)/shard_map/all_to_all | solution.py:430
  122.5 0.0 copy-start.4
  122.5 13.7 %fourier.1 = f32[128,2,2,2,8,128]{5,4,3,2,1,0:T(8,128)S(1)} custom-call(f32[8,2,1024,128]{3,2,1,0:T(8,128)S(1)} %bitcast.8, bf16[2,1024,1024]{2,1,0:T(8,128)(2,1)S(1)} %table.1.table_ref), custom_call_target="tpu_custom_call" | custom-call | tf_op jit(solution)/shard_map/fourier/pallas_call | solution.py:241
  136.3 0.0 copy-start.1
  136.3 0.0 copy-start.2
  136.3 65.9 %all_to_all.21.refs_1_ = f32[128,2,2,2,8,128]{5,4,3,2,1,0:T(8,128)S(1)} all-to-all(f32[128,2,2,2,8,128]{5,4,3,2,1,0:T(8,128)S(1)} %fourier.1), channel_id=1, replica_groups=mesh['az'=8,'col'=16] {'az','col'}, dimensions={0} | all-to-all | bytes 8388608 | tf_op jit(solution)/shard_map/all_to_all | solution.py:430
  202.1 0.0 copy-done.4
  202.1 0.0 copy-done.1
  202.1 0.0 copy-done.2
  202.1 10.4 %spectral.1 = f32[128,4,8,128]{3,2,1,0:T(8,128)S(1)} custom-call(s32[4]{0:T(128)S(1)} %dynamic-slice_reduce_fusion.refs_0_, f32[128,2,2,2,8,128]{5,4,3,2,1,0:T(8,128)S(1)} %all_to_all.21.refs_1_, bf16[4,1024,512]{2,1,0:T(8,128)(2,1)S(1)} %copy-done.1, bf16[64,64,512]{2,1,0:T(8,128)(2,1)S(1)} %bitcast.11, f32[128,512]{1,0:T(8,128)S(1)} %copy-done.4), custom_call_target="tpu_custom_call" | custom-call | tf_op jit(solution)/shard_map/spectral/pallas_call | solution.py:321
  212.5 35.7 %all_to_all.22 = f32[128,4,8,128]{3,2,1,0:T(8,128)S(1)} all-to-all(f32[128,4,8,128]{3,2,1,0:T(8,128)S(1)} %spectral.1), channel_id=1, replica_groups=mesh['az'=8,'col'=16] {'az','col'}, dimensions={0} | all-to-all | bytes 4194304 | tf_op jit(solution)/shard_map/all_to_all | solution.py:430
  248.2 6.3 %inverse.1 = f32[2,4,1024,128]{3,2,1,0:T(8,128)S(1)} custom-call(f32[4096,128]{1,0:T(8,128)S(1)} %bitcast.10, bf16[2,1024,1024]{2,1,0:T(8,128)(2,1)S(1)} %table.1.table_ref), custom_call_target="tpu_custom_call" | custom-call | tf_op jit(solution)/shard_map/inverse/pallas_call | solution.py:391
  254.6 51.6 %all_to_all.23.w_ref = f32[8,64,2,8,128]{4,3,2,1,0:T(8,128)S(1)} all-to-all(f32[8,64,2,8,128]{4,3,2,1,0:T(8,128)S(1)} %bitcast.9), channel_id=1, replica_groups=mesh['az'=8,'col'=16] {'az'}, dimensions={0} | all-to-all | bytes 8388608 | tf_op jit(solution)/shard_map/all_to_all | solution.py:430
  306.2 2.6 gather.1
  (4 shorter events, 0.0 us)
Async XLA Ops:
  0.0 16.6 %copy-start.3 = (f32[1024,128]{1,0:T(8,128)S(1)}, f32[1024,128]{1,0:T(8,128)}, u32[]{:S(2)}) copy-start(f32[1024,128]{1,0:T(8,128)} %constant.66.clone.refs_4_) | copy-start | bytes 1572868
  0.0 16.6 %copy-start.5 = (f32[64]{0:T(128)S(1)}, f32[64]{0:T(128)}, u32[]{:S(2)}) copy-start(f32[64]{0:T(128)} %constant.68.clone.refs_1_) | copy-start | bytes 772
  0.0 11.8 %slice-start = ((s32[128,4]{0,1:T(4,128)}), s32[128,2]{0,1:T(2,128)S(1)}, s32[]{:S(2)}) async-start(s32[128,4]{0,1:T(4,128)} %param.10), calls=%async_computation.4 | async-start | bytes 2048 | tf_op jit(solution)/shard_map/slice | solution.py:168
  0.0 14.3 %copy-start.6 = (s32[128,4]{0,1:T(4,128)S(1)}, s32[128,4]{0,1:T(4,128)}, u32[]{:S(2)}) copy-start(s32[128,4]{0,1:T(4,128)} %param.10) | copy-start | bytes 6148
  4.4 12.1 %collective-permute-start = (f32[64,128]{1,0:T(8,128)}, f32[64,128]{1,0:T(8,128)S(1)}, u32[]{:S(2)}, u32[]{:S(2)}) collective-permute-start(f32[64,128]{1,0:T(8,128)} %get-tuple-element.12), channel_id=1, source_target_pairs={{0,16},{16,32},{32,48},{48,64},{64,80},{80,96},{96,112},{112,0},{1... | collective-permute-start | bytes 98312 | tf_op jit(solution)/shard_map/ppermute | solution.py:453
  6.2 10.4 %collective-permute-start.1 = (f32[64,128]{1,0:T(8,128)}, f32[64,128]{1,0:T(8,128)S(1)}, u32[]{:S(2)}, u32[]{:S(2)}) collective-permute-start(f32[64,128]{1,0:T(8,128)} %get-tuple-element.13), channel_id=1, source_target_pairs={{16,0},{32,16},{48,32},{64,48},{80,64},{96,80},{112,96},{0,112},{1... | collective-permute-start | bytes 98312 | tf_op jit(solution)/shard_map/ppermute | solution.py:454
  9.0 7.5 %collective-permute-start.2 = (f32[64,256]{1,0:T(8,128)}, f32[64,256]{1,0:T(8,128)S(1)}, u32[]{:S(2)}, u32[]{:S(2)}) collective-permute-start(f32[64,256]{1,0:T(8,128)} %get-tuple-element.14), channel_id=1, source_target_pairs={{0,1},{1,2},{2,3},{3,4},{4,5},{5,6},{6,7},{7,8},{8,9},{9,10},{10,1... | collective-permute-start | bytes 196616 | tf_op jit(solution)/shard_map/ppermute | solution.py:455
  10.5 6.1 %collective-permute-start.3 = (f32[64,256]{1,0:T(8,128)}, f32[64,256]{1,0:T(8,128)S(1)}, u32[]{:S(2)}, u32[]{:S(2)}) collective-permute-start(f32[64,256]{1,0:T(8,128)} %get-tuple-element.15), channel_id=1, source_target_pairs={{1,0},{2,1},{3,2},{4,3},{5,4},{6,5},{7,6},{8,7},{9,8},{10,9},{11,1... | collective-permute-start | bytes 196616 | tf_op jit(solution)/shard_map/ppermute | solution.py:456
  14.3 2.4 copy-start
  122.5 79.6 %copy-start.4 = (f32[128,512]{1,0:T(8,128)S(1)}, f32[128,512]{1,0:T(8,128)}, u32[]{:S(2)}) copy-start(f32[128,512]{1,0:T(8,128)} %constant.67.clone.refs_4_) | copy-start | bytes 786436
  136.3 65.9 %copy-start.1 = (bf16[4,1024,512]{2,1,0:T(8,128)(2,1)S(1)}, bf16[4,1024,512]{2,1,0:T(8,128)(2,1)}, u32[]{:S(2)}) copy-start(bf16[4,1024,512]{2,1,0:T(8,128)(2,1)} %refs_2_.3) | copy-start | bytes 12582916
  136.3 65.9 %copy-start.2 = (bf16[512,64,64]{0,2,1:T(8,128)(2,1)S(1)}, bf16[512,64,64]{0,2,1:T(8,128)(2,1)}, u32[]{:S(2)}) copy-start(bf16[512,64,64]{0,2,1:T(8,128)(2,1)} %param.12) | copy-start | bytes 12582916

commit v4 on v3

--- a/solution.py
+++ b/solution.py
@@ -50,63 +50,62 @@
     return first, second
 
 
-def edges_kernel(c_ref, west_ref, east_ref, north_ref, south_ref):
+def edges_kernel(where_ref, c_ref, az_even_ref, az_odd_ref, col_even_ref, col_odd_ref):
     shells, rows, cols = c_ref.shape
-    block = pl.program_id(0)
     lane = lax.broadcasted_iota(jnp.int32, (rows, 128), 1)
-    west = jnp.where(block == 0, 0.0, west_ref[...])
-    east = jnp.where(block == 0, 0.0, east_ref[...])
+    low = jnp.zeros((rows, 128), f32)
+    high = jnp.zeros((rows, 128), f32)
     for k in range(shells):
-        at = block * shells + k
-        west = jnp.where(lane == at, pltpu.roll(c_ref[k, :, :128], at, 1), west)
-        east = jnp.where(lane == at, pltpu.roll(c_ref[k, :, cols - 128 :], at + 1, 1), east)
-    west_ref[...] = west
-    east_ref[...] = east
-    north_ref[...] = c_ref[:, 0, :]
-    south_ref[...] = c_ref[:, rows - 1, :]
-
-
-def edges_stage(phase):
+        low = jnp.where(lane == k, pltpu.roll(c_ref[k, :, :128], k, 1), low)
+        high = jnp.where(lane == k, pltpu.roll(c_ref[k, :, cols - 128 :], k + 1, 1), high)
+    odd = where_ref[0] % 2 == 1
+    az_even_ref[...] = jnp.where(odd, low, high)
+    az_odd_ref[...] = jnp.where(odd, high, low)
+    low, high = c_ref[:, 0, :], c_ref[:, rows - 1, :]
+    odd = where_ref[1] % 2 == 1
+    col_even_ref[...] = jnp.where(odd, low, high)
+    col_odd_ref[...] = jnp.where(odd, high, low)
+
+
+def edges_stage(phase, where):
     shells, rows, cols = phase.shape
-    kb = 16
+    whole = pl.BlockSpec(memory_space=pltpu.VMEM)
     return pl.pallas_call(
         edges_kernel,
-        grid=(shells // kb,),
-        in_specs=[pl.BlockSpec((kb, rows, cols), lambda i: (i, 0, 0))],
-        out_specs=[
-            pl.BlockSpec((rows, 128), lambda i: (0, 0)),
-            pl.BlockSpec((rows, 128), lambda i: (0, 0)),
-            pl.BlockSpec((kb, cols), lambda i: (i, 0)),
-            pl.BlockSpec((kb, cols), lambda i: (i, 0)),
-        ],
+        in_specs=[pl.BlockSpec(memory_space=pltpu.SMEM), whole],
+        out_specs=[whole] * 4,
         out_shape=[
             jax.ShapeDtypeStruct((rows, 128), f32),
             jax.ShapeDtypeStruct((rows, 128), f32),
             jax.ShapeDtypeStruct((shells, cols), f32),
             jax.ShapeDtypeStruct((shells, cols), f32),
         ],
-        compiler_params=params(61),
+        compiler_params=params(32),
         name="edges",
-    )(phase)
-
-
-def stencil_kernel(scale_phi, where_ref, scale_ref, c_ref, v_ref, w_ref, west_ref, east_ref, north_ref, south_ref, out_ref):
+    )(where, phase)
+
+
+def stencil_kernel(scale_phi, where_ref, scale_ref, c_ref, v_ref, w_ref, az_even_ref, az_odd_ref, col_even_ref, col_odd_ref, out_ref):
     shells, rows, cols = c_ref.shape
     block = pl.program_id(0)
     weights = jnp.concatenate([w_ref[...]] * (cols // 128), axis=1)
     lane = lax.broadcasted_iota(jnp.int32, (rows, cols), 1)
     row = lax.broadcasted_iota(jnp.int32, (rows, cols), 0)
     turn = jnp.where(block == 0, 0, 128 - block * shells)
-    west_all = pltpu.roll(west_ref[...], turn, 1)
-    east_all = pltpu.roll(east_ref[...], turn, 1)
+    odd = where_ref[0] % 2 == 1
+    west_all = pltpu.roll(jnp.where(odd, az_even_ref[...], az_odd_ref[...]), turn, 1)
+    east_all = pltpu.roll(jnp.where(odd, az_odd_ref[...], az_even_ref[...]), turn, 1)
+    odd = where_ref[1] % 2 == 1
+    north_all = jnp.where(odd, col_even_ref[...], col_odd_ref[...])
+    south_all = jnp.where(odd, col_odd_ref[...], col_even_ref[...])
     for k in range(shells):
         x = c_ref[k]
         west_edge = jnp.broadcast_to(west_all[:, k : k + 1], (rows, cols))
         east_edge = jnp.broadcast_to(east_all[:, k : k + 1], (rows, cols))
         west = jnp.where(lane == 0, west_edge, pltpu.roll(x, 1, 1))
         east = jnp.where(lane == cols - 1, east_edge, pltpu.roll(x, cols - 1, 1))
-        north = jnp.where(row == 0, north_ref[k : k + 1, :], pltpu.roll(x, 1, 0))
-        south = jnp.where(row == rows - 1, south_ref[k : k + 1, :], pltpu.roll(x, rows - 1, 0))
+        north = jnp.where(row == 0, north_all[k : k + 1, :], pltpu.roll(x, 1, 0))
+        south = jnp.where(row == rows - 1, south_all[k : k + 1, :], pltpu.roll(x, rows - 1, 0))
         spin = v_ref[0, k].astype(f32)
         sweep = v_ref[1, k].astype(f32)
         scale_theta = scale_ref[block * shells + k]
@@ -119,7 +118,7 @@
                 out_ref[a, 1, k, h] = z[8 * a : 8 * a + 8, 128 * h : 128 * h + 128]
 
 
-def stencil_stage(phase, velocity, weights, where, west, east, north, south, scale_phi, scale_theta):
+def stencil_stage(phase, velocity, weights, where, halos, scale_phi, scale_theta):
     shells, rows, cols = phase.shape
     kb = 16
 
@@ -135,7 +134,7 @@
                 pl.BlockSpec(memory_space=pltpu.SMEM),
                 pl.BlockSpec((kb, rows, cols), lambda i, s: (i, 0, 0)),
                 pl.BlockSpec((2, kb, rows, cols), lambda i, s: (0, i, 0, 0)),
-                pl.BlockSpec((rows, 128), lambda i, s: (s[0], 0)),
+                pl.BlockSpec((rows, 128), lambda i, s: (s[1], 0)),
                 pl.BlockSpec((rows, 128), lambda i, s: (0, 0)),
                 pl.BlockSpec((rows, 128), lambda i, s: (0, 0)),
                 pl.BlockSpec((kb, cols), lambda i, s: (i, 0)),
@@ -146,7 +145,7 @@
         out_shape=jax.ShapeDtypeStruct((rows // 8, 2, shells, cols // 128, 8, 128), f32),
         compiler_params=params(48),
         name="stencil",
-    )(where, scale_theta, phase, velocity, weights, west, east, north, south)
+    )(where, scale_theta, phase, velocity, weights, *halos)
 
 
 def table_kernel(fine_ref, coarse_ref, out_ref):
@@ -197,60 +196,60 @@
     )(fine, coarse)
 
 
-def fourier_kernel(p_ref, table_ref, out_ref, xh, xl, ysc):
+def fourier_kernel(p_ref, table_ref, out_ref, xh, xl):
     parts, fields = p_ref.shape[:2]
     half = parts // 2
-    per = xh.shape[0] // 8
-    tiles = xh.shape[1] // half // 128
+    per = xh.shape[1] // 8
+    tiles = xh.shape[2] // half // 128
     both = table_ref.shape[1] // 2
     count = both // 2
     owners = count // 2
-
-    def one(index, carry):
-        f, parity = index // 2, index % 2
-        sign = jnp.where(parity == 0, 1.0, -1.0).astype(f32)
+    stride = out_ref.shape[0] // owners
+
+    def one(f, carry):
         for a in range(half):
             for t in range(8):
                 for j in range(tiles):
                     strided = pl.ds(8 * j + t, per, stride=8 * tiles)
-                    x = p_ref[a, f, strided, :] + sign * p_ref[a + half, f, strided, :]
-                    h, l = split(x)
+                    near, far = p_ref[a, f, strided, :], p_ref[a + half, f, strided, :]
                     lanes = slice((a * tiles + j) * 128, (a * tiles + j + 1) * 128)
-                    xh[t * per : (t + 1) * per, lanes] = h
-                    xl[t * per : (t + 1) * per, lanes] = l
-        y = dot_nt(table_ref[parity], xh[...])
-        y = y[:both] + (y[both:] + dot_nt(table_ref[parity, :both], xl[...]))
-        for u in range(4):
-            first, second = swap_halves(y[:count, 128 * u : 128 * u + 128], y[count:, 128 * u : 128 * u + 128])
-            ysc[pl.ds(2 * u, count, stride=8), :] = first
-            ysc[pl.ds(2 * u + 1, count, stride=8), :] = second
-        for s in range(2):
-            out_ref[:, f, parity, s] = ysc[s * owners * 8 : (s + 1) * owners * 8, :].reshape(owners, 8, 128)
+                    for parity, x in enumerate((near + far, near - far)):
+                        h, l = split(x)
+                        xh[parity, t * per : (t + 1) * per, lanes] = h
+                        xl[parity, t * per : (t + 1) * per, lanes] = l
+        for parity in range(2):
+            y = dot_nt(table_ref[parity], xh[parity])
+            y = y[:both] + (y[both:] + dot_nt(table_ref[parity, :both], xl[parity]))
+            for u in range(4):
+                pair = swap_halves(y[:count, 128 * u : 128 * u + 128], y[count:, 128 * u : 128 * u + 128])
+                for s in range(2):
+                    for v in range(2):
+                        at = f * (stride // fields) + (2 * parity + s) * 8 + 2 * u + v
+                        out_ref[pl.ds(at, owners, stride=stride), :] = pair[v][s * owners : (s + 1) * owners]
         return carry
 
-    lax.fori_loop(0, 2 * fields, one, 0)
+    lax.fori_loop(0, fields, one, 0)
 
 
 def fourier_stage(rows_all, table):
     parts, fields, shells, tiles, tb, _ = rows_all.shape
     half_phi = table.shape[2]
-    modes2 = table.shape[1] // 2
-    owners = modes2 // 4
+    owners = table.shape[1] // 8
     flat = rows_all.reshape(parts, fields, shells * tiles * tb, 128)
     whole = pl.BlockSpec(memory_space=pltpu.VMEM)
-    return pl.pallas_call(
+    out = pl.pallas_call(
         fourier_kernel,
         in_specs=[whole, whole],
         out_specs=whole,
-        out_shape=jax.ShapeDtypeStruct((owners, fields, 2, 2, 8, 128), f32),
+        out_shape=jax.ShapeDtypeStruct((owners * fields * 4 * 8, 128), f32),
         scratch_shapes=[
-            pltpu.VMEM((shells * tb, half_phi), bf16),
-            pltpu.VMEM((shells * tb, half_phi), bf16),
-            pltpu.VMEM((modes2 * 4, 128), f32),
+            pltpu.VMEM((2, shells * tb, half_phi), bf16),
+            pltpu.VMEM((2, shells * tb, half_phi), bf16),
         ],
         compiler_params=params(32),
         name="fourier",
     )(flat, table)
+    return out.reshape(owners, fields, 2, 2, 8, 128)
 
 
 def spectral_kernel(az, col, mode_ref, r_ref, leg, rad, fac_ref, out_ref, xh, xl, rhs, sol, radf):
@@ -443,17 +442,19 @@
 
     weights = (colat_weights(theta_count) / phi_count).astype(np.float32)
     weights = jnp.asarray(np.repeat(weights[:, None], 128, axis=1))
-    where = jnp.reshape(col_here, (1,)).astype(jnp.int32)
-
-    west_out, east_out, north_out, south_out = edges_stage(phase_field)
-    forward_az = [(i, (i + 1) % az_count) for i in range(az_count)]
-    backward_az = [(target, source) for source, target in forward_az]
-    forward_col = [(i, i + 1) for i in range(col_count - 1)]
-    backward_col = [(target, source) for source, target in forward_col]
-    west = lax.ppermute(east_out, "az", forward_az)
-    east = lax.ppermute(west_out, "az", backward_az)
-    north = lax.ppermute(south_out, "col", forward_col)
-    south = lax.ppermute(north_out, "col", backward_col)
+    where = jnp.stack([az_here, col_here]).astype(jnp.int32)
+
+    az_even, az_odd, col_even, col_odd = edges_stage(phase_field, where)
+    even_az = [(i, i ^ 1) for i in range(az_count)]
+    odd_az = [(i, (i + 1 if i % 2 else i - 1) % az_count) for i in range(az_count)]
+    even_col = [(i, i ^ 1) for i in range(col_count)]
+    odd_col = [(i, i + 1 if i % 2 else i - 1) for i in range(1, col_count - 1)]
+    halos = (
+        lax.ppermute(az_even, "az", even_az),
+        lax.ppermute(az_odd, "az", odd_az),
+        lax.ppermute(col_even, "col", even_col),
+        lax.ppermute(col_odd, "col", odd_col),
+    )
 
     here = az_here * col_count + col_here
     own = lax.dynamic_slice(owned_modes, (here, 0), (1, owned_modes.shape[1])).reshape(-1)
@@ -466,7 +467,7 @@
     scale_phi = step_time * phi_count / (4.0 * math.pi)
     scale_theta = jnp.asarray((step_time * theta_count / (2.0 * math.pi) / radius).astype(np.float32))
     fields = stencil_stage(
-        phase_field, velocity, weights, where, west, east, north, south, scale_phi, scale_theta
+        phase_field, velocity, weights, where, halos, scale_phi, scale_theta
     )
     fields, table, own = lax.optimization_barrier((fields, table, own))
     received = exchange(fourier_stage(exchange(fields, "az"), table), everyone)

time: 309 us -> 306 us (level)
  Pallas kernels: 47.6 us -> 44.2 us
where the time goes in v4:
time: 306 us; the launch traced here: 305 us
  blocking collectives  250 us (82%)
  Pallas kernels  44.2 us (14%)
  starting transfers between devices  5.93 us (2%)
    all_to_all x4, blocking collectives, exchange(): return lax.all_to_all(x, axes, split_axis=0, concat_axis=0, tiled=True)  250 us
    pallas_call x1, Pallas kernels, fourier_stage(): pl.pallas_call(fourier_kernel, in_specs=[whole, whole], out_specs=whole,...  12.6 us
    pallas_call x1, Pallas kernels, spectral_stage(): pl.pallas_call(kernel, in_specs=[pl.BlockSpec(memory_space=pltpu.SMEM), w...  10.3 us
    pallas_call x1, Pallas kernels, stencil_stage(): pl.pallas_call(kernel, grid_spec=pltpu.PrefetchScalarGridSpec(num_scalar_...  8.45 us
    pallas_call x1, Pallas kernels, inverse_stage(): pl.pallas_call(inverse_kernel, in_specs=[whole, whole], out_specs=whole,...  6.26 us
  transfers between devices with their start and end apart: 4, of which 0 were waited for; matrix products, arithmetic and copies ran while one was open for 1% of the time, Pallas kernels for 1%

profile of v4, /device:TPU:0, one launch (start us, length us, event | category | flops | bytes accessed | tf_op | source)
XLA Modules:
  0.0 305.1 jit_solution(10778735466433190290)
XLA Ops:
  0.0 0.0 slice-start
  0.0 0.0 copy-start.7
  0.0 0.1 pad_add_fusion.1.where_ref.refs_0_
  0.1 0.0 copy-start
  0.1 2.2 copy-done
  2.3 0.0 copy-start.4
  2.3 0.0 copy-start.6
  2.3 1.8 edges.1
  4.1 1.7 collective-permute-start
  5.8 3.5 %collective-permute-start.1 = (f32[64,128]{1,0:T(8,128)S(1)}, f32[64,128]{1,0:T(8,128)S(1)}, u32[]{:S(2)}, u32[]{:S(2)}) collective-permute-start(f32[64,128]{1,0:T(8,128)S(1)} %get-tuple-element.13), channel_id=1, source_target_pairs={{0,112},{16,32},{32,16},{48,64},{64,48},{80,96},{96,80},{112,0},{1... | collective-permute-start | bytes 98312 | tf_op jit(solution)/shard_map/ppermute | solution.py:454
  9.3 0.0 collective-permute-start.2
  9.3 0.7 collective-permute-start.3
  10.0 0.0 slice-done
  10.1 0.1 iota_multiply_fusion
  10.2 0.1 broadcast_multiply_fusion
  10.3 2.0 fusion.2.fine_ref
  12.2 0.2 fusion.6.coarse_ref
  12.5 0.0 copy-done.7
  12.5 0.0 copy-start.1
  12.5 0.2 dynamic-slice_reduce_fusion.refs_0_
  12.7 2.1 table.1.table_ref
  14.8 0.0 collective-permute-done.refs_5_
  14.8 0.0 collective-permute-done.1.refs_6_
  14.8 0.0 collective-permute-done.2.refs_7_
  14.8 0.0 collective-permute-done.3.refs_8_
  14.8 0.0 copy-done.4
  14.8 0.0 copy-done.6
  14.8 0.0 copy-done.1
  14.8 8.5 %stencil.1 = f32[8,2,64,2,8,128]{5,4,3,2,1,0:T(8,128)} custom-call(s32[2]{0:T(128)S(1)} %pad_add_fusion.1.where_ref.refs_0_, f32[64]{0:T(128)S(1)} %copy-done.6, f32[64,64,256]{2,1,0:T(8,128)S(1)} %copy-done.1, bf16[2,64,64,256]{3,2,1,0:T(8,128)(2,1)} %refs_3_.1, f32[1024,128]{1,0:T(8,128)S(1)} %copy-done.4, f32[64,128]{1,0:T(8,128)S(1)} %collective-permute-done.refs_5_, ...), custom_call_target="tpu_custom_call" | custom-call | tf_op jit(solution)/shard_map/stencil/pallas_call | solution.py:128
  23.3 98.0 %all_to_all.20 = f32[8,2,64,2,8,128]{5,4,3,2,1,0:T(8,128)S(1)} all-to-all(f32[8,2,64,2,8,128]{5,4,3,2,1,0:T(8,128)} %stencil.1), channel_id=1, replica_groups=mesh['az'=8,'col'=16] {'az'}, dimensions={0} | all-to-all | bytes 16777216 | tf_op jit(solution)/shard_map/all_to_all | solution.py:429
  121.2 0.0 copy-start.5
  121.2 12.6 %fourier.1 = f32[8192,128]{1,0:T(8,128)S(1)} custom-call(f32[8,2,1024,128]{3,2,1,0:T(8,128)S(1)} %bitcast.10, bf16[2,1024,1024]{2,1,0:T(8,128)(2,1)S(1)} %table.1.table_ref), custom_call_target="tpu_custom_call" | custom-call | tf_op jit(solution)/shard_map/fourier/pallas_call | solution.py:240
  133.9 0.0 copy-start.2
  133.9 0.0 copy-start.3
  133.9 64.7 %all_to_all.21.refs_1_ = f32[128,2,2,2,8,128]{5,4,3,2,1,0:T(8,128)S(1)} all-to-all(f32[128,2,2,2,8,128]{5,4,3,2,1,0:T(8,128)S(1)} %bitcast.12), channel_id=1, replica_groups=mesh['az'=8,'col'=16] {'az','col'}, dimensions={0} | all-to-all | bytes 8388608 | tf_op jit(solution)/shard_map/all_to_all | solution.py:429
  198.5 0.0 copy-done.5
  198.5 0.0 copy-done.2
  198.5 0.0 copy-done.3
  198.5 10.3 %spectral.1 = f32[128,4,8,128]{3,2,1,0:T(8,128)S(1)} custom-call(s32[4]{0:T(128)S(1)} %dynamic-slice_reduce_fusion.refs_0_, f32[128,2,2,2,8,128]{5,4,3,2,1,0:T(8,128)S(1)} %all_to_all.21.refs_1_, bf16[4,1024,512]{2,1,0:T(8,128)(2,1)S(1)} %copy-done.2, bf16[64,64,512]{2,1,0:T(8,128)(2,1)S(1)} %bitcast.14, f32[128,512]{1,0:T(8,128)S(1)} %copy-done.5), custom_call_target="tpu_custom_call" | custom-call | tf_op jit(solution)/shard_map/spectral/pallas_call | solution.py:320
  208.9 35.7 %all_to_all.22 = f32[128,4,8,128]{3,2,1,0:T(8,128)S(1)} all-to-all(f32[128,4,8,128]{3,2,1,0:T(8,128)S(1)} %spectral.1), channel_id=1, replica_groups=mesh['az'=8,'col'=16] {'az','col'}, dimensions={0} | all-to-all | bytes 4194304 | tf_op jit(solution)/shard_map/all_to_all | solution.py:429
  244.6 6.3 %inverse.1 = f32[2,4,1024,128]{3,2,1,0:T(8,128)S(1)} custom-call(f32[4096,128]{1,0:T(8,128)S(1)} %bitcast.13, bf16[2,1024,1024]{2,1,0:T(8,128)(2,1)S(1)} %table.1.table_ref), custom_call_target="tpu_custom_call" | custom-call | tf_op jit(solution)/shard_map/inverse/pallas_call | solution.py:390
  250.9 51.6 %all_to_all.23.w_ref = f32[8,64,2,8,128]{4,3,2,1,0:T(8,128)S(1)} all-to-all(f32[8,64,2,8,128]{4,3,2,1,0:T(8,128)S(1)} %bitcast.11), channel_id=1, replica_groups=mesh['az'=8,'col'=16] {'az'}, dimensions={0} | all-to-all | bytes 8388608 | tf_op jit(solution)/shard_map/all_to_all | solution.py:429
  302.5 2.6 gather.1
  (4 shorter events, 0.0 us)
Async XLA Ops:
  0.0 10.0 %slice-start = ((s32[128,4]{0,1:T(4,128)}), s32[128,2]{0,1:T(2,128)S(1)}, s32[]{:S(2)}) async-start(s32[128,4]{0,1:T(4,128)} %param.10), calls=%async_computation.4 | async-start | bytes 2048 | tf_op jit(solution)/shard_map/slice | solution.py:167
  0.0 12.5 %copy-start.7 = (s32[128,4]{0,1:T(4,128)S(1)}, s32[128,4]{0,1:T(4,128)}, u32[]{:S(2)}) copy-start(s32[128,4]{0,1:T(4,128)} %param.10) | copy-start | bytes 6148
  0.1 2.2 copy-start
  2.3 12.5 %copy-start.4 = (f32[1024,128]{1,0:T(8,128)S(1)}, f32[1024,128]{1,0:T(8,128)}, u32[]{:S(2)}) copy-start(f32[1024,128]{1,0:T(8,128)} %constant.66.clone.refs_4_) | copy-start | bytes 1572868
  2.3 12.5 %copy-start.6 = (f32[64]{0:T(128)S(1)}, f32[64]{0:T(128)}, u32[]{:S(2)}) copy-start(f32[64]{0:T(128)} %constant.68.clone.refs_1_) | copy-start | bytes 772
  4.1 10.7 %collective-permute-start = (f32[64,128]{1,0:T(8,128)S(1)}, f32[64,128]{1,0:T(8,128)S(1)}, u32[]{:S(2)}, u32[]{:S(2)}) collective-permute-start(f32[64,128]{1,0:T(8,128)S(1)} %get-tuple-element.12), channel_id=1, source_target_pairs={{0,16},{16,0},{32,48},{48,32},{64,80},{80,64},{96,112},{112,96},{1... | collective-permute-start | bytes 98312 | tf_op jit(solution)/shard_map/ppermute | solution.py:453
  5.8 9.0 %collective-permute-start.1 = (f32[64,128]{1,0:T(8,128)S(1)}, f32[64,128]{1,0:T(8,128)S(1)}, u32[]{:S(2)}, u32[]{:S(2)}) collective-permute-start(f32[64,128]{1,0:T(8,128)S(1)} %get-tuple-element.13), channel_id=1, source_target_pairs={{0,112},{16,32},{32,16},{48,64},{64,48},{80,96},{96,80},{112,0},{1... | collective-permute-start | bytes 98312 | tf_op jit(solution)/shard_map/ppermute | solution.py:454
  9.3 5.4 %collective-permute-start.2 = (f32[64,256]{1,0:T(8,128)S(1)}, f32[64,256]{1,0:T(8,128)S(1)}, u32[]{:S(2)}, u32[]{:S(2)}) collective-permute-start(f32[64,256]{1,0:T(8,128)S(1)} %get-tuple-element.14), channel_id=1, source_target_pairs={{0,1},{1,0},{2,3},{3,2},{4,5},{5,4},{6,7},{7,6},{8,9},{9,8},{10,11... | collective-permute-start | bytes 196616 | tf_op jit(solution)/shard_map/ppermute | solution.py:455
  9.3 5.5 %collective-permute-start.3 = (f32[64,256]{1,0:T(8,128)S(1)}, f32[64,256]{1,0:T(8,128)S(1)}, u32[]{:S(2)}, u32[]{:S(2)}) collective-permute-start(f32[64,256]{1,0:T(8,128)S(1)} %get-tuple-element.15), channel_id=1, source_target_pairs={{1,2},{2,1},{3,4},{4,3},{5,6},{6,5},{7,8},{8,7},{9,10},{10,9},{11,... | collective-permute-start | bytes 196616 | tf_op jit(solution)/shard_map/ppermute | solution.py:456
  12.5 2.4 copy-start.1
  121.2 77.3 %copy-start.5 = (f32[128,512]{1,0:T(8,128)S(1)}, f32[128,512]{1,0:T(8,128)}, u32[]{:S(2)}) copy-start(f32[128,512]{1,0:T(8,128)} %constant.67.clone.refs_4_) | copy-start | bytes 786436
  133.9 64.7 %copy-start.2 = (bf16[4,1024,512]{2,1,0:T(8,128)(2,1)S(1)}, bf16[4,1024,512]{2,1,0:T(8,128)(2,1)}, u32[]{:S(2)}) copy-start(bf16[4,1024,512]{2,1,0:T(8,128)(2,1)} %refs_2_.3) | copy-start | bytes 12582916
  133.9 64.7 %copy-start.3 = (bf16[512,64,64]{0,2,1:T(8,128)(2,1)S(1)}, bf16[512,64,64]{0,2,1:T(8,128)(2,1)}, u32[]{:S(2)}) copy-start(bf16[512,64,64]{0,2,1:T(8,128)(2,1)} %param.12) | copy-start | bytes 12582916

commit v5 on v4

--- a/solution.py
+++ b/solution.py
@@ -50,12 +50,22 @@
     return first, second
 
 
-def edges_kernel(where_ref, c_ref, az_even_ref, az_odd_ref, col_even_ref, col_odd_ref):
+def edges_kernel(where_ref, c_hbm, az_even_ref, az_odd_ref, col_even_ref, col_odd_ref, c_ref, sems):
     shells, rows, cols = c_ref.shape
+    chunks = sems.shape[0]
+    size = shells // chunks
+    copies = [
+        pltpu.make_async_copy(c_hbm.at[pl.ds(n * size, size)], c_ref.at[pl.ds(n * size, size)], sems.at[n])
+        for n in range(chunks)
+    ]
+    for copy in copies:
+        copy.start()
     lane = lax.broadcasted_iota(jnp.int32, (rows, 128), 1)
     low = jnp.zeros((rows, 128), f32)
     high = jnp.zeros((rows, 128), f32)
     for k in range(shells):
+        if k % size == 0:
+            copies[k // size].wait()
         low = jnp.where(lane == k, pltpu.roll(c_ref[k, :, :128], k, 1), low)
         high = jnp.where(lane == k, pltpu.roll(c_ref[k, :, cols - 128 :], k + 1, 1), high)
     odd = where_ref[0] % 2 == 1
@@ -72,7 +82,7 @@
     whole = pl.BlockSpec(memory_space=pltpu.VMEM)
     return pl.pallas_call(
         edges_kernel,
-        in_specs=[pl.BlockSpec(memory_space=pltpu.SMEM), whole],
+        in_specs=[pl.BlockSpec(memory_space=pltpu.SMEM), pl.BlockSpec(memory_space=pl.ANY)],
         out_specs=[whole] * 4,
         out_shape=[
             jax.ShapeDtypeStruct((rows, 128), f32),
@@ -80,42 +90,62 @@
             jax.ShapeDtypeStruct((shells, cols), f32),
             jax.ShapeDtypeStruct((shells, cols), f32),
         ],
-        compiler_params=params(32),
+        scratch_shapes=[pltpu.VMEM(phase.shape, f32), pltpu.SemaphoreType.DMA((8,))],
+        compiler_params=params(61),
         name="edges",
     )(where, phase)
 
 
-def stencil_kernel(scale_phi, where_ref, scale_ref, c_ref, v_ref, w_ref, az_even_ref, az_odd_ref, col_even_ref, col_odd_ref, out_ref):
+def stencil_kernel(
+    scale_phi, where_ref, scale_ref, c_ref, v_ref, w_ref, az_even_ref, az_odd_ref, col_even_ref, col_odd_ref, out_ref
+):
     shells, rows, cols = c_ref.shape
     block = pl.program_id(0)
-    weights = jnp.concatenate([w_ref[...]] * (cols // 128), axis=1)
-    lane = lax.broadcasted_iota(jnp.int32, (rows, cols), 1)
-    row = lax.broadcasted_iota(jnp.int32, (rows, cols), 0)
+    tiles, strips = cols // 128, rows // 8
+    lane = lax.broadcasted_iota(jnp.int32, (8, 128), 1)
+    row = lax.broadcasted_iota(jnp.int32, (8, 128), 0)
+    not_first, not_last = lane > 0, lane < 127
+    not_top, not_bottom = row > 0, row < 7
+    az_odd = where_ref[0] % 2 == 1
+    col_odd = where_ref[1] % 2 == 1
     turn = jnp.where(block == 0, 0, 128 - block * shells)
-    odd = where_ref[0] % 2 == 1
-    west_all = pltpu.roll(jnp.where(odd, az_even_ref[...], az_odd_ref[...]), turn, 1)
-    east_all = pltpu.roll(jnp.where(odd, az_odd_ref[...], az_even_ref[...]), turn, 1)
-    odd = where_ref[1] % 2 == 1
-    north_all = jnp.where(odd, col_even_ref[...], col_odd_ref[...])
-    south_all = jnp.where(odd, col_odd_ref[...], col_even_ref[...])
+    west_all = pltpu.roll(jnp.where(az_odd, az_even_ref[...], az_odd_ref[...]), turn, 1)
+    east_all = pltpu.roll(jnp.where(az_odd, az_odd_ref[...], az_even_ref[...]), turn, 1)
+    north_all = jnp.where(col_odd, col_even_ref[...], col_odd_ref[...])
+    south_all = jnp.where(col_odd, col_odd_ref[...], col_even_ref[...])
     for k in range(shells):
-        x = c_ref[k]
-        west_edge = jnp.broadcast_to(west_all[:, k : k + 1], (rows, cols))
-        east_edge = jnp.broadcast_to(east_all[:, k : k + 1], (rows, cols))
-        west = jnp.where(lane == 0, west_edge, pltpu.roll(x, 1, 1))
-        east = jnp.where(lane == cols - 1, east_edge, pltpu.roll(x, cols - 1, 1))
-        north = jnp.where(row == 0, north_all[k : k + 1, :], pltpu.roll(x, 1, 0))
-        south = jnp.where(row == rows - 1, south_all[k : k + 1, :], pltpu.roll(x, rows - 1, 0))
-        spin = v_ref[0, k].astype(f32)
-        sweep = v_ref[1, k].astype(f32)
         scale_theta = scale_ref[block * shells + k]
-        y = x - (spin * ((east - west) * scale_phi) + sweep * ((south - north) * scale_theta))
-        y = y * weights
-        z = (x * x * x - x) * weights
-        for a in range(rows // 8):
-            for h in range(cols // 128):
-                out_ref[a, 0, k, h] = y[8 * a : 8 * a + 8, 128 * h : 128 * h + 128]
-                out_ref[a, 1, k, h] = z[8 * a : 8 * a + 8, 128 * h : 128 * h + 128]
+        above, below = [], []
+        for h in range(tiles):
+            lanes = slice(128 * h, 128 * h + 128)
+            above.append(jnp.broadcast_to(north_all[k : k + 1, lanes], (8, 128)))
+            below.append(jnp.broadcast_to(south_all[k : k + 1, lanes], (8, 128)))
+        for r in range(strips):
+            these = slice(8 * r, 8 * r + 8)
+            x = [c_ref[k, these, 128 * h : 128 * h + 128] for h in range(tiles)]
+            to_east = [pltpu.roll(t, 1, 1) for t in x]
+            to_west = [pltpu.roll(t, 127, 1) for t in x]
+            west_edge = jnp.broadcast_to(west_all[these, k : k + 1], (8, 128))
+            east_edge = jnp.broadcast_to(east_all[these, k : k + 1], (8, 128))
+            weights = w_ref[these, :]
+            for h in range(tiles):
+                lanes = slice(128 * h, 128 * h + 128)
+                west = jnp.where(not_first, to_east[h], to_east[h - 1] if h else west_edge)
+                east = jnp.where(not_last, to_west[h], to_west[h + 1] if h + 1 < tiles else east_edge)
+                down = pltpu.roll(x[h], 1, 0)
+                north = jnp.where(not_top, down, above[h])
+                above[h] = down
+                up = pltpu.roll(x[h], 7, 0)
+                if r + 1 < strips:
+                    following = pltpu.roll(c_ref[k, 8 * r + 8 : 8 * r + 16, lanes], 7, 0)
+                else:
+                    following = below[h]
+                south = jnp.where(not_bottom, up, following)
+                spin = v_ref[0, k, these, lanes].astype(f32)
+                sweep = v_ref[1, k, these, lanes].astype(f32)
+                y = x[h] - (spin * ((east - west) * scale_phi) + sweep * ((south - north) * scale_theta))
+                out_ref[r, 0, k, h] = y * weights
+                out_ref[r, 1, k, h] = (x[h] * x[h] * x[h] - x[h]) * weights
 
 
 def stencil_stage(phase, velocity, weights, where, halos, scale_phi, scale_theta):
@@ -148,19 +178,38 @@
     )(where, scale_theta, phase, velocity, weights, *halos)
 
 
-def table_kernel(fine_ref, coarse_ref, out_ref):
-    modes = fine_ref.shape[2]
-    tiles = out_ref.shape[2] // 128
-    fc, fs = fine_ref[0, 0], fine_ref[1, 0]
-    coarse = [coarse_ref[i, 0].T for i in range(2)]
-    for u in range(tiles):
-        cc = jnp.broadcast_to(coarse[0][:, u : u + 1], (modes, 128))
-        cs = jnp.broadcast_to(coarse[1][:, u : u + 1], (modes, 128))
-        for i, value in enumerate((fc * cc - fs * cs, fs * cc + fc * cs)):
-            h, l = split(value)
-            lanes = slice(128 * u, 128 * u + 128)
-            out_ref[0, i * modes : (i + 1) * modes, lanes] = h
-            out_ref[0, (2 + i) * modes : (3 + i) * modes, lanes] = l
+def cos_and_minus_sin(turns, full):
+    shift = (full // 4).bit_length() - 1
+    quadrant = (turns + full // 8) >> shift
+    rest = turns - (quadrant << shift)
+    x = rest.astype(f32) * (2.0 * math.pi / full)
+    q = quadrant & 3
+    x2 = x * x
+    cos = 1.0 + x2 * (-1.0 / 2 + x2 * (1.0 / 24 + x2 * (-1.0 / 720 + x2 * (1.0 / 40320))))
+    sin = x + x * x2 * (-1.0 / 6 + x2 * (1.0 / 120 + x2 * (-1.0 / 5040 + x2 * (1.0 / 362880))))
+    swap = (q & 1) == 1
+    c = jnp.where(swap, sin, cos)
+    s = jnp.where(swap, cos, sin)
+    return jnp.where((q == 1) | (q == 2), -c, c), jnp.where(q >= 2, s, -s)
+
+
+def table_kernel(mode_ref, out_ref):
+    parities, modes, _ = mode_ref.shape
+    half_phi = out_ref.shape[2]
+    tiles = half_phi // 128
+    lane = lax.broadcasted_iota(jnp.int32, (modes, 128), 1)
+    for parity in range(parities):
+        orders = mode_ref[parity]
+        fc, fs = cos_and_minus_sin(orders * lane, 2 * half_phi)
+        coarse_c, coarse_s = cos_and_minus_sin(orders * lane * 128, 2 * half_phi)
+        for u in range(tiles):
+            cc = jnp.broadcast_to(coarse_c[:, u : u + 1], (modes, 128))
+            cs = jnp.broadcast_to(coarse_s[:, u : u + 1], (modes, 128))
+            for i, value in enumerate((fc * cc - fs * cs, fs * cc + fc * cs)):
+                h, l = split(value)
+                lanes = slice(128 * u, 128 * u + 128)
+                out_ref[parity, i * modes : (i + 1) * modes, lanes] = h
+                out_ref[parity, (2 + i) * modes : (3 + i) * modes, lanes] = l
 
 
 def wave_tables(owned_modes, phi_count):
@@ -169,31 +218,15 @@
     even = jnp.where(first_half % 2 == 0, first_half, top - first_half)
     modes = jnp.stack([even, top - even])
     count = modes.shape[1]
-    half_phi = phi_count // 2
-
-    quarter = jnp.arange(2, dtype=jnp.int32) * (phi_count // 4)
-
-    def waves(turns):
-        turns = (turns + quarter[:, None, None, None]) % phi_count
-        return jnp.cos(turns.astype(f32) * (2.0 * math.pi / phi_count))
-
-    lanes = jnp.arange(128, dtype=jnp.int32)
-    tiles = jnp.arange(half_phi // 128, dtype=jnp.int32) * 128
-    fine = waves(modes[None, :, :, None] * lanes)
-    coarse = waves(modes[None, :, None, :] * tiles[:, None])
-
+    whole = pl.BlockSpec(memory_space=pltpu.VMEM)
     return pl.pallas_call(
         table_kernel,
-        grid=(2,),
-        in_specs=[
-            pl.BlockSpec((2, 1, count, 128), lambda i: (0, i, 0, 0)),
-            pl.BlockSpec((2, 1, half_phi // 128, count), lambda i: (0, i, 0, 0)),
-        ],
-        out_specs=pl.BlockSpec((1, 4 * count, half_phi), lambda i: (i, 0, 0)),
-        out_shape=jax.ShapeDtypeStruct((2, 4 * count, half_phi), bf16),
-        compiler_params=params(40),
+        in_specs=[whole],
+        out_specs=whole,
+        out_shape=jax.ShapeDtypeStruct((2, 4 * count, phi_count // 2), bf16),
+        compiler_params=params(24),
         name="table",
-    )(fine, coarse)
+    )(jnp.broadcast_to(modes[:, :, None], (2, count, 128)))
 
 
 def fourier_kernel(p_ref, table_ref, out_ref, xh, xl):
@@ -402,24 +435,32 @@
     return out.reshape(az, shells, cols // 128, tb, 128)
 
 
-def gather_kernel(w_ref, out_ref):
-    parts, shells = w_ref.shape[:2]
-    for k in range(shells):
-        for a in range(parts):
-            for h in range(w_ref.shape[2]):
-                out_ref[k, 8 * a : 8 * a + 8, 128 * h : 128 * h + 128] = w_ref[a, k, h]
+def gather_kernel(w_ref, out_ref, sem):
+    parts, shells, tiles = w_ref.shape[:3]
+    copies = []
+    for a in range(parts):
+        for h in range(tiles):
+            copies.append(
+                pltpu.make_async_copy(
+                    w_ref.at[a, :, h],
+                    out_ref.at[:, pl.ds(8 * a, 8), pl.ds(128 * h, 128)],
+                    sem.at[a * tiles + h],
+                )
+            )
+    for copy in copies:
+        copy.start()
+    for copy in copies:
+        copy.wait()
 
 
 def gather_stage(blocks):
     parts, shells, tiles, tb, _ = blocks.shape
-    cols = tiles * 128
-    kb = 16
     return pl.pallas_call(
         gather_kernel,
-        grid=(shells // kb,),
-        in_specs=[pl.BlockSpec((parts, kb, tiles, tb, 128), lambda i: (0, i, 0, 0, 0))],
-        out_specs=pl.BlockSpec((kb, parts * tb, cols), lambda i: (i, 0, 0)),
-        out_shape=jax.ShapeDtypeStruct((shells, parts * tb, cols), f32),
+        in_specs=[pl.BlockSpec(memory_space=pltpu.VMEM)],
+        out_specs=pl.BlockSpec(memory_space=pl.ANY),
+        out_shape=jax.ShapeDtypeStruct((shells, parts * tb, tiles * 128), f32),
+        scratch_shapes=[pltpu.SemaphoreType.DMA((parts * tiles,))],
         compiler_params=params(16),
         name="gather",
     )(blocks)

time: 306 us -> 304 us (level)
  transfers between devices with their start and end apart: 4 -> 4, of which waited for: 0 -> 0; matrix products, arithmetic and copies ran while one was open for 1% -> 0% of each run, Pallas kernels for 1% -> 1%
where the time goes in v5:
time: 304 us
  blocking collectives  250 us (82%)
  Pallas kernels  45.9 us (15%)
  starting transfers between devices  5.93 us (2%)
    all_to_all x4, blocking collectives, exchange(): return lax.all_to_all(x, axes, split_axis=0, concat_axis=0, tiled=True)  250 us
    pallas_call x1, Pallas kernels, fourier_stage(): pl.pallas_call(fourier_kernel, in_specs=[whole, whole], out_specs=whole,...  12.6 us
    pallas_call x1, Pallas kernels, spectral_stage(): pl.pallas_call(kernel, in_specs=[pl.BlockSpec(memory_space=pltpu.SMEM), w...  10.3 us
    pallas_call x1, Pallas kernels, stencil_stage(): pl.pallas_call(kernel, grid_spec=pltpu.PrefetchScalarGridSpec(num_scalar_...  8.22 us
    pallas_call x1, Pallas kernels, inverse_stage(): pl.pallas_call(inverse_kernel, in_specs=[whole, whole], out_specs=whole,...  6.26 us
  transfers between devices with their start and end apart: 4, of which 0 were waited for; matrix products, arithmetic and copies ran while one was open for 0% of the time, Pallas kernels for 1%

profile of v5, /device:TPU:0, one launch (start us, length us, event | category | flops | bytes accessed | tf_op | source)
XLA Modules:
  0.0 303.6 jit_solution(6256679584468363022)
XLA Ops:
  0.0 0.0 slice-start
  0.0 0.0 copy-start.7
  0.0 0.6 pad_add_fusion.1.where_ref.refs_0_
  0.6 0.0 copy-start.3
  0.6 0.0 copy-start.5
  0.6 0.0 copy-start.6
  0.6 4.2 %edges.1 = (f32[64,128]{1,0:T(8,128)}, f32[64,128]{1,0:T(8,128)}, f32[64,256]{1,0:T(8,128)}, f32[64,256]{1,0:T(8,128)}) custom-call(s32[2]{0:T(128)} %pad_add_fusion.1.where_ref.refs_0_, f32[64,64,256]{2,1,0:T(8,128)} %refs_2_.2), custom_call_target="tpu_custom_call" | custom-call | tf_op jit(solution)/shard_map/edges/pallas_call | solution.py:83
  4.8 1.7 collective-permute-start
  6.6 3.5 %collective-permute-start.1 = (f32[64,128]{1,0:T(8,128)}, f32[64,128]{1,0:T(8,128)S(1)}, u32[]{:S(2)}, u32[]{:S(2)}) collective-permute-start(f32[64,128]{1,0:T(8,128)} %get-tuple-element.13), channel_id=1, source_target_pairs={{0,112},{16,32},{32,16},{48,64},{64,48},{80,96},{96,80},{112,0},{1... | collective-permute-start | bytes 98312 | tf_op jit(solution)/shard_map/ppermute | solution.py:495
  10.1 0.0 collective-permute-start.2
  10.1 0.7 collective-permute-start.3
  10.8 0.0 slice-done
  10.8 0.0 copy-done.7
  10.8 0.0 copy-start
  10.9 0.2 dynamic-slice_reduce_fusion.refs_0_
  11.0 0.1 broadcast_in_dim.2.mode_ref
  11.2 2.2 table.1.table_ref
  13.4 0.0 collective-permute-done.refs_5_
  13.4 0.0 collective-permute-done.1.refs_6_
  13.4 0.0 collective-permute-done.2.refs_7_
  13.4 0.0 collective-permute-done.3.refs_8_
  13.4 0.0 copy-done.3
  13.4 0.0 copy-done.5
  13.4 0.0 copy-done.6
  13.4 0.0 copy-done
  13.4 8.2 %stencil.1 = f32[8,2,64,2,8,128]{5,4,3,2,1,0:T(8,128)} custom-call(s32[2]{0:T(128)S(1)} %copy-done.5, f32[64]{0:T(128)S(1)} %copy-done.6, f32[64,64,256]{2,1,0:T(8,128)S(1)} %copy-done, bf16[2,64,64,256]{3,2,1,0:T(8,128)(2,1)} %refs_3_.1, f32[1024,128]{1,0:T(8,128)S(1)} %copy-done.3, f32[64,128]{1,0:T(8,128)S(1)} %collective-permute-done.refs_5_, ...), custom_call_target="tpu_custom_call" | custom-call | tf_op jit(solution)/shard_map/stencil/pallas_call | solution.py:158
  21.7 98.5 %all_to_all.20 = f32[8,2,64,2,8,128]{5,4,3,2,1,0:T(8,128)S(1)} all-to-all(f32[8,2,64,2,8,128]{5,4,3,2,1,0:T(8,128)} %stencil.1), channel_id=1, replica_groups=mesh['az'=8,'col'=16] {'az'}, dimensions={0} | all-to-all | bytes 16777216 | tf_op jit(solution)/shard_map/all_to_all | solution.py:470
  120.1 0.0 copy-start.4
  120.1 12.6 %fourier.1 = f32[8192,128]{1,0:T(8,128)S(1)} custom-call(f32[8,2,1024,128]{3,2,1,0:T(8,128)S(1)} %bitcast.10, bf16[2,1024,1024]{2,1,0:T(8,128)(2,1)S(1)} %table.1.table_ref), custom_call_target="tpu_custom_call" | custom-call | tf_op jit(solution)/shard_map/fourier/pallas_call | solution.py:273
  132.7 0.0 copy-start.1
  132.7 0.0 copy-start.2
  132.8 64.6 %all_to_all.21.refs_1_ = f32[128,2,2,2,8,128]{5,4,3,2,1,0:T(8,128)S(1)} all-to-all(f32[128,2,2,2,8,128]{5,4,3,2,1,0:T(8,128)S(1)} %bitcast.12), channel_id=1, replica_groups=mesh['az'=8,'col'=16] {'az','col'}, dimensions={0} | all-to-all | bytes 8388608 | tf_op jit(solution)/shard_map/all_to_all | solution.py:470
  197.4 0.0 copy-done.4
  197.4 0.0 copy-done.1
  197.4 0.0 copy-done.2
  197.4 10.3 %spectral.1 = f32[128,4,8,128]{3,2,1,0:T(8,128)S(1)} custom-call(s32[4]{0:T(128)S(1)} %dynamic-slice_reduce_fusion.refs_0_, f32[128,2,2,2,8,128]{5,4,3,2,1,0:T(8,128)S(1)} %all_to_all.21.refs_1_, bf16[4,1024,512]{2,1,0:T(8,128)(2,1)S(1)} %copy-done.1, bf16[64,64,512]{2,1,0:T(8,128)(2,1)S(1)} %bitcast.14, f32[128,512]{1,0:T(8,128)S(1)} %copy-done.4), custom_call_target="tpu_custom_call" | custom-call | tf_op jit(solution)/shard_map/spectral/pallas_call | solution.py:353
  207.7 35.7 %all_to_all.22 = f32[128,4,8,128]{3,2,1,0:T(8,128)S(1)} all-to-all(f32[128,4,8,128]{3,2,1,0:T(8,128)S(1)} %spectral.1), channel_id=1, replica_groups=mesh['az'=8,'col'=16] {'az','col'}, dimensions={0} | all-to-all | bytes 4194304 | tf_op jit(solution)/shard_map/all_to_all | solution.py:470
  243.4 6.3 %inverse.1 = f32[2,4,1024,128]{3,2,1,0:T(8,128)S(1)} custom-call(f32[4096,128]{1,0:T(8,128)S(1)} %bitcast.13, bf16[2,1024,1024]{2,1,0:T(8,128)(2,1)S(1)} %table.1.table_ref), custom_call_target="tpu_custom_call" | custom-call | tf_op jit(solution)/shard_map/inverse/pallas_call | solution.py:423
  249.7 51.6 %all_to_all.23.w_ref = f32[8,64,2,8,128]{4,3,2,1,0:T(8,128)S(1)} all-to-all(f32[8,64,2,8,128]{4,3,2,1,0:T(8,128)S(1)} %bitcast.11), channel_id=1, replica_groups=mesh['az'=8,'col'=16] {'az'}, dimensions={0} | all-to-all | bytes 8388608 | tf_op jit(solution)/shard_map/all_to_all | solution.py:470
  301.3 2.1 gather.1
  (2 shorter events, 0.0 us)
Async XLA Ops:
  0.0 10.8 %slice-start = ((s32[128,4]{0,1:T(4,128)}), s32[128,2]{0,1:T(2,128)S(1)}, s32[]{:S(2)}) async-start(s32[128,4]{0,1:T(4,128)} %param.10), calls=%async_computation.4 | async-start | bytes 2048 | tf_op jit(solution)/shard_map/slice | solution.py:216
  0.0 10.8 %copy-start.7 = (s32[128,4]{0,1:T(4,128)S(1)}, s32[128,4]{0,1:T(4,128)}, u32[]{:S(2)}) copy-start(s32[128,4]{0,1:T(4,128)} %param.10) | copy-start | bytes 6148
  0.6 12.8 %copy-start.3 = (f32[1024,128]{1,0:T(8,128)S(1)}, f32[1024,128]{1,0:T(8,128)}, u32[]{:S(2)}) copy-start(f32[1024,128]{1,0:T(8,128)} %constant.38.clone.refs_4_) | copy-start | bytes 1572868
  0.6 12.8 %copy-start.5 = (s32[2]{0:T(128)S(1)}, s32[2]{0:T(128)}, u32[]{:S(2)}) copy-start(s32[2]{0:T(128)} %pad_add_fusion.1.where_ref.refs_0_) | copy-start | bytes 28
  0.6 12.8 %copy-start.6 = (f32[64]{0:T(128)S(1)}, f32[64]{0:T(128)}, u32[]{:S(2)}) copy-start(f32[64]{0:T(128)} %constant.40.clone.refs_1_) | copy-start | bytes 772
  4.8 8.5 %collective-permute-start = (f32[64,128]{1,0:T(8,128)}, f32[64,128]{1,0:T(8,128)S(1)}, u32[]{:S(2)}, u32[]{:S(2)}) collective-permute-start(f32[64,128]{1,0:T(8,128)} %get-tuple-element.12), channel_id=1, source_target_pairs={{0,16},{16,0},{32,48},{48,32},{64,80},{80,64},{96,112},{112,96},{1... | collective-permute-start | bytes 98312 | tf_op jit(solution)/shard_map/ppermute | solution.py:494
  6.6 6.8 %collective-permute-start.1 = (f32[64,128]{1,0:T(8,128)}, f32[64,128]{1,0:T(8,128)S(1)}, u32[]{:S(2)}, u32[]{:S(2)}) collective-permute-start(f32[64,128]{1,0:T(8,128)} %get-tuple-element.13), channel_id=1, source_target_pairs={{0,112},{16,32},{32,16},{48,64},{64,48},{80,96},{96,80},{112,0},{1... | collective-permute-start | bytes 98312 | tf_op jit(solution)/shard_map/ppermute | solution.py:495
  10.1 3.3 %collective-permute-start.2 = (f32[64,256]{1,0:T(8,128)}, f32[64,256]{1,0:T(8,128)S(1)}, u32[]{:S(2)}, u32[]{:S(2)}) collective-permute-start(f32[64,256]{1,0:T(8,128)} %get-tuple-element.14), channel_id=1, source_target_pairs={{0,1},{1,0},{2,3},{3,2},{4,5},{5,4},{6,7},{7,6},{8,9},{9,8},{10,11... | collective-permute-start | bytes 196616 | tf_op jit(solution)/shard_map/ppermute | solution.py:496
  10.1 3.3 %collective-permute-start.3 = (f32[64,256]{1,0:T(8,128)}, f32[64,256]{1,0:T(8,128)S(1)}, u32[]{:S(2)}, u32[]{:S(2)}) collective-permute-start(f32[64,256]{1,0:T(8,128)} %get-tuple-element.15), channel_id=1, source_target_pairs={{1,2},{2,1},{3,4},{4,3},{5,6},{6,5},{7,8},{8,7},{9,10},{10,9},{11,... | collective-permute-start | bytes 196616 | tf_op jit(solution)/shard_map/ppermute | solution.py:497
  10.8 2.6 copy-start
  120.1 77.3 %copy-start.4 = (f32[128,512]{1,0:T(8,128)S(1)}, f32[128,512]{1,0:T(8,128)}, u32[]{:S(2)}) copy-start(f32[128,512]{1,0:T(8,128)} %constant.39.clone.refs_4_) | copy-start | bytes 786436
  132.7 64.7 %copy-start.1 = (bf16[4,1024,512]{2,1,0:T(8,128)(2,1)S(1)}, bf16[4,1024,512]{2,1,0:T(8,128)(2,1)}, u32[]{:S(2)}) copy-start(bf16[4,1024,512]{2,1,0:T(8,128)(2,1)} %refs_2_.3) | copy-start | bytes 12582916
  132.7 64.7 %copy-start.2 = (bf16[512,64,64]{0,2,1:T(8,128)(2,1)S(1)}, bf16[512,64,64]{0,2,1:T(8,128)(2,1)}, u32[]{:S(2)}) copy-start(bf16[512,64,64]{0,2,1:T(8,128)(2,1)} %param.12) | copy-start | bytes 12582916

commit v6 on v5

--- a/solution.py
+++ b/solution.py
@@ -50,7 +50,7 @@
     return first, second
 
 
-def edges_kernel(where_ref, c_hbm, az_even_ref, az_odd_ref, col_even_ref, col_odd_ref, c_ref, sems):
+def edges_kernel(c_hbm, az_even_ref, az_odd_ref, col_even_ref, col_odd_ref, c_ref, sems):
     shells, rows, cols = c_ref.shape
     chunks = sems.shape[0]
     size = shells // chunks
@@ -68,21 +68,21 @@
             copies[k // size].wait()
         low = jnp.where(lane == k, pltpu.roll(c_ref[k, :, :128], k, 1), low)
         high = jnp.where(lane == k, pltpu.roll(c_ref[k, :, cols - 128 :], k + 1, 1), high)
-    odd = where_ref[0] % 2 == 1
+    odd = lax.axis_index("az") % 2 == 1
     az_even_ref[...] = jnp.where(odd, low, high)
     az_odd_ref[...] = jnp.where(odd, high, low)
     low, high = c_ref[:, 0, :], c_ref[:, rows - 1, :]
-    odd = where_ref[1] % 2 == 1
+    odd = lax.axis_index("col") % 2 == 1
     col_even_ref[...] = jnp.where(odd, low, high)
     col_odd_ref[...] = jnp.where(odd, high, low)
 
 
-def edges_stage(phase, where):
+def edges_stage(phase):
     shells, rows, cols = phase.shape
     whole = pl.BlockSpec(memory_space=pltpu.VMEM)
     return pl.pallas_call(
         edges_kernel,
-        in_specs=[pl.BlockSpec(memory_space=pltpu.SMEM), pl.BlockSpec(memory_space=pl.ANY)],
+        in_specs=[pl.BlockSpec(memory_space=pl.ANY)],
         out_specs=[whole] * 4,
         out_shape=[
             jax.ShapeDtypeStruct((rows, 128), f32),
@@ -91,13 +91,13 @@
             jax.ShapeDtypeStruct((shells, cols), f32),
         ],
         scratch_shapes=[pltpu.VMEM(phase.shape, f32), pltpu.SemaphoreType.DMA((8,))],
-        compiler_params=params(61),
+        compiler_params=params(52),
         name="edges",
-    )(where, phase)
+    )(phase)
 
 
 def stencil_kernel(
-    scale_phi, where_ref, scale_ref, c_ref, v_ref, w_ref, az_even_ref, az_odd_ref, col_even_ref, col_odd_ref, out_ref
+    scale_phi, scale_ref, c_ref, v_ref, w_ref, az_even_ref, az_odd_ref, col_even_ref, col_odd_ref, out_ref
 ):
     shells, rows, cols = c_ref.shape
     block = pl.program_id(0)
@@ -106,8 +106,9 @@
     row = lax.broadcasted_iota(jnp.int32, (8, 128), 0)
     not_first, not_last = lane > 0, lane < 127
     not_top, not_bottom = row > 0, row < 7
-    az_odd = where_ref[0] % 2 == 1
-    col_odd = where_ref[1] % 2 == 1
+    az_odd = lax.axis_index("az") % 2 == 1
+    col_here = lax.axis_index("col")
+    col_odd = col_here % 2 == 1
     turn = jnp.where(block == 0, 0, 128 - block * shells)
     west_all = pltpu.roll(jnp.where(az_odd, az_even_ref[...], az_odd_ref[...]), turn, 1)
     east_all = pltpu.roll(jnp.where(az_odd, az_odd_ref[...], az_even_ref[...]), turn, 1)
@@ -127,7 +128,7 @@
             to_west = [pltpu.roll(t, 127, 1) for t in x]
             west_edge = jnp.broadcast_to(west_all[these, k : k + 1], (8, 128))
             east_edge = jnp.broadcast_to(east_all[these, k : k + 1], (8, 128))
-            weights = w_ref[these, :]
+            weights = w_ref[pl.ds(pl.multiple_of(col_here * rows + 8 * r, 8), 8), :]
             for h in range(tiles):
                 lanes = slice(128 * h, 128 * h + 128)
                 west = jnp.where(not_first, to_east[h], to_east[h - 1] if h else west_edge)
@@ -148,7 +149,7 @@
                 out_ref[r, 1, k, h] = (x[h] * x[h] * x[h] - x[h]) * weights
 
 
-def stencil_stage(phase, velocity, weights, where, halos, scale_phi, scale_theta):
+def stencil_stage(phase, velocity, weights, halos, scale_phi, scale_theta):
     shells, rows, cols = phase.shape
     kb = 16
 
@@ -157,25 +158,22 @@
 
     return pl.pallas_call(
         kernel,
-        grid_spec=pltpu.PrefetchScalarGridSpec(
-            num_scalar_prefetch=1,
-            grid=(shells // kb,),
-            in_specs=[
-                pl.BlockSpec(memory_space=pltpu.SMEM),
-                pl.BlockSpec((kb, rows, cols), lambda i, s: (i, 0, 0)),
-                pl.BlockSpec((2, kb, rows, cols), lambda i, s: (0, i, 0, 0)),
-                pl.BlockSpec((rows, 128), lambda i, s: (s[1], 0)),
-                pl.BlockSpec((rows, 128), lambda i, s: (0, 0)),
-                pl.BlockSpec((rows, 128), lambda i, s: (0, 0)),
-                pl.BlockSpec((kb, cols), lambda i, s: (i, 0)),
-                pl.BlockSpec((kb, cols), lambda i, s: (i, 0)),
-            ],
-            out_specs=pl.BlockSpec((rows // 8, 2, kb, cols // 128, 8, 128), lambda i, s: (0, 0, i, 0, 0, 0)),
-        ),
+        grid=(shells // kb,),
+        in_specs=[
+            pl.BlockSpec(memory_space=pltpu.SMEM),
+            pl.BlockSpec((kb, rows, cols), lambda i: (i, 0, 0)),
+            pl.BlockSpec((2, kb, rows, cols), lambda i: (0, i, 0, 0)),
+            pl.BlockSpec(weights.shape, lambda i: (0, 0)),
+            pl.BlockSpec((rows, 128), lambda i: (0, 0)),
+            pl.BlockSpec((rows, 128), lambda i: (0, 0)),
+            pl.BlockSpec((kb, cols), lambda i: (i, 0)),
+            pl.BlockSpec((kb, cols), lambda i: (i, 0)),
+        ],
+        out_specs=pl.BlockSpec((rows // 8, 2, kb, cols // 128, 8, 128), lambda i: (0, 0, i, 0, 0, 0)),
         out_shape=jax.ShapeDtypeStruct((rows // 8, 2, shells, cols // 128, 8, 128), f32),
         compiler_params=params(48),
         name="stencil",
-    )(where, scale_theta, phase, velocity, weights, *halos)
+    )(scale_theta, phase, velocity, weights, *halos)
 
 
 def cos_and_minus_sin(turns, full):
@@ -290,6 +288,7 @@
     shells = rad.shape[0]
     tb = az * 8
     tiles = degrees // 128
+    half = degrees // 2
     for q in range(4):
         parity = mode_ref[q] % 2
         for f in range(2):
@@ -297,15 +296,27 @@
                 [r_ref[a * col + c, f, parity, q % 2] for c in range(col) for a in range(az)], axis=0
             )
             h, l = split(x.T)
-            xh[f * 128 : (f + 1) * 128, :] = h
-            xl[f * 128 : (f + 1) * 128, :] = l
-        coef = dot_nn(xh[...], leg[q]) + dot_nn(xl[...], leg[q])
-        right = coef[:128] - fac_ref[...] * coef[128:]
+            xh[q, f * 128 : (f + 1) * 128, :] = h
+            xl[q, f * 128 : (f + 1) * 128, :] = l
+
+    def right_side(q, lanes):
+        coef = dot_nn(xh[q], leg[q, :, lanes]) + dot_nn(xl[q], leg[q, :, lanes])
+        return coef[:128] - fac_ref[:, lanes] * coef[128:]
+
+    def put(q, first, right):
         for i in range(2):
-            for lt in range(tiles):
-                rhs[lt, pl.ds(2 * q + i, shells, stride=8), :] = right[
-                    i * shells : (i + 1) * shells, lt * 128 : lt * 128 + 128
+            for n in range(tiles // 2):
+                rhs[first + n, pl.ds(2 * q + i, shells, stride=8), :] = right[
+                    i * shells : (i + 1) * shells, n * 128 : n * 128 + 128
                 ]
+
+    for q in range(4):
+        put(q, tiles // 2, right_side(q, slice(half, degrees)))
+    low = [jnp.where(mode_ref[s] < half, s, s + 2) for s in range(2)]
+    high = [jnp.where(mode_ref[s] < half, s + 2, s) for s in range(2)]
+    for s in range(2):
+        put(low[s], 0, right_side(low[s], slice(0, half)))
+        put(high[s], 0, jnp.zeros((2 * shells, half), f32))
 
     rb = 8
 
@@ -324,21 +335,25 @@
 
     lax.fori_loop(0, shells // rb, outer, 0)
 
-    for q in range(4):
-        parity = mode_ref[q] % 2
-        gain = jnp.where(mode_ref[q] == 0, 1.0, 2.0).astype(f32)
-        x = jnp.concatenate(
-            [
-                jnp.concatenate([sol[lt, pl.ds(2 * q + i, shells, stride=8), :] for lt in range(tiles)], axis=1)
-                for i in range(2)
-            ],
-            axis=0,
-        )
-        h, l = split(x * gain)
-        y = dot_nt(leg[q], h) + dot_nt(leg[q], l)
-        for c in range(col):
-            for a in range(az):
-                out_ref[a * col + c, 2 * parity + q % 2] = y[c * tb + a * 8 : c * tb + a * 8 + 8]
+    for s in range(2):
+        for q, first in ((low[s], 0), (high[s], tiles // 2)):
+            gain = jnp.where(mode_ref[q] == 0, 1.0, 2.0).astype(f32)
+            x = jnp.concatenate(
+                [
+                    jnp.concatenate(
+                        [sol[lt, pl.ds(2 * q + i, shells, stride=8), :] for lt in range(first, tiles)], axis=1
+                    )
+                    for i in range(2)
+                ],
+                axis=0,
+            )
+            h, l = split(x * gain)
+            matrix = leg[q, :, first * 128 :]
+            y = dot_nt(matrix, h) + dot_nt(matrix, l)
+            slot = 2 * (mode_ref[q] % 2) + s
+            for c in range(col):
+                for a in range(az):
+                    out_ref[a * col + c, slot] = y[c * tb + a * 8 : c * tb + a * 8 + 8]
 
 
 def spectral_stage(received, legendre, radial, factor, own, az, col):
@@ -355,8 +370,8 @@
         in_specs=[pl.BlockSpec(memory_space=pltpu.SMEM), whole, whole, whole, whole],
         out_specs=whole,
         scratch_shapes=[
-            pltpu.VMEM((256, theta), bf16),
-            pltpu.VMEM((256, theta), bf16),
+            pltpu.VMEM((4, 256, theta), bf16),
+            pltpu.VMEM((4, 256, theta), bf16),
             pltpu.VMEM((degrees // 128, 8 * shells, 128), f32),
             pltpu.VMEM((degrees // 128, 8 * shells, 128), f32),
             pltpu.VMEM((8, shells, degrees), f32),
@@ -393,15 +408,14 @@
                 h, l = split(halves[i][s].T)
                 at = (2 * i + s) * owners
                 gh[par, :, at : at + owners] = h
+                gh[par, :, both + at : both + at + owners] = h
                 gl[par, :, at : at + owners] = l
 
     for quarter in range(quarters):
         lanes = slice(quarter * cols, (quarter + 1) * cols)
         sums = []
         for par in range(2):
-            th, tl = table_ref[par, :both, lanes], table_ref[par, both:, lanes]
-            h, l = gh[par], gl[par]
-            sums.append(dot_nn(h, th) + (dot_nn(h, tl) + dot_nn(l, th)))
+            sums.append(dot_nn(gh[par], table_ref[par, :, lanes]) + dot_nn(gl[par], table_ref[par, :both, lanes]))
         near = sums[0] + sums[1]
         far = sums[0] - sums[1]
         for t in range(8):
@@ -426,7 +440,7 @@
         out_specs=whole,
         out_shape=jax.ShapeDtypeStruct((2, az // 2, rows * cols // 128, 128), f32),
         scratch_shapes=[
-            pltpu.VMEM((2, rows, modes2), bf16),
+            pltpu.VMEM((2, rows, 2 * modes2), bf16),
             pltpu.VMEM((2, rows, modes2), bf16),
         ],
         compiler_params=params(32),
@@ -483,9 +497,8 @@
 
     weights = (colat_weights(theta_count) / phi_count).astype(np.float32)
     weights = jnp.asarray(np.repeat(weights[:, None], 128, axis=1))
-    where = jnp.stack([az_here, col_here]).astype(jnp.int32)
-
-    az_even, az_odd, col_even, col_odd = edges_stage(phase_field, where)
+
+    az_even, az_odd, col_even, col_odd = edges_stage(phase_field)
     even_az = [(i, i ^ 1) for i in range(az_count)]
     odd_az = [(i, (i + 1 if i % 2 else i - 1) % az_count) for i in range(az_count)]
     even_col = [(i, i ^ 1) for i in range(col_count)]
@@ -508,7 +521,7 @@
     scale_phi = step_time * phi_count / (4.0 * math.pi)
     scale_theta = jnp.asarray((step_time * theta_count / (2.0 * math.pi) / radius).astype(np.float32))
     fields = stencil_stage(
-        phase_field, velocity, weights, where, halos, scale_phi, scale_theta
+        phase_field, velocity, weights, halos, scale_phi, scale_theta
     )
     fields, table, own = lax.optimization_barrier((fields, table, own))
     received = exchange(fourier_stage(exchange(fields, "az"), table), everyone)

time: 304 us -> 301 us (level)
  no operation moved by 1% of the time
where the time goes in v6:
time: 301 us
  blocking collectives  250 us (83%)
  Pallas kernels  44 us (15%)
  starting transfers between devices  5.93 us (2%)
    all_to_all x4, blocking collectives, exchange(): return lax.all_to_all(x, axes, split_axis=0, concat_axis=0, tiled=True)  250 us
    pallas_call x1, Pallas kernels, fourier_stage(): pl.pallas_call(fourier_kernel, in_specs=[whole, whole], out_specs=whole,...  13.1 us
    pallas_call x1, Pallas kernels, spectral_stage(): pl.pallas_call(kernel, in_specs=[pl.BlockSpec(memory_space=pltpu.SMEM), w...  9.59 us
    pallas_call x1, Pallas kernels, stencil_stage(): pl.pallas_call(kernel, grid=(shells // kb,), in_specs=[pl.BlockSpec(memor...  7.84 us
    pallas_call x1, Pallas kernels, inverse_stage(): pl.pallas_call(inverse_kernel, in_specs=[whole, whole], out_specs=whole,...  6.3 us
  transfers between devices with their start and end apart: 4, of which 0 were waited for; matrix products, arithmetic and copies ran while one was open for 0% of the time, Pallas kernels for 1%

profile of v6, /device:TPU:0, one launch (start us, length us, event | category | flops | bytes accessed | tf_op | source)
XLA Modules:
  0.0 300.9 jit_solution(12375464562040635589)
XLA Ops:
  0.0 0.0 copy-start.3
  0.0 0.0 copy-start.5
  0.0 0.0 slice-start
  0.0 0.0 copy-start.6
  0.0 2.9 edges.1
  2.9 1.7 collective-permute-start
  4.6 3.5 %collective-permute-start.1 = (f32[64,128]{1,0:T(8,128)S(1)}, f32[64,128]{1,0:T(8,128)S(1)}, u32[]{:S(2)}, u32[]{:S(2)}) collective-permute-start(f32[64,128]{1,0:T(8,128)S(1)} %get-tuple-element.13), channel_id=1, source_target_pairs={{0,112},{16,32},{32,16},{48,64},{64,48},{80,96},{96,80},{112,0},{1... | collective-permute-start | bytes 98312 | tf_op jit(solution)/shard_map/ppermute | solution.py:508
  8.2 0.0 collective-permute-start.2
  8.2 0.7 collective-permute-start.3
  8.8 0.0 slice-done
  8.9 0.0 copy-done.6
  8.9 0.0 copy-start
  8.9 0.2 dynamic-slice_reduce_fusion.refs_0_
  9.1 0.1 broadcast_in_dim.2.mode_ref
  9.2 2.2 table.1.table_ref
  11.4 0.0 collective-permute-done.refs_4_
  11.4 0.0 collective-permute-done.1.refs_5_
  11.4 0.0 collective-permute-done.2.refs_6_
  11.4 0.0 collective-permute-done.3.refs_7_
  11.4 0.0 copy-done.3
  11.4 0.0 copy-done.5
  11.5 0.0 copy-done
  11.5 7.8 %stencil.1 = f32[8,2,64,2,8,128]{5,4,3,2,1,0:T(8,128)} custom-call(f32[64]{0:T(128)S(1)} %copy-done.5, f32[64,64,256]{2,1,0:T(8,128)S(1)} %copy-done, bf16[2,64,64,256]{3,2,1,0:T(8,128)(2,1)} %refs_2_.2, f32[1024,128]{1,0:T(8,128)S(1)} %copy-done.3, f32[64,128]{1,0:T(8,128)S(1)} %collective-permute-done.refs_4_, ...), custom_call_target="tpu_custom_call" | custom-call | tf_op jit(solution)/shard_map/stencil/pallas_call | solution.py:159
  19.3 98.2 %all_to_all.20 = f32[8,2,64,2,8,128]{5,4,3,2,1,0:T(8,128)S(1)} all-to-all(f32[8,2,64,2,8,128]{5,4,3,2,1,0:T(8,128)} %stencil.1), channel_id=1, replica_groups=mesh['az'=8,'col'=16] {'az'}, dimensions={0} | all-to-all | bytes 16777216 | tf_op jit(solution)/shard_map/all_to_all | solution.py:484
  117.5 0.0 copy-start.4
  117.5 13.1 %fourier.1 = f32[8192,128]{1,0:T(8,128)S(1)} custom-call(f32[8,2,1024,128]{3,2,1,0:T(8,128)S(1)} %bitcast.8, bf16[2,1024,1024]{2,1,0:T(8,128)(2,1)S(1)} %table.1.table_ref), custom_call_target="tpu_custom_call" | custom-call | tf_op jit(solution)/shard_map/fourier/pallas_call | solution.py:271
  130.6 0.0 copy-start.1
  130.6 0.0 copy-start.2
  130.6 64.7 %all_to_all.21.refs_1_ = f32[128,2,2,2,8,128]{5,4,3,2,1,0:T(8,128)S(1)} all-to-all(f32[128,2,2,2,8,128]{5,4,3,2,1,0:T(8,128)S(1)} %bitcast.10), channel_id=1, replica_groups=mesh['az'=8,'col'=16] {'az','col'}, dimensions={0} | all-to-all | bytes 8388608 | tf_op jit(solution)/shard_map/all_to_all | solution.py:484
  195.3 0.0 copy-done.4
  195.3 0.0 copy-done.1
  195.3 0.0 copy-done.2
  195.3 9.6 %spectral.1 = f32[128,4,8,128]{3,2,1,0:T(8,128)S(1)} custom-call(s32[4]{0:T(128)S(1)} %dynamic-slice_reduce_fusion.refs_0_, f32[128,2,2,2,8,128]{5,4,3,2,1,0:T(8,128)S(1)} %all_to_all.21.refs_1_, bf16[4,1024,512]{2,1,0:T(8,128)(2,1)S(1)} %copy-done.1, bf16[64,64,512]{2,1,0:T(8,128)(2,1)S(1)} %bitcast.12, f32[128,512]{1,0:T(8,128)S(1)} %copy-done.4), custom_call_target="tpu_custom_call" | custom-call | tf_op jit(solution)/shard_map/spectral/pallas_call | solution.py:368
  204.9 35.7 %all_to_all.22 = f32[128,4,8,128]{3,2,1,0:T(8,128)S(1)} all-to-all(f32[128,4,8,128]{3,2,1,0:T(8,128)S(1)} %spectral.1), channel_id=1, replica_groups=mesh['az'=8,'col'=16] {'az','col'}, dimensions={0} | all-to-all | bytes 4194304 | tf_op jit(solution)/shard_map/all_to_all | solution.py:484
  240.6 6.3 %inverse.1 = f32[2,4,1024,128]{3,2,1,0:T(8,128)S(1)} custom-call(f32[4096,128]{1,0:T(8,128)S(1)} %bitcast.11, bf16[2,1024,1024]{2,1,0:T(8,128)(2,1)S(1)} %table.1.table_ref), custom_call_target="tpu_custom_call" | custom-call | tf_op jit(solution)/shard_map/inverse/pallas_call | solution.py:437
  246.9 51.6 %all_to_all.23.w_ref = f32[8,64,2,8,128]{4,3,2,1,0:T(8,128)S(1)} all-to-all(f32[8,64,2,8,128]{4,3,2,1,0:T(8,128)S(1)} %bitcast.9), channel_id=1, replica_groups=mesh['az'=8,'col'=16] {'az'}, dimensions={0} | all-to-all | bytes 8388608 | tf_op jit(solution)/shard_map/all_to_all | solution.py:484
  298.6 2.1 gather.1
  (2 shorter events, 0.0 us)
Async XLA Ops:
  0.0 11.4 %copy-start.3 = (f32[1024,128]{1,0:T(8,128)S(1)}, f32[1024,128]{1,0:T(8,128)}, u32[]{:S(2)}) copy-start(f32[1024,128]{1,0:T(8,128)} %constant.38.clone.refs_3_) | copy-start | bytes 1572868
  0.0 11.4 %copy-start.5 = (f32[64]{0:T(128)S(1)}, f32[64]{0:T(128)}, u32[]{:S(2)}) copy-start(f32[64]{0:T(128)} %constant.40.clone.refs_0_) | copy-start | bytes 772
  0.0 8.8 %slice-start = ((s32[128,4]{0,1:T(4,128)}), s32[128,2]{0,1:T(2,128)S(1)}, s32[]{:S(2)}) async-start(s32[128,4]{0,1:T(4,128)} %param.10), calls=%async_computation.4 | async-start | bytes 2048 | tf_op jit(solution)/shard_map/slice | solution.py:214
  0.0 8.9 %copy-start.6 = (s32[128,4]{0,1:T(4,128)S(1)}, s32[128,4]{0,1:T(4,128)}, u32[]{:S(2)}) copy-start(s32[128,4]{0,1:T(4,128)} %param.10) | copy-start | bytes 6148
  2.9 8.5 %collective-permute-start = (f32[64,128]{1,0:T(8,128)S(1)}, f32[64,128]{1,0:T(8,128)S(1)}, u32[]{:S(2)}, u32[]{:S(2)}) collective-permute-start(f32[64,128]{1,0:T(8,128)S(1)} %get-tuple-element.12), channel_id=1, source_target_pairs={{0,16},{16,0},{32,48},{48,32},{64,80},{80,64},{96,112},{112,96},{1... | collective-permute-start | bytes 98312 | tf_op jit(solution)/shard_map/ppermute | solution.py:507
  4.6 6.8 %collective-permute-start.1 = (f32[64,128]{1,0:T(8,128)S(1)}, f32[64,128]{1,0:T(8,128)S(1)}, u32[]{:S(2)}, u32[]{:S(2)}) collective-permute-start(f32[64,128]{1,0:T(8,128)S(1)} %get-tuple-element.13), channel_id=1, source_target_pairs={{0,112},{16,32},{32,16},{48,64},{64,48},{80,96},{96,80},{112,0},{1... | collective-permute-start | bytes 98312 | tf_op jit(solution)/shard_map/ppermute | solution.py:508
  8.2 3.3 %collective-permute-start.2 = (f32[64,256]{1,0:T(8,128)S(1)}, f32[64,256]{1,0:T(8,128)S(1)}, u32[]{:S(2)}, u32[]{:S(2)}) collective-permute-start(f32[64,256]{1,0:T(8,128)S(1)} %get-tuple-element.14), channel_id=1, source_target_pairs={{0,1},{1,0},{2,3},{3,2},{4,5},{5,4},{6,7},{7,6},{8,9},{9,8},{10,11... | collective-permute-start | bytes 196616 | tf_op jit(solution)/shard_map/ppermute | solution.py:509
  8.2 3.3 %collective-permute-start.3 = (f32[64,256]{1,0:T(8,128)S(1)}, f32[64,256]{1,0:T(8,128)S(1)}, u32[]{:S(2)}, u32[]{:S(2)}) collective-permute-start(f32[64,256]{1,0:T(8,128)S(1)} %get-tuple-element.15), channel_id=1, source_target_pairs={{1,2},{2,1},{3,4},{4,3},{5,6},{6,5},{7,8},{8,7},{9,10},{10,9},{11,... | collective-permute-start | bytes 196616 | tf_op jit(solution)/shard_map/ppermute | solution.py:510
  8.9 2.6 copy-start
  117.5 77.8 %copy-start.4 = (f32[128,512]{1,0:T(8,128)S(1)}, f32[128,512]{1,0:T(8,128)}, u32[]{:S(2)}) copy-start(f32[128,512]{1,0:T(8,128)} %constant.39.clone.refs_4_) | copy-start | bytes 786436
  130.6 64.7 %copy-start.1 = (bf16[4,1024,512]{2,1,0:T(8,128)(2,1)S(1)}, bf16[4,1024,512]{2,1,0:T(8,128)(2,1)}, u32[]{:S(2)}) copy-start(bf16[4,1024,512]{2,1,0:T(8,128)(2,1)} %refs_2_.3) | copy-start | bytes 12582916
  130.6 64.7 %copy-start.2 = (bf16[512,64,64]{0,2,1:T(8,128)(2,1)S(1)}, bf16[512,64,64]{0,2,1:T(8,128)(2,1)}, u32[]{:S(2)}) copy-start(bf16[512,64,64]{0,2,1:T(8,128)(2,1)} %param.12) | copy-start | bytes 12582916

commit v7 on v6

--- a/solution.py
+++ b/solution.py
@@ -50,7 +50,41 @@
     return first, second
 
 
-def edges_kernel(c_hbm, az_even_ref, az_odd_ref, col_even_ref, col_odd_ref, c_ref, sems):
+def row_edges_kernel(c_hbm, even_ref, odd_ref, top_ref, bottom_ref, sems):
+    rows = c_hbm.shape[1]
+    copies = [
+        pltpu.make_async_copy(c_hbm.at[:, pl.ds(0, 8)], top_ref, sems.at[0]),
+        pltpu.make_async_copy(c_hbm.at[:, pl.ds(rows - 8, 8)], bottom_ref, sems.at[1]),
+    ]
+    for copy in copies:
+        copy.start()
+    for copy in copies:
+        copy.wait()
+    low, high = top_ref[:, 0, :], bottom_ref[:, 7, :]
+    odd = lax.axis_index("col") % 2 == 1
+    even_ref[...] = jnp.where(odd, low, high)
+    odd_ref[...] = jnp.where(odd, high, low)
+
+
+def row_edges_stage(phase):
+    shells, _, cols = phase.shape
+    whole = pl.BlockSpec(memory_space=pltpu.VMEM)
+    return pl.pallas_call(
+        row_edges_kernel,
+        in_specs=[pl.BlockSpec(memory_space=pl.ANY)],
+        out_specs=[whole] * 2,
+        out_shape=[jax.ShapeDtypeStruct((shells, cols), f32)] * 2,
+        scratch_shapes=[
+            pltpu.VMEM((shells, 8, cols), f32),
+            pltpu.VMEM((shells, 8, cols), f32),
+            pltpu.SemaphoreType.DMA((2,)),
+        ],
+        compiler_params=params(52),
+        name="row_edges",
+    )(phase)
+
+
+def column_edges_kernel(c_hbm, even_ref, odd_ref, c_ref, sems):
     shells, rows, cols = c_ref.shape
     chunks = sems.shape[0]
     size = shells // chunks
@@ -69,30 +103,21 @@
         low = jnp.where(lane == k, pltpu.roll(c_ref[k, :, :128], k, 1), low)
         high = jnp.where(lane == k, pltpu.roll(c_ref[k, :, cols - 128 :], k + 1, 1), high)
     odd = lax.axis_index("az") % 2 == 1
-    az_even_ref[...] = jnp.where(odd, low, high)
-    az_odd_ref[...] = jnp.where(odd, high, low)
-    low, high = c_ref[:, 0, :], c_ref[:, rows - 1, :]
-    odd = lax.axis_index("col") % 2 == 1
-    col_even_ref[...] = jnp.where(odd, low, high)
-    col_odd_ref[...] = jnp.where(odd, high, low)
-
-
-def edges_stage(phase):
-    shells, rows, cols = phase.shape
+    even_ref[...] = jnp.where(odd, low, high)
+    odd_ref[...] = jnp.where(odd, high, low)
+
+
+def column_edges_stage(phase):
+    _, rows, _ = phase.shape
     whole = pl.BlockSpec(memory_space=pltpu.VMEM)
     return pl.pallas_call(
-        edges_kernel,
+        column_edges_kernel,
         in_specs=[pl.BlockSpec(memory_space=pl.ANY)],
-        out_specs=[whole] * 4,
-        out_shape=[
-            jax.ShapeDtypeStruct((rows, 128), f32),
-            jax.ShapeDtypeStruct((rows, 128), f32),
-            jax.ShapeDtypeStruct((shells, cols), f32),
-            jax.ShapeDtypeStruct((shells, cols), f32),
-        ],
+        out_specs=[whole] * 2,
+        out_shape=[jax.ShapeDtypeStruct((rows, 128), f32)] * 2,
         scratch_shapes=[pltpu.VMEM(phase.shape, f32), pltpu.SemaphoreType.DMA((8,))],
         compiler_params=params(52),
-        name="edges",
+        name="column_edges",
     )(phase)
 
 
@@ -498,17 +523,16 @@
     weights = (colat_weights(theta_count) / phi_count).astype(np.float32)
     weights = jnp.asarray(np.repeat(weights[:, None], 128, axis=1))
 
-    az_even, az_odd, col_even, col_odd = edges_stage(phase_field)
     even_az = [(i, i ^ 1) for i in range(az_count)]
     odd_az = [(i, (i + 1 if i % 2 else i - 1) % az_count) for i in range(az_count)]
     even_col = [(i, i ^ 1) for i in range(col_count)]
     odd_col = [(i, i + 1 if i % 2 else i - 1) for i in range(1, col_count - 1)]
-    halos = (
-        lax.ppermute(az_even, "az", even_az),
-        lax.ppermute(az_odd, "az", odd_az),
-        lax.ppermute(col_even, "col", even_col),
-        lax.ppermute(col_odd, "col", odd_col),
-    )
+    col_even, col_odd = row_edges_stage(phase_field)
+    col_halos = (lax.ppermute(col_even, "col", even_col), lax.ppermute(col_odd, "col", odd_col))
+    field, _ = lax.optimization_barrier((phase_field, col_odd))
+    az_even, az_odd = column_edges_stage(field)
+    az_halos = (lax.ppermute(az_even, "az", even_az), lax.ppermute(az_odd, "az", odd_az))
+    halos = az_halos + col_halos
 
     here = az_here * col_count + col_here
     own = lax.dynamic_slice(owned_modes, (here, 0), (1, owned_modes.shape[1])).reshape(-1)

time: 301 us -> 303 us (level)
  transfers between devices with their start and end apart: 4 -> 4, of which waited for: 0 -> 0; matrix products, arithmetic and copies ran while one was open for 0% -> 0% of each run, Pallas kernels for 1% -> 2%
where the time goes in v7:
time: 303 us; the launch traced here: 302 us
  blocking collectives  248 us (82%)
  Pallas kernels  45.1 us (15%)
  starting transfers between devices  8.36 us (3%)
    all_to_all x4, blocking collectives, exchange(): return lax.all_to_all(x, axes, split_axis=0, concat_axis=0, tiled=True)  248 us
    pallas_call x1, Pallas kernels, fourier_stage(): pl.pallas_call(fourier_kernel, in_specs=[whole, whole], out_specs=whole,...  13.1 us
    pallas_call x1, Pallas kernels, spectral_stage(): pl.pallas_call(kernel, in_specs=[pl.BlockSpec(memory_space=pltpu.SMEM), w...  9.59 us
    pallas_call x1, Pallas kernels, stencil_stage(): pl.pallas_call(kernel, grid=(shells // kb,), in_specs=[pl.BlockSpec(memor...  7.77 us
    pallas_call x1, Pallas kernels, inverse_stage(): pl.pallas_call(inverse_kernel, in_specs=[whole, whole], out_specs=whole,...  6.3 us
  transfers between devices with their start and end apart: 4, of which 0 were waited for; matrix products, arithmetic and copies ran while one was open for 0% of the time, Pallas kernels for 2%

profile of v7, /device:TPU:0, one launch (start us, length us, event | category | flops | bytes accessed | tf_op | source)
XLA Modules:
  0.0 302.4 jit_solution(10367180584609690030)
XLA Ops:
  0.0 0.0 slice-start
  0.0 0.0 copy-start.6
  0.0 1.3 row_edges.1
  1.4 0.0 copy-start.3
  1.4 0.0 copy-start.5
  1.4 0.8 collective-permute-start.3
  2.2 2.7 column_edges.1
  4.9 1.7 collective-permute-start
  6.7 3.5 %collective-permute-start.1 = (f32[64,128]{1,0:T(8,128)S(1)}, f32[64,128]{1,0:T(8,128)S(1)}, u32[]{:S(2)}, u32[]{:S(2)}) collective-permute-start(f32[64,128]{1,0:T(8,128)S(1)} %get-tuple-element.16), channel_id=1, source_target_pairs={{0,112},{16,32},{32,16},{48,64},{64,48},{80,96},{96,80},{112,0},{1... | collective-permute-start | bytes 98312 | tf_op jit(solution)/shard_map/ppermute | solution.py:534
  10.2 2.3 collective-permute-start.2
  12.5 0.0 slice-done
  12.5 0.0 copy-done.6
  12.5 0.0 copy-start
  12.5 0.2 dynamic-slice_reduce_fusion.refs_0_
  12.7 0.1 broadcast_in_dim.2.mode_ref
  12.9 2.2 table.1.table_ref
  15.0 0.0 collective-permute-done.refs_4_
  15.1 0.0 collective-permute-done.1.refs_5_
  15.1 0.0 collective-permute-done.2.refs_6_
  15.1 0.0 collective-permute-done.3.refs_7_
  15.1 0.0 copy-done.3
  15.1 0.0 copy-done.5
  15.1 0.0 copy-done
  15.1 7.8 %stencil.1 = f32[8,2,64,2,8,128]{5,4,3,2,1,0:T(8,128)} custom-call(f32[64]{0:T(128)S(1)} %copy-done.5, f32[64,64,256]{2,1,0:T(8,128)S(1)} %copy-done, bf16[2,64,64,256]{3,2,1,0:T(8,128)(2,1)} %refs_2_.2, f32[1024,128]{1,0:T(8,128)S(1)} %copy-done.3, f32[64,128]{1,0:T(8,128)S(1)} %collective-permute-done.refs_4_, ...), custom_call_target="tpu_custom_call" | custom-call | tf_op jit(solution)/shard_map/stencil/pallas_call | solution.py:184
  22.9 98.6 %all_to_all.20 = f32[8,2,64,2,8,128]{5,4,3,2,1,0:T(8,128)S(1)} all-to-all(f32[8,2,64,2,8,128]{5,4,3,2,1,0:T(8,128)} %stencil.1), channel_id=1, replica_groups=mesh['az'=8,'col'=16] {'az'}, dimensions={0} | all-to-all | bytes 16777216 | tf_op jit(solution)/shard_map/all_to_all | solution.py:509
  121.5 0.0 copy-start.4
  121.5 13.1 %fourier.1 = f32[8192,128]{1,0:T(8,128)S(1)} custom-call(f32[8,2,1024,128]{3,2,1,0:T(8,128)S(1)} %bitcast.8, bf16[2,1024,1024]{2,1,0:T(8,128)(2,1)S(1)} %table.1.table_ref), custom_call_target="tpu_custom_call" | custom-call | tf_op jit(solution)/shard_map/fourier/pallas_call | solution.py:296
  134.6 0.0 copy-start.1
  134.6 0.0 copy-start.2
  134.6 62.3 %all_to_all.21.refs_1_ = f32[128,2,2,2,8,128]{5,4,3,2,1,0:T(8,128)S(1)} all-to-all(f32[128,2,2,2,8,128]{5,4,3,2,1,0:T(8,128)S(1)} %bitcast.10), channel_id=1, replica_groups=mesh['az'=8,'col'=16] {'az','col'}, dimensions={0} | all-to-all | bytes 8388608 | tf_op jit(solution)/shard_map/all_to_all | solution.py:509
  196.9 0.0 copy-done.4
  196.9 0.0 copy-done.1
  196.9 0.0 copy-done.2
  196.9 9.6 %spectral.1 = f32[128,4,8,128]{3,2,1,0:T(8,128)S(1)} custom-call(s32[4]{0:T(128)S(1)} %dynamic-slice_reduce_fusion.refs_0_, f32[128,2,2,2,8,128]{5,4,3,2,1,0:T(8,128)S(1)} %all_to_all.21.refs_1_, bf16[4,1024,512]{2,1,0:T(8,128)(2,1)S(1)} %copy-done.1, bf16[64,64,512]{2,1,0:T(8,128)(2,1)S(1)} %bitcast.12, f32[128,512]{1,0:T(8,128)S(1)} %copy-done.4), custom_call_target="tpu_custom_call" | custom-call | tf_op jit(solution)/shard_map/spectral/pallas_call | solution.py:393
  206.5 35.7 %all_to_all.22 = f32[128,4,8,128]{3,2,1,0:T(8,128)S(1)} all-to-all(f32[128,4,8,128]{3,2,1,0:T(8,128)S(1)} %spectral.1), channel_id=1, replica_groups=mesh['az'=8,'col'=16] {'az','col'}, dimensions={0} | all-to-all | bytes 4194304 | tf_op jit(solution)/shard_map/all_to_all | solution.py:509
  242.2 6.3 %inverse.1 = f32[2,4,1024,128]{3,2,1,0:T(8,128)S(1)} custom-call(f32[4096,128]{1,0:T(8,128)S(1)} %bitcast.11, bf16[2,1024,1024]{2,1,0:T(8,128)(2,1)S(1)} %table.1.table_ref), custom_call_target="tpu_custom_call" | custom-call | tf_op jit(solution)/shard_map/inverse/pallas_call | solution.py:462
  248.5 51.6 %all_to_all.23.w_ref = f32[8,64,2,8,128]{4,3,2,1,0:T(8,128)S(1)} all-to-all(f32[8,64,2,8,128]{4,3,2,1,0:T(8,128)S(1)} %bitcast.9), channel_id=1, replica_groups=mesh['az'=8,'col'=16] {'az'}, dimensions={0} | all-to-all | bytes 8388608 | tf_op jit(solution)/shard_map/all_to_all | solution.py:509
  300.1 2.1 gather.1
  (2 shorter events, 0.0 us)
Async XLA Ops:
  0.0 12.5 %slice-start = ((s32[128,4]{0,1:T(4,128)}), s32[128,2]{0,1:T(2,128)S(1)}, s32[]{:S(2)}) async-start(s32[128,4]{0,1:T(4,128)} %param.10), calls=%async_computation.4 | async-start | bytes 2048 | tf_op jit(solution)/shard_map/slice | solution.py:239
  0.0 12.5 %copy-start.6 = (s32[128,4]{0,1:T(4,128)S(1)}, s32[128,4]{0,1:T(4,128)}, u32[]{:S(2)}) copy-start(s32[128,4]{0,1:T(4,128)} %param.10) | copy-start | bytes 6148
  1.4 13.7 %copy-start.3 = (f32[1024,128]{1,0:T(8,128)S(1)}, f32[1024,128]{1,0:T(8,128)}, u32[]{:S(2)}) copy-start(f32[1024,128]{1,0:T(8,128)} %constant.38.clone.refs_3_) | copy-start | bytes 1572868
  1.4 13.7 %copy-start.5 = (f32[64]{0:T(128)S(1)}, f32[64]{0:T(128)}, u32[]{:S(2)}) copy-start(f32[64]{0:T(128)} %constant.40.clone.refs_0_) | copy-start | bytes 772
  1.4 13.7 %collective-permute-start.3 = (f32[64,256]{1,0:T(8,128)S(1)}, f32[64,256]{1,0:T(8,128)S(1)}, u32[]{:S(2)}, u32[]{:S(2)}) collective-permute-start(f32[64,256]{1,0:T(8,128)S(1)} %get-tuple-element.13), channel_id=1, source_target_pairs={{1,2},{2,1},{3,4},{4,3},{5,6},{6,5},{7,8},{8,7},{9,10},{10,9},{11,... | collective-permute-start | bytes 196616 | tf_op jit(solution)/shard_map/ppermute | solution.py:531
  4.9 10.1 %collective-permute-start = (f32[64,128]{1,0:T(8,128)S(1)}, f32[64,128]{1,0:T(8,128)S(1)}, u32[]{:S(2)}, u32[]{:S(2)}) collective-permute-start(f32[64,128]{1,0:T(8,128)S(1)} %get-tuple-element.15), channel_id=1, source_target_pairs={{0,16},{16,0},{32,48},{48,32},{64,80},{80,64},{96,112},{112,96},{1... | collective-permute-start | bytes 98312 | tf_op jit(solution)/shard_map/ppermute | solution.py:534
  6.7 8.4 %collective-permute-start.1 = (f32[64,128]{1,0:T(8,128)S(1)}, f32[64,128]{1,0:T(8,128)S(1)}, u32[]{:S(2)}, u32[]{:S(2)}) collective-permute-start(f32[64,128]{1,0:T(8,128)S(1)} %get-tuple-element.16), channel_id=1, source_target_pairs={{0,112},{16,32},{32,16},{48,64},{64,48},{80,96},{96,80},{112,0},{1... | collective-permute-start | bytes 98312 | tf_op jit(solution)/shard_map/ppermute | solution.py:534
  10.2 4.9 %collective-permute-start.2 = (f32[64,256]{1,0:T(8,128)S(1)}, f32[64,256]{1,0:T(8,128)S(1)}, u32[]{:S(2)}, u32[]{:S(2)}) collective-permute-start(f32[64,256]{1,0:T(8,128)S(1)} %get-tuple-element.17), channel_id=1, source_target_pairs={{0,1},{1,0},{2,3},{3,2},{4,5},{5,4},{6,7},{7,6},{8,9},{9,8},{10,11... | collective-permute-start | bytes 196616 | tf_op jit(solution)/shard_map/ppermute | solution.py:531
  12.5 2.6 copy-start
  121.5 75.4 %copy-start.4 = (f32[128,512]{1,0:T(8,128)S(1)}, f32[128,512]{1,0:T(8,128)}, u32[]{:S(2)}) copy-start(f32[128,512]{1,0:T(8,128)} %constant.39.clone.refs_4_) | copy-start | bytes 786436
  134.6 62.3 %copy-start.1 = (bf16[4,1024,512]{2,1,0:T(8,128)(2,1)S(1)}, bf16[4,1024,512]{2,1,0:T(8,128)(2,1)}, u32[]{:S(2)}) copy-start(bf16[4,1024,512]{2,1,0:T(8,128)(2,1)} %refs_2_.3) | copy-start | bytes 12582916
  134.6 62.3 %copy-start.2 = (bf16[512,64,64]{0,2,1:T(8,128)(2,1)S(1)}, bf16[512,64,64]{0,2,1:T(8,128)(2,1)}, u32[]{:S(2)}) copy-start(bf16[512,64,64]{0,2,1:T(8,128)(2,1)} %param.12) | copy-start | bytes 12582916

commit v8 on v6

--- a/solution.py
+++ b/solution.py
@@ -97,7 +97,7 @@
 
 
 def stencil_kernel(
-    scale_phi, scale_ref, c_ref, v_ref, w_ref, az_even_ref, az_odd_ref, col_even_ref, col_odd_ref, out_ref
+    scale_phi, scale_ref, c_ref, v_ref, w_ref, col_odd_ref, az_odd_ref, az_even_ref, col_even_ref, out_ref
 ):
     shells, rows, cols = c_ref.shape
     block = pl.program_id(0)
@@ -164,9 +164,9 @@
             pl.BlockSpec((kb, rows, cols), lambda i: (i, 0, 0)),
             pl.BlockSpec((2, kb, rows, cols), lambda i: (0, i, 0, 0)),
             pl.BlockSpec(weights.shape, lambda i: (0, 0)),
+            pl.BlockSpec((kb, cols), lambda i: (i, 0)),
             pl.BlockSpec((rows, 128), lambda i: (0, 0)),
             pl.BlockSpec((rows, 128), lambda i: (0, 0)),
-            pl.BlockSpec((kb, cols), lambda i: (i, 0)),
             pl.BlockSpec((kb, cols), lambda i: (i, 0)),
         ],
         out_specs=pl.BlockSpec((rows // 8, 2, kb, cols // 128, 8, 128), lambda i: (0, 0, i, 0, 0, 0)),
@@ -504,10 +504,10 @@
     even_col = [(i, i ^ 1) for i in range(col_count)]
     odd_col = [(i, i + 1 if i % 2 else i - 1) for i in range(1, col_count - 1)]
     halos = (
+        lax.ppermute(col_odd, "col", odd_col),
+        lax.ppermute(az_odd, "az", odd_az),
         lax.ppermute(az_even, "az", even_az),
-        lax.ppermute(az_odd, "az", odd_az),
         lax.ppermute(col_even, "col", even_col),
-        lax.ppermute(col_odd, "col", odd_col),
     )
 
     here = az_here * col_count + col_here

time: 301 us -> 301 us (level)
  no operation moved by 1% of the time
where the time goes in v8:
time: 301 us; the launch traced here: 300 us
  blocking collectives  247 us (82%)
  Pallas kernels  44 us (15%)
  starting transfers between devices  8.12 us (3%)
    all_to_all x4, blocking collectives, exchange(): return lax.all_to_all(x, axes, split_axis=0, concat_axis=0, tiled=True)  247 us
    pallas_call x1, Pallas kernels, fourier_stage(): pl.pallas_call(fourier_kernel, in_specs=[whole, whole], out_specs=whole,...  13.1 us
    pallas_call x1, Pallas kernels, spectral_stage(): pl.pallas_call(kernel, in_specs=[pl.BlockSpec(memory_space=pltpu.SMEM), w...  9.59 us
    pallas_call x1, Pallas kernels, stencil_stage(): pl.pallas_call(kernel, grid=(shells // kb,), in_specs=[pl.BlockSpec(memor...  7.84 us
    pallas_call x1, Pallas kernels, inverse_stage(): pl.pallas_call(inverse_kernel, in_specs=[whole, whole], out_specs=whole,...  6.3 us
  transfers between devices with their start and end apart: 4, of which 0 were waited for; matrix products, arithmetic and copies ran while one was open for 0% of the time, Pallas kernels for 1%

profile of v8, /device:TPU:0, one launch (start us, length us, event | category | flops | bytes accessed | tf_op | source)
XLA Modules:
  0.0 300.2 jit_solution(14114340919959259293)
XLA Ops:
  0.0 0.0 copy-start.3
  0.0 0.0 copy-start.5
  0.0 0.0 slice-start
  0.0 0.0 copy-start.6
  0.0 2.9 edges.1
  2.9 4.5 %collective-permute-start.1 = (f32[64,128]{1,0:T(8,128)S(1)}, f32[64,128]{1,0:T(8,128)S(1)}, u32[]{:S(2)}, u32[]{:S(2)}) collective-permute-start(f32[64,128]{1,0:T(8,128)S(1)} %get-tuple-element.13), channel_id=1, source_target_pairs={{0,112},{16,32},{32,16},{48,64},{64,48},{80,96},{96,80},{112,0},{1... | collective-permute-start | bytes 98312 | tf_op jit(solution)/shard_map/ppermute | solution.py:508
  7.4 0.0 collective-permute-start.2
  7.4 0.7 collective-permute-start
  8.1 2.9 collective-permute-start.3
  11.0 0.0 slice-done
  11.0 0.0 copy-done.6
  11.1 0.0 copy-start
  11.1 0.2 dynamic-slice_reduce_fusion.refs_0_
  11.2 0.1 broadcast_in_dim.2.mode_ref
  11.4 2.2 table.1.table_ref
  13.6 0.0 collective-permute-done.1.refs_5_
  13.6 0.0 collective-permute-done.2.refs_6_
  13.6 0.0 collective-permute-done.refs_4_
  13.6 0.0 collective-permute-done.3.refs_7_
  13.6 0.0 copy-done.3
  13.6 0.0 copy-done.5
  13.6 0.0 copy-done
  13.6 7.8 %stencil.1 = f32[8,2,64,2,8,128]{5,4,3,2,1,0:T(8,128)} custom-call(f32[64]{0:T(128)S(1)} %copy-done.5, f32[64,64,256]{2,1,0:T(8,128)S(1)} %copy-done, bf16[2,64,64,256]{3,2,1,0:T(8,128)(2,1)} %refs_2_.2, f32[1024,128]{1,0:T(8,128)S(1)} %copy-done.3, f32[64,256]{1,0:T(8,128)S(1)} %collective-permute-done.refs_4_, ...), custom_call_target="tpu_custom_call" | custom-call | tf_op jit(solution)/shard_map/stencil/pallas_call | solution.py:159
  21.5 98.6 %all_to_all.20 = f32[8,2,64,2,8,128]{5,4,3,2,1,0:T(8,128)S(1)} all-to-all(f32[8,2,64,2,8,128]{5,4,3,2,1,0:T(8,128)} %stencil.1), channel_id=1, replica_groups=mesh['az'=8,'col'=16] {'az'}, dimensions={0} | all-to-all | bytes 16777216 | tf_op jit(solution)/shard_map/all_to_all | solution.py:484
  120.1 0.0 copy-start.4
  120.1 13.1 %fourier.1 = f32[8192,128]{1,0:T(8,128)S(1)} custom-call(f32[8,2,1024,128]{3,2,1,0:T(8,128)S(1)} %bitcast.8, bf16[2,1024,1024]{2,1,0:T(8,128)(2,1)S(1)} %table.1.table_ref), custom_call_target="tpu_custom_call" | custom-call | tf_op jit(solution)/shard_map/fourier/pallas_call | solution.py:271
  133.2 0.0 copy-start.1
  133.2 0.0 copy-start.2
  133.2 61.4 %all_to_all.21.refs_1_ = f32[128,2,2,2,8,128]{5,4,3,2,1,0:T(8,128)S(1)} all-to-all(f32[128,2,2,2,8,128]{5,4,3,2,1,0:T(8,128)S(1)} %bitcast.10), channel_id=1, replica_groups=mesh['az'=8,'col'=16] {'az','col'}, dimensions={0} | all-to-all | bytes 8388608 | tf_op jit(solution)/shard_map/all_to_all | solution.py:484
  194.6 0.0 copy-done.4
  194.6 0.0 copy-done.1
  194.6 0.0 copy-done.2
  194.7 9.6 %spectral.1 = f32[128,4,8,128]{3,2,1,0:T(8,128)S(1)} custom-call(s32[4]{0:T(128)S(1)} %dynamic-slice_reduce_fusion.refs_0_, f32[128,2,2,2,8,128]{5,4,3,2,1,0:T(8,128)S(1)} %all_to_all.21.refs_1_, bf16[4,1024,512]{2,1,0:T(8,128)(2,1)S(1)} %copy-done.1, bf16[64,64,512]{2,1,0:T(8,128)(2,1)S(1)} %bitcast.12, f32[128,512]{1,0:T(8,128)S(1)} %copy-done.4), custom_call_target="tpu_custom_call" | custom-call | tf_op jit(solution)/shard_map/spectral/pallas_call | solution.py:368
  204.2 35.7 %all_to_all.22 = f32[128,4,8,128]{3,2,1,0:T(8,128)S(1)} all-to-all(f32[128,4,8,128]{3,2,1,0:T(8,128)S(1)} %spectral.1), channel_id=1, replica_groups=mesh['az'=8,'col'=16] {'az','col'}, dimensions={0} | all-to-all | bytes 4194304 | tf_op jit(solution)/shard_map/all_to_all | solution.py:484
  239.9 6.3 %inverse.1 = f32[2,4,1024,128]{3,2,1,0:T(8,128)S(1)} custom-call(f32[4096,128]{1,0:T(8,128)S(1)} %bitcast.11, bf16[2,1024,1024]{2,1,0:T(8,128)(2,1)S(1)} %table.1.table_ref), custom_call_target="tpu_custom_call" | custom-call | tf_op jit(solution)/shard_map/inverse/pallas_call | solution.py:437
  246.2 51.6 %all_to_all.23.w_ref = f32[8,64,2,8,128]{4,3,2,1,0:T(8,128)S(1)} all-to-all(f32[8,64,2,8,128]{4,3,2,1,0:T(8,128)S(1)} %bitcast.9), channel_id=1, replica_groups=mesh['az'=8,'col'=16] {'az'}, dimensions={0} | all-to-all | bytes 8388608 | tf_op jit(solution)/shard_map/all_to_all | solution.py:484
  297.9 2.1 gather.1
  (2 shorter events, 0.0 us)
Async XLA Ops:
  0.0 13.6 %copy-start.3 = (f32[1024,128]{1,0:T(8,128)S(1)}, f32[1024,128]{1,0:T(8,128)}, u32[]{:S(2)}) copy-start(f32[1024,128]{1,0:T(8,128)} %constant.38.clone.refs_3_) | copy-start | bytes 1572868
  0.0 13.6 %copy-start.5 = (f32[64]{0:T(128)S(1)}, f32[64]{0:T(128)}, u32[]{:S(2)}) copy-start(f32[64]{0:T(128)} %constant.40.clone.refs_0_) | copy-start | bytes 772
  0.0 11.0 %slice-start = ((s32[128,4]{0,1:T(4,128)}), s32[128,2]{0,1:T(2,128)S(1)}, s32[]{:S(2)}) async-start(s32[128,4]{0,1:T(4,128)} %param.10), calls=%async_computation.4 | async-start | bytes 2048 | tf_op jit(solution)/shard_map/slice | solution.py:214
  0.0 11.0 %copy-start.6 = (s32[128,4]{0,1:T(4,128)S(1)}, s32[128,4]{0,1:T(4,128)}, u32[]{:S(2)}) copy-start(s32[128,4]{0,1:T(4,128)} %param.10) | copy-start | bytes 6148
  2.9 10.7 %collective-permute-start.1 = (f32[64,128]{1,0:T(8,128)S(1)}, f32[64,128]{1,0:T(8,128)S(1)}, u32[]{:S(2)}, u32[]{:S(2)}) collective-permute-start(f32[64,128]{1,0:T(8,128)S(1)} %get-tuple-element.13), channel_id=1, source_target_pairs={{0,112},{16,32},{32,16},{48,64},{64,48},{80,96},{96,80},{112,0},{1... | collective-permute-start | bytes 98312 | tf_op jit(solution)/shard_map/ppermute | solution.py:508
  7.4 6.2 %collective-permute-start.2 = (f32[64,128]{1,0:T(8,128)S(1)}, f32[64,128]{1,0:T(8,128)S(1)}, u32[]{:S(2)}, u32[]{:S(2)}) collective-permute-start(f32[64,128]{1,0:T(8,128)S(1)} %get-tuple-element.14), channel_id=1, source_target_pairs={{0,16},{16,0},{32,48},{48,32},{64,80},{80,64},{96,112},{112,96},{1... | collective-permute-start | bytes 98312 | tf_op jit(solution)/shard_map/ppermute | solution.py:509
  7.4 6.2 %collective-permute-start = (f32[64,256]{1,0:T(8,128)S(1)}, f32[64,256]{1,0:T(8,128)S(1)}, u32[]{:S(2)}, u32[]{:S(2)}) collective-permute-start(f32[64,256]{1,0:T(8,128)S(1)} %get-tuple-element.12), channel_id=1, source_target_pairs={{1,2},{2,1},{3,4},{4,3},{5,6},{6,5},{7,8},{8,7},{9,10},{10,9},{11,... | collective-permute-start | bytes 196616 | tf_op jit(solution)/shard_map/ppermute | solution.py:507
  8.1 5.5 %collective-permute-start.3 = (f32[64,256]{1,0:T(8,128)S(1)}, f32[64,256]{1,0:T(8,128)S(1)}, u32[]{:S(2)}, u32[]{:S(2)}) collective-permute-start(f32[64,256]{1,0:T(8,128)S(1)} %get-tuple-element.15), channel_id=1, source_target_pairs={{0,1},{1,0},{2,3},{3,2},{4,5},{5,4},{6,7},{7,6},{8,9},{9,8},{10,11... | collective-permute-start | bytes 196616 | tf_op jit(solution)/shard_map/ppermute | solution.py:510
  11.1 2.6 copy-start
  120.1 74.6 %copy-start.4 = (f32[128,512]{1,0:T(8,128)S(1)}, f32[128,512]{1,0:T(8,128)}, u32[]{:S(2)}) copy-start(f32[128,512]{1,0:T(8,128)} %constant.39.clone.refs_4_) | copy-start | bytes 786436
  133.2 61.4 %copy-start.1 = (bf16[4,1024,512]{2,1,0:T(8,128)(2,1)S(1)}, bf16[4,1024,512]{2,1,0:T(8,128)(2,1)}, u32[]{:S(2)}) copy-start(bf16[4,1024,512]{2,1,0:T(8,128)(2,1)} %refs_2_.3) | copy-start | bytes 12582916
  133.2 61.4 %copy-start.2 = (bf16[512,64,64]{0,2,1:T(8,128)(2,1)S(1)}, bf16[512,64,64]{0,2,1:T(8,128)(2,1)}, u32[]{:S(2)}) copy-start(bf16[512,64,64]{0,2,1:T(8,128)(2,1)} %param.12) | copy-start | bytes 12582916

commit v9 on v8

--- a/solution.py
+++ b/solution.py
@@ -151,7 +151,7 @@
 
 def stencil_stage(phase, velocity, weights, halos, scale_phi, scale_theta):
     shells, rows, cols = phase.shape
-    kb = 16
+    kb = 32
 
     def kernel(*refs):
         stencil_kernel(scale_phi, *refs)

time: 301 us -> 300 us (level)
  no operation moved by 1% of the time
where the time goes in v9:
time: 300 us
  blocking collectives  247 us (82%)
  Pallas kernels  43.7 us (15%)
  starting transfers between devices  8.12 us (3%)
    all_to_all x4, blocking collectives, exchange(): return lax.all_to_all(x, axes, split_axis=0, concat_axis=0, tiled=True)  247 us
    pallas_call x1, Pallas kernels, fourier_stage(): pl.pallas_call(fourier_kernel, in_specs=[whole, whole], out_specs=whole,...  13.1 us
    pallas_call x1, Pallas kernels, spectral_stage(): pl.pallas_call(kernel, in_specs=[pl.BlockSpec(memory_space=pltpu.SMEM), w...  9.59 us
    pallas_call x1, Pallas kernels, stencil_stage(): pl.pallas_call(kernel, grid=(shells // kb,), in_specs=[pl.BlockSpec(memor...  7.57 us
    pallas_call x1, Pallas kernels, inverse_stage(): pl.pallas_call(inverse_kernel, in_specs=[whole, whole], out_specs=whole,...  6.3 us
  transfers between devices with their start and end apart: 4, of which 0 were waited for; matrix products, arithmetic and copies ran while one was open for 0% of the time, Pallas kernels for 1%

profile of v9, /device:TPU:0, one launch (start us, length us, event | category | flops | bytes accessed | tf_op | source)
XLA Modules:
  0.0 299.9 jit_solution(6185237890127643970)
XLA Ops:
  0.0 0.0 copy-start.3
  0.0 0.0 copy-start.5
  0.0 0.0 slice-start
  0.0 0.0 copy-start.6
  0.0 2.9 edges.1
  2.9 4.5 %collective-permute-start.1 = (f32[64,128]{1,0:T(8,128)S(1)}, f32[64,128]{1,0:T(8,128)S(1)}, u32[]{:S(2)}, u32[]{:S(2)}) collective-permute-start(f32[64,128]{1,0:T(8,128)S(1)} %get-tuple-element.13), channel_id=1, source_target_pairs={{0,112},{16,32},{32,16},{48,64},{64,48},{80,96},{96,80},{112,0},{1... | collective-permute-start | bytes 98312 | tf_op jit(solution)/shard_map/ppermute | solution.py:508
  7.4 0.0 collective-permute-start.2
  7.4 0.7 collective-permute-start
  8.1 2.9 collective-permute-start.3
  11.0 0.0 slice-done
  11.0 0.0 copy-done.6
  11.1 0.0 copy-start
  11.1 0.2 dynamic-slice_reduce_fusion.refs_0_
  11.2 0.1 broadcast_in_dim.2.mode_ref
  11.4 2.2 table.1.table_ref
  13.6 0.0 collective-permute-done.1.refs_5_
  13.6 0.0 collective-permute-done.2.refs_6_
  13.6 0.0 collective-permute-done.refs_4_
  13.6 0.0 collective-permute-done.3.refs_7_
  13.6 0.0 copy-done.3
  13.6 0.0 copy-done.5
  13.6 0.0 copy-done
  13.6 7.6 %stencil.1 = f32[8,2,64,2,8,128]{5,4,3,2,1,0:T(8,128)} custom-call(f32[64]{0:T(128)S(1)} %copy-done.5, f32[64,64,256]{2,1,0:T(8,128)S(1)} %copy-done, bf16[2,64,64,256]{3,2,1,0:T(8,128)(2,1)} %refs_2_.2, f32[1024,128]{1,0:T(8,128)S(1)} %copy-done.3, f32[64,256]{1,0:T(8,128)S(1)} %collective-permute-done.refs_4_, ...), custom_call_target="tpu_custom_call" | custom-call | tf_op jit(solution)/shard_map/stencil/pallas_call | solution.py:159
  21.2 98.6 %all_to_all.20 = f32[8,2,64,2,8,128]{5,4,3,2,1,0:T(8,128)S(1)} all-to-all(f32[8,2,64,2,8,128]{5,4,3,2,1,0:T(8,128)} %stencil.1), channel_id=1, replica_groups=mesh['az'=8,'col'=16] {'az'}, dimensions={0} | all-to-all | bytes 16777216 | tf_op jit(solution)/shard_map/all_to_all | solution.py:484
  119.8 0.0 copy-start.4
  119.8 13.1 %fourier.1 = f32[8192,128]{1,0:T(8,128)S(1)} custom-call(f32[8,2,1024,128]{3,2,1,0:T(8,128)S(1)} %bitcast.8, bf16[2,1024,1024]{2,1,0:T(8,128)(2,1)S(1)} %table.1.table_ref), custom_call_target="tpu_custom_call" | custom-call | tf_op jit(solution)/shard_map/fourier/pallas_call | solution.py:271
  132.9 0.0 copy-start.1
  132.9 0.0 copy-start.2
  132.9 61.4 %all_to_all.21.refs_1_ = f32[128,2,2,2,8,128]{5,4,3,2,1,0:T(8,128)S(1)} all-to-all(f32[128,2,2,2,8,128]{5,4,3,2,1,0:T(8,128)S(1)} %bitcast.10), channel_id=1, replica_groups=mesh['az'=8,'col'=16] {'az','col'}, dimensions={0} | all-to-all | bytes 8388608 | tf_op jit(solution)/shard_map/all_to_all | solution.py:484
  194.4 0.0 copy-done.4
  194.4 0.0 copy-done.1
  194.4 0.0 copy-done.2
  194.4 9.6 %spectral.1 = f32[128,4,8,128]{3,2,1,0:T(8,128)S(1)} custom-call(s32[4]{0:T(128)S(1)} %dynamic-slice_reduce_fusion.refs_0_, f32[128,2,2,2,8,128]{5,4,3,2,1,0:T(8,128)S(1)} %all_to_all.21.refs_1_, bf16[4,1024,512]{2,1,0:T(8,128)(2,1)S(1)} %copy-done.1, bf16[64,64,512]{2,1,0:T(8,128)(2,1)S(1)} %bitcast.12, f32[128,512]{1,0:T(8,128)S(1)} %copy-done.4), custom_call_target="tpu_custom_call" | custom-call | tf_op jit(solution)/shard_map/spectral/pallas_call | solution.py:368
  204.0 35.7 %all_to_all.22 = f32[128,4,8,128]{3,2,1,0:T(8,128)S(1)} all-to-all(f32[128,4,8,128]{3,2,1,0:T(8,128)S(1)} %spectral.1), channel_id=1, replica_groups=mesh['az'=8,'col'=16] {'az','col'}, dimensions={0} | all-to-all | bytes 4194304 | tf_op jit(solution)/shard_map/all_to_all | solution.py:484
  239.7 6.3 %inverse.1 = f32[2,4,1024,128]{3,2,1,0:T(8,128)S(1)} custom-call(f32[4096,128]{1,0:T(8,128)S(1)} %bitcast.11, bf16[2,1024,1024]{2,1,0:T(8,128)(2,1)S(1)} %table.1.table_ref), custom_call_target="tpu_custom_call" | custom-call | tf_op jit(solution)/shard_map/inverse/pallas_call | solution.py:437
  246.0 51.6 %all_to_all.23.w_ref = f32[8,64,2,8,128]{4,3,2,1,0:T(8,128)S(1)} all-to-all(f32[8,64,2,8,128]{4,3,2,1,0:T(8,128)S(1)} %bitcast.9), channel_id=1, replica_groups=mesh['az'=8,'col'=16] {'az'}, dimensions={0} | all-to-all | bytes 8388608 | tf_op jit(solution)/shard_map/all_to_all | solution.py:484
  297.6 2.1 gather.1
  (2 shorter events, 0.0 us)
Async XLA Ops:
  0.0 13.6 %copy-start.3 = (f32[1024,128]{1,0:T(8,128)S(1)}, f32[1024,128]{1,0:T(8,128)}, u32[]{:S(2)}) copy-start(f32[1024,128]{1,0:T(8,128)} %constant.38.clone.refs_3_) | copy-start | bytes 1572868
  0.0 13.6 %copy-start.5 = (f32[64]{0:T(128)S(1)}, f32[64]{0:T(128)}, u32[]{:S(2)}) copy-start(f32[64]{0:T(128)} %constant.40.clone.refs_0_) | copy-start | bytes 772
  0.0 11.0 %slice-start = ((s32[128,4]{0,1:T(4,128)}), s32[128,2]{0,1:T(2,128)S(1)}, s32[]{:S(2)}) async-start(s32[128,4]{0,1:T(4,128)} %param.10), calls=%async_computation.4 | async-start | bytes 2048 | tf_op jit(solution)/shard_map/slice | solution.py:214
  0.0 11.0 %copy-start.6 = (s32[128,4]{0,1:T(4,128)S(1)}, s32[128,4]{0,1:T(4,128)}, u32[]{:S(2)}) copy-start(s32[128,4]{0,1:T(4,128)} %param.10) | copy-start | bytes 6148
  2.9 10.7 %collective-permute-start.1 = (f32[64,128]{1,0:T(8,128)S(1)}, f32[64,128]{1,0:T(8,128)S(1)}, u32[]{:S(2)}, u32[]{:S(2)}) collective-permute-start(f32[64,128]{1,0:T(8,128)S(1)} %get-tuple-element.13), channel_id=1, source_target_pairs={{0,112},{16,32},{32,16},{48,64},{64,48},{80,96},{96,80},{112,0},{1... | collective-permute-start | bytes 98312 | tf_op jit(solution)/shard_map/ppermute | solution.py:508
  7.4 6.2 %collective-permute-start.2 = (f32[64,128]{1,0:T(8,128)S(1)}, f32[64,128]{1,0:T(8,128)S(1)}, u32[]{:S(2)}, u32[]{:S(2)}) collective-permute-start(f32[64,128]{1,0:T(8,128)S(1)} %get-tuple-element.14), channel_id=1, source_target_pairs={{0,16},{16,0},{32,48},{48,32},{64,80},{80,64},{96,112},{112,96},{1... | collective-permute-start | bytes 98312 | tf_op jit(solution)/shard_map/ppermute | solution.py:509
  7.4 6.2 %collective-permute-start = (f32[64,256]{1,0:T(8,128)S(1)}, f32[64,256]{1,0:T(8,128)S(1)}, u32[]{:S(2)}, u32[]{:S(2)}) collective-permute-start(f32[64,256]{1,0:T(8,128)S(1)} %get-tuple-element.12), channel_id=1, source_target_pairs={{1,2},{2,1},{3,4},{4,3},{5,6},{6,5},{7,8},{8,7},{9,10},{10,9},{11,... | collective-permute-start | bytes 196616 | tf_op jit(solution)/shard_map/ppermute | solution.py:507
  8.1 5.5 %collective-permute-start.3 = (f32[64,256]{1,0:T(8,128)S(1)}, f32[64,256]{1,0:T(8,128)S(1)}, u32[]{:S(2)}, u32[]{:S(2)}) collective-permute-start(f32[64,256]{1,0:T(8,128)S(1)} %get-tuple-element.15), channel_id=1, source_target_pairs={{0,1},{1,0},{2,3},{3,2},{4,5},{5,4},{6,7},{7,6},{8,9},{9,8},{10,11... | collective-permute-start | bytes 196616 | tf_op jit(solution)/shard_map/ppermute | solution.py:510
  11.1 2.6 copy-start
  119.8 74.6 %copy-start.4 = (f32[128,512]{1,0:T(8,128)S(1)}, f32[128,512]{1,0:T(8,128)}, u32[]{:S(2)}) copy-start(f32[128,512]{1,0:T(8,128)} %constant.39.clone.refs_4_) | copy-start | bytes 786436
  132.9 61.5 %copy-start.1 = (bf16[4,1024,512]{2,1,0:T(8,128)(2,1)S(1)}, bf16[4,1024,512]{2,1,0:T(8,128)(2,1)}, u32[]{:S(2)}) copy-start(bf16[4,1024,512]{2,1,0:T(8,128)(2,1)} %refs_2_.3) | copy-start | bytes 12582916
  132.9 61.5 %copy-start.2 = (bf16[512,64,64]{0,2,1:T(8,128)(2,1)S(1)}, bf16[512,64,64]{0,2,1:T(8,128)(2,1)}, u32[]{:S(2)}) copy-start(bf16[512,64,64]{0,2,1:T(8,128)(2,1)} %param.12) | copy-start | bytes 12582916
